TPU v7x, 32 devices: a whole 2x2x4 slice. The times are simulated.
32 devices in a mesh: rows: 4 (over x, core), cols: 8 (over z, y).
Axes of the slice: x: 2, y: 2, z: 4, core: 2. Of those that a mesh axis runs over, the one named last changes fastest.
Arguments:
- features: bfloat16 [1024, 512], P(('rows', 'cols')), may hold values from -0.59765625 to 0.59765625
- positions: float32 [3, 1024], P(None, ('rows', 'cols')), may hold values from 0 to 1, as said below
- cell_lengths: float32 [3], replicated, may hold values from 30 to 60
- block_lists: int32 [32, 8], P(('rows', 'cols')), may hold values from 0 to 31, as said below
- image_offsets: int32 [3, 32, 8], P(None, ('rows', 'cols')), may hold values from -1 to 1
- block_valid: int32 [32, 8], P(('rows', 'cols')), may hold values from 0 to 1, as said below
- norm_gain: float32 [512], replicated, may hold values from 0.1 to 1.9
- w_qkv: bfloat16 [512, 1536], replicated, may hold values from -1 to 1
- w_out: bfloat16 [512, 512], replicated, may hold values from -0.25 to 0.25
- rbf_weight: float32 [16, 64], replicated, may hold values from -5 to 5
- rbf_offset: float32 [64], replicated, may hold values from -4 to 4
- pair_weight: float32 [64, 16], replicated, may hold values from -30 to 30
- cosine_scale: float32 [16], replicated, may hold values from -80 to 80, as said below
Outputs:
- updated: bfloat16 [1024, 512], P(('rows', 'cols'))
Inputs may be any that keep to these rules, and one draw needn't show every extreme that they name: `block_lists`: block b lies at grid row b // 8 and column b % 8. Every entry names a block whose row and column each differ from b's by at most one, counted around the grid; the first entry is b itself and the entries of a block differ. `block_valid`: the first entry of every block is 1 and a block's ones come before its zeros; some block has all 8 entries 1. `positions`: atoms of block b have their first coordinate within [r, r + 1] / 4 and their second within [c, c + 1] / 8, with r = b // 8 and c = b % 8. `cosine_scale`: every magnitude is 0.3 or more.
All inputs are finite; a program needn't handle non-finite values.
Results may differ from a plain program's by a relative error of at most 0.012.
The roundings to bfloat16 on the way count: a program that leaves them out, or rounds other values in their place, can miss the bound.
Values may be sent and summed in bfloat16 or wider, within the bound.
No kernel may reach another device: no remote copies, remote signals or barrier semaphores. Data moves between devices by JAX's collectives and lax.ppermute only.
A program may use at most 64 MiB of HBM per device.

v0:
```python
import math

import jax
import jax.numpy as jnp
from jax import lax
from jax.sharding import PartitionSpec as P

rbf_step = 2.0
rbf_width = 2.0
two_pi = 2.0 * math.pi
highest = lax.Precision.HIGHEST


def with_halo(cells, sides, width):
    for axis, dim in sides:
        count = lax.axis_size(axis)
        head = lax.slice_in_dim(cells, 0, width, axis=dim)
        tail = lax.slice_in_dim(cells, cells.shape[dim] - width, cells.shape[dim], axis=dim)
        cells = jnp.concatenate(
            [
                lax.ppermute(tail, axis, [(i, (i + 1) % count) for i in range(count)]),
                cells,
                lax.ppermute(head, axis, [((i + 1) % count, i) for i in range(count)]),
            ],
            axis=dim,
        )
    return cells


def rms_rows(values, norm_gain):
    floats = values.astype(jnp.float32)
    spread = jnp.mean(floats * floats, axis=-1, keepdims=True)
    return (floats * lax.rsqrt(spread + 1e-06) * norm_gain).astype(jnp.bfloat16)


def near_attention(
    query_rows,
    own_pos,
    keys,
    key_pos,
    shifts,
    live,
    cell_lengths,
    rbf_weight,
    rbf_offset,
    pair_weight,
):
    entries, block_len = (keys.shape[0], keys.shape[1])
    model_dim = query_rows.shape[1]
    head_count = pair_weight.shape[1]
    head_dim = model_dim // head_count
    key_coords = key_pos.transpose(1, 0, 2) + shifts.astype(jnp.float32)[:, :, None]
    key_coords = key_coords.reshape(3, entries * block_len)
    displace = (key_coords[:, None, :] - own_pos[:, :, None]) * cell_lengths[:, None, None]
    distance = jnp.sqrt(jnp.sum(displace * displace, axis=0) + 0.25)
    centers = jnp.arange(rbf_weight.shape[0], dtype=jnp.float32) * rbf_step
    radial = jnp.exp(-((distance[None] - centers[:, None, None]) ** 2) * (0.5 / rbf_width**2))
    radial = radial.reshape(rbf_weight.shape[0], -1)
    hidden = jax.nn.silu(jnp.dot(rbf_weight.T, radial, precision=highest) + rbf_offset[:, None])
    pair_bias = jnp.dot(pair_weight.T, hidden, precision=highest).reshape(
        head_count, query_rows.shape[0], entries * block_len
    )
    query_heads = query_rows.reshape(-1, head_count, head_dim)
    key_heads = keys[:, :, :model_dim].reshape(entries * block_len, head_count, head_dim)
    value_heads = keys[:, :, model_dim:].reshape(entries * block_len, head_count, head_dim)
    scores = (
        jnp.einsum("ahd,khd->hak", query_heads, key_heads, preferred_element_type=jnp.float32)
        * head_dim ** (-0.5)
        + pair_bias
    )
    allowed = jnp.repeat(live > 0, block_len)
    scores = jnp.where(allowed[None, None, :], scores, -1e30)
    row_max = jnp.max(scores, axis=-1, keepdims=True)
    weights = jnp.exp(scores - row_max)
    row_sum = jnp.sum(weights, axis=-1, keepdims=True)
    prob_bf = weights.astype(jnp.bfloat16)
    attended = jnp.einsum(
        "hak,khd->ahd", prob_bf, value_heads, preferred_element_type=jnp.float32
    ) / row_sum.transpose(1, 0, 2)
    return attended.reshape(-1, model_dim).astype(jnp.bfloat16)


def on_device(
    features,
    positions,
    cell_lengths,
    block_lists,
    image_offsets,
    block_valid,
    norm_gain,
    w_qkv,
    w_out,
    rbf_weight,
    rbf_offset,
    pair_weight,
    cosine_scale,
):
    atom_count, model_dim = features.shape
    head_count = pair_weight.shape[1]
    head_dim = model_dim // head_count
    row_count = lax.axis_size("rows")
    col_count = lax.axis_size("cols")
    row_index = lax.axis_index("rows")
    col_index = lax.axis_index("cols")
    per_dev = head_count // row_count
    normed = rms_rows(features, norm_gain)
    packed = jnp.dot(normed, w_qkv, preferred_element_type=jnp.float32).astype(jnp.bfloat16)
    every_pos = lax.all_gather(positions, ("rows", "cols"), axis=1, tiled=True)
    near_rows = with_halo(normed[None, None], (("rows", 0), ("cols", 1)), 1)
    near_kv = jnp.dot(
        near_rows.reshape(9 * atom_count, model_dim),
        w_qkv[:, model_dim:],
        preferred_element_type=jnp.float32,
    )
    near_kv = near_kv.astype(jnp.bfloat16).reshape(9, atom_count, 2 * model_dim)
    listed = block_lists[0]
    list_row = listed // col_count
    list_col = listed % col_count
    slots = (list_row - row_index + 1) % row_count * 3 + (list_col - col_index + 1) % col_count
    keys = jnp.take(near_kv, slots, axis=0)
    block_pos = every_pos.reshape(3, row_count * col_count, atom_count)
    key_pos = jnp.take(block_pos, listed, axis=1).transpose(1, 0, 2)
    local_out = near_attention(
        packed[:, :model_dim],
        positions,
        keys,
        key_pos,
        image_offsets[:, 0, :],
        block_valid[0],
        cell_lengths,
        rbf_weight,
        rbf_offset,
        pair_weight,
    )
    grouped = (
        packed.reshape(atom_count, 3, head_count, head_dim)
        .transpose(1, 2, 0, 3)
        .reshape(3, head_count, atom_count * head_dim)
    )
    regrouped = lax.all_to_all(grouped, "rows", split_axis=1, concat_axis=2, tiled=True)
    query_count = row_count * atom_count
    queries = regrouped[0].reshape(per_dev, query_count, head_dim)
    key_vals = regrouped[1:]
    cycle_pos = (
        every_pos.reshape(3, row_count, col_count, atom_count).transpose(0, 2, 1, 3).reshape(3, -1)
    )
    query_pos = lax.dynamic_slice_in_dim(cycle_pos, col_index * query_count, query_count, 1)
    cycle_feats = jnp.concatenate(
        [jnp.cos(two_pi * cycle_pos), jnp.sin(two_pi * cycle_pos)], axis=0
    )
    query_feats = jnp.concatenate(
        [jnp.cos(two_pi * query_pos), jnp.sin(two_pi * query_pos)], axis=0
    )
    strengths = lax.dynamic_slice_in_dim(cosine_scale, row_index * per_dev, per_dev)
    scale = head_dim ** (-0.5)

    def update(state, kv_block, key_start, block_len):
        run_max, run_sum, accum = state
        scores = (
            jnp.einsum("hqd,hkd->hqk", queries, kv_block[0], preferred_element_type=jnp.float32)
            * scale
        )
        coords = lax.dynamic_slice_in_dim(cycle_feats, key_start, block_len, 1)
        cos_bias = jnp.dot(query_feats.T, coords, precision=highest)
        scores = scores + strengths[:, None, None] * cos_bias[None]
        new_max = jnp.maximum(run_max, jnp.max(scores, axis=-1))
        keep_part = jnp.exp(run_max - new_max)
        weights = jnp.exp(scores - new_max[:, :, None])
        run_sum = run_sum * keep_part + jnp.sum(weights, axis=-1)
        prob_bf = weights.astype(jnp.bfloat16)
        accum = accum * keep_part[:, None, :] + jnp.einsum(
            "hqk,hkd->hdq", prob_bf, kv_block[1], preferred_element_type=jnp.float32
        )
        return (new_max, run_sum, accum)

    initial = (
        jnp.full((per_dev, query_count), -1e30, jnp.float32),
        jnp.zeros((per_dev, query_count), jnp.float32),
        jnp.zeros((per_dev, head_dim, query_count), jnp.float32),
    )
    piece = lax.all_gather(key_vals, "cols", axis=2, tiled=True)
    key_total = piece.shape[2] // head_dim
    if key_total > 1024 and key_total % 1024 == 0:
        block_len = 1024
    else:
        block_len = key_total
    block_count = key_total // block_len
    kv_blocks = piece.reshape(2, per_dev, block_count, block_len, head_dim).transpose(2, 0, 1, 3, 4)
    block_starts = jnp.arange(block_count, dtype=jnp.int32) * block_len

    def one_block(state, block_in):
        kv_block, key_start = block_in
        return (update(state, kv_block, key_start, block_len), None)

    state, _ = lax.scan(one_block, initial, (kv_blocks, block_starts))
    run_max, run_sum, accum = state
    head_out = (
        (accum / run_sum[:, None, :])
        .transpose(0, 2, 1)
        .astype(jnp.bfloat16)
        .reshape(per_dev, query_count * head_dim)
    )
    returned = lax.all_to_all(head_out, "rows", split_axis=1, concat_axis=0, tiled=True)
    global_out = (
        returned.reshape(head_count, atom_count, head_dim)
        .transpose(1, 0, 2)
        .reshape(atom_count, model_dim)
    )
    combined = (local_out.astype(jnp.float32) + global_out.astype(jnp.float32)).astype(jnp.bfloat16)
    updated = features.astype(jnp.float32) + jnp.dot(
        combined, w_out, preferred_element_type=jnp.float32
    )
    return updated.astype(jnp.bfloat16)


def solution(mesh):
    return jax.shard_map(
        on_device,
        mesh=mesh,
        in_specs=(
            P(("rows", "cols"), None),
            P(None, ("rows", "cols")),
            P(),
            P(("rows", "cols"), None),
            P(None, ("rows", "cols"), None),
            P(("rows", "cols"), None),
            P(),
            P(),
            P(),
            P(),
            P(),
            P(),
            P(),
        ),
        out_specs=P(("rows", "cols"), None),
        check_vma=False,
    )
```

profile of v0, /device:TPU:0, one launch (start us, length us, event | category | flops | bytes accessed | tf_op | source)
XLA Modules:
  0.0 150.0 jit_solution(17204059788164106067)
XLA Ops:
  0.0 0.9 fusion.38
  0.9 1.5 fusion.46
  2.4 0.5 collective-permute-start
  2.9 2.0 %collective-permute-start.1 = (bf16[1,1,32,512]{3,2,1,0:T(8,128)(2,1)}, bf16[1,1,32,512]{3,2,1,0:T(8,128)(2,1)}, u32[]{:S(2)}, u32[]{:S(2)}) collective-permute-start(bf16[1,1,32,512]{3,2,1,0:T(8,128)(2,1)} %fusion.46), channel_id=1, source_target_pairs={{8,0},{16,8},{24,16},{0,24},{9,1},{17,9},{25,17},{1,25},{10,2},{18... | collective-permute-start | bytes 98312 | tf_op jit(solution)/shard_map/ppermute | solution.py:23
  4.9 1.9 %convolution_convert_fusion = bf16[32,1536]{1,0:T(8,128)(2,1)S(1)} fusion(bf16[512,1536]{1,0:T(8,128)(2,1)} %param.20, bf16[32,512]{1,0:T(8,128)(2,1)} %param.13, f32[512]{0:T(512)} %param.19, f32[32]{0:T(128)S(1)} %add_rsqrt_fusion), kind=kOutput, calls=%fused_computation.4 | convolution fusion | flops 50446336 | bytes 1706112 | tf_op jit(solution)/shard_map/dot_general | solution.py:107
  6.8 0.2 reshape.360
  7.0 0.1 copy.97
  7.1 0.4 reshape.361
  7.5 0.7 copy.68
  8.3 3.5 %all-to-all-start = ((bf16[3,16,1024]{2,0,1:T(4,128)(2,1)}), bf16[3,16,1024]{2,0,1:T(4,128)(2,1)S(1)}, u32[]{:S(2)}, u32[]{:S(2)}) async-start(bf16[3,16,1024]{2,0,1:T(4,128)(2,1)} %copy.68), calls=%async_computation | async-start | bytes 262144 | tf_op jit(solution)/shard_map/all_to_all | solution.py:140
  11.8 0.6 compare_and_fusion
  12.4 69.9 %all-gather = f32[32,32,3]{1,2,0:T(4,128)S(1)} all-gather(f32[1,32,3]{1,2,0:T(4,128)S(1)} %bitcast.118), channel_id=1, replica_groups=mesh['rows'=4,'cols'=8] {'rows','cols'}, dimensions={0}, use_global_device_ids=true | all-gather | bytes 12672 | tf_op jit(solution)/shard_map/all_gather | solution.py:108
  82.7 0.1 multiply_cosine_fusion
  83.0 0.6 gather_fusion.1
  84.1 1.9 %fusion = f32[64,8192]{1,0:T(8,128)S(1)} fusion(f32[16,64]{1,0:T(8,128)S(1)} %copy-done.4, f32[64]{0:T(128)S(1)} %copy-done.11, f32[16]{0:T(128)S(1)} %iota_multiply_fusion, f32[8192]{0:T(1024)S(1)} %bitcast.114), kind=kOutput, calls=%fused_computation.3 | convolution fusion | flops 101711872 | bytes 2134336 | tf_op jit(solution)/shard_map/dot_general | solution.py:59
  86.0 1.6 %fusion.1 = f32[8192,16]{0,1:T(8,128)S(1)} fusion(f32[64,16]{0,1:T(8,128)S(1)} %copy-done.12, f32[64,8192]{1,0:T(8,128)S(1)} %fusion), kind=kOutput, calls=%fused_computation.7 | convolution fusion | flops 102760448 | bytes 2625536 | tf_op jit(solution)/shard_map/dot_general | solution.py:60
  87.7 0.2 copy.82
  87.8 0.1 reshape.356
  88.1 0.6 broadcast_in_dim.76
  88.7 1.5 fusion.41
  90.4 31.2 %all_gather.7 = bf16[2,4,32768]{2,1,0:T(4,128)(2,1)S(1)} all-gather(bf16[2,4,4096]{2,1,0:T(4,128)(2,1)S(1)} %slice.38), channel_id=1, replica_groups=mesh['rows'=4,'cols'=8] {'cols'}, dimensions={2}, use_global_device_ids=true | all-gather | bytes 589824 | tf_op jit(solution)/shard_map/all_gather | solution.py:181
  121.6 0.2 fusion.70
  121.8 1.6 %squeeze.23 = bf16[4,1024,32]{2,1,0:T(8,128)(2,1)} reshape(bf16[1,4,32768]{2,1,0:T(4,128)(2,1)S(1)} %get-tuple-element.21) | data formatting | bytes 524288 | tf_op jit(solution)/shard_map/while/body/eval_jaxpr/squeeze | solution.py:160
  123.3 0.8 reshape_squeeze.3
  124.1 1.9 %fusion.72 = (f32[4,128]{1,0:T(4,128)S(1)}, f32[4,128,1024]{2,1,0:T(8,128)S(1)}) fusion(f32[128,1024]{1,0:T(8,128)} %fusion.41, f32[4]{0:T(128)S(1)} %dynamic_slice.14, bf16[4,128,32]{2,1,0:T(8,128)(2,1)} %reshape_squeeze.3, bf16[4,1024,32]{2,1,0:T(8,128)(2,1)} %squeeze.23), kind=kOutput, calls=%fused_computation.134 | convolution fusion | flops 35651072 | bytes 2918416 | tf_op jit(solution)/shard_map/while/body/eval_jaxpr/hqd,hkd->hqk/dot_general | solution.py:160
  126.1 0.5 fusion.7
  126.6 1.6 %squeeze.24 = bf16[4,1024,32]{2,1,0:T(8,128)(2,1)} reshape(bf16[1,4,32768]{2,1,0:T(4,128)(2,1)S(1)} %get-tuple-element.22) | data formatting | bytes 524288 | tf_op jit(solution)/shard_map/while/body/eval_jaxpr/squeeze | solution.py:172
  128.1 2.4 %fusion.17 = bf16[4,128,32]{1,2,0:T(8,128)(2,1)} fusion(bf16[4,1024,32]{2,1,0:T(8,128)(2,1)} %squeeze.24, f32[4,128,1024]{2,1,0:T(8,128)S(1)} %get-tuple-element.47, f32[4,128]{1,0:T(4,128)S(1)} %broadcast_maximum_fusion, f32[4,128]{1,0:T(4,128)S(1)} %get-tuple-element.41, f32[4,128]{1,0:T(4,128)S(1)} %get-tuple-element.40), kind=kOutput, calls=%fused_computation.28 | convolution fusion | flops 34652160 | bytes 2398208 | tf_op jit(solution)/shard_map/while/body/eval_jaxpr/hqk,hkd->hdq/dot_general | solution.py:171
  130.5 1.0 copy.74
  131.5 0.2 all_to_all.24
  131.7 0.6 copy.75
  132.3 3.3 %all-to-all-start.1 = ((bf16[4,4,1024]{2,0,1:T(4,128)(2,1)}), bf16[4,4,1024]{2,0,1:T(4,128)(2,1)S(1)}, u32[]{:S(2)}, u32[]{:S(2)}) async-start(bf16[4,4,1024]{2,0,1:T(4,128)(2,1)} %copy.75), calls=%async_computation.1 | async-start | bytes 65536 | tf_op jit(solution)/shard_map/all_to_all | solution.py:203
  135.6 0.8 pad_maximum_fusion.1
  136.5 4.7 %collective-permute-start.3 = (bf16[3,1,32,512]{3,2,1,0:T(8,128)(2,1)S(1)}, bf16[3,1,32,512]{3,2,1,0:T(8,128)(2,1)S(1)}, u32[]{:S(2)}, u32[]{:S(2)}) collective-permute-start(bf16[3,1,32,512]{3,2,1,0:T(8,128)(2,1)S(1)} %pad_maximum_fusion.1), channel_id=1, source_target_pairs={{1,0},{2,1},{3,2},{4,3},{5,4},{6,5},{7,6},{0,7},{9,8},{10,9},{11,1... | collective-permute-start | bytes 294920 | tf_op jit(solution)/shard_map/ppermute | solution.py:23
  141.2 0.1 reshape.364
  141.4 0.8 copy.76
  142.2 2.1 %collective-permute-done.2 = bf16[3,1,32,512]{3,2,1,0:T(8,128)(2,1)S(1)} collective-permute-done((bf16[3,1,32,512]{3,2,1,0:T(8,128)(2,1)S(1)}, bf16[3,1,32,512]{3,2,1,0:T(8,128)(2,1)S(1)}, u32[]{:S(2)}, u32[]{:S(2)}) %collective-permute-start.2) | collective-permute-done | bytes 98336 | tf_op jit(solution)/shard_map/ppermute | solution.py:21
  144.3 0.8 pad_maximum_fusion
  145.2 0.5 convolution_convert_fusion.1
  145.7 0.6 gather_fusion
  146.3 0.1 broadcast_select_fusion
  146.4 0.6 reshape.357
  147.0 0.6 reshape.355
  147.7 0.5 fusion.73
  148.2 0.3 fusion.30
  148.5 0.1 copy-done.3
  148.6 0.6 fusion.15
  149.2 0.8 fusion.18
  (71 shorter events, 1.6 us)
Async XLA Ops:
  0.0 149.2 %copy-start = (bf16[512,512]{1,0:T(8,128)(2,1)S(1)}, bf16[512,512]{1,0:T(8,128)(2,1)}, u32[]{:S(2)}) copy-start(bf16[512,512]{1,0:T(8,128)(2,1)} %param.21) | copy-start | bytes 1572868
  0.0 11.8 %copy-start.7 = (s32[1,8]{1,0:T(1,128)S(1)}, s32[1,8]{1,0:T(1,128)}, u32[]{:S(2)}) copy-start(s32[1,8]{1,0:T(1,128)} %param.16) | copy-start | bytes 100
  0.0 12.4 %copy-start.5 = (f32[3,32]{1,0:T(4,128)S(1)}, f32[3,32]{1,0:T(4,128)}, u32[]{:S(2)}) copy-start(f32[3,32]{1,0:T(4,128)} %param.14) | copy-start | bytes 1156
  2.4 81.4 %copy-start.8 = (s32[3,1,8]{2,1,0:T(1,128)S(1)}, s32[3,1,8]{2,1,0:T(1,128)}, u32[]{:S(2)}) copy-start(s32[3,1,8]{2,1,0:T(1,128)} %param.17) | copy-start | bytes 292
  2.4 81.5 %copy-start.9 = (f32[3]{0:T(128)S(1)}, f32[3]{0:T(128)}, u32[]{:S(2)}) copy-start(f32[3]{0:T(128)} %param.15) | copy-start | bytes 40
  2.4 133.2 %collective-permute-start = (bf16[1,1,32,512]{3,2,1,0:T(8,128)(2,1)}, bf16[1,1,32,512]{3,2,1,0:T(8,128)(2,1)}, u32[]{:S(2)}, u32[]{:S(2)}) collective-permute-start(bf16[1,1,32,512]{3,2,1,0:T(8,128)(2,1)} %fusion.46), channel_id=1, source_target_pairs={{0,8},{8,16},{16,24},{24,0},{1,9},{9,17},{17,25},{25,1},{2,10},{10... | collective-permute-start | bytes 98312 | tf_op jit(solution)/shard_map/ppermute | solution.py:21
  2.9 132.7 %collective-permute-start.1 = (bf16[1,1,32,512]{3,2,1,0:T(8,128)(2,1)}, bf16[1,1,32,512]{3,2,1,0:T(8,128)(2,1)}, u32[]{:S(2)}, u32[]{:S(2)}) collective-permute-start(bf16[1,1,32,512]{3,2,1,0:T(8,128)(2,1)} %fusion.46), channel_id=1, source_target_pairs={{8,0},{16,8},{24,16},{0,24},{9,1},{17,9},{25,17},{1,25},{10,2},{18... | collective-permute-start | bytes 98312 | tf_op jit(solution)/shard_map/ppermute | solution.py:23
  6.8 77.4 %copy-start.4 = (f32[16,64]{1,0:T(8,128)S(1)}, f32[16,64]{1,0:T(8,128)}, u32[]{:S(2)}) copy-start(f32[16,64]{1,0:T(8,128)} %param.22) | copy-start | bytes 12292
  6.8 77.4 %copy-start.11 = (f32[64]{0:T(128)S(1)}, f32[64]{0:T(128)}, u32[]{:S(2)}) copy-start(f32[64]{0:T(128)} %param.23) | copy-start | bytes 772
  7.1 78.9 %copy-start.12 = (f32[64,16]{0,1:T(8,128)S(1)}, f32[64,16]{0,1:T(8,128)}, u32[]{:S(2)}) copy-start(f32[64,16]{0,1:T(8,128)} %param.24) | copy-start | bytes 12292
  8.3 81.9 %all-to-all-start = ((bf16[3,16,1024]{2,0,1:T(4,128)(2,1)}), bf16[3,16,1024]{2,0,1:T(4,128)(2,1)S(1)}, u32[]{:S(2)}, u32[]{:S(2)}) async-start(bf16[3,16,1024]{2,0,1:T(4,128)(2,1)} %copy.68), calls=%async_computation | async-start | bytes 262144 | tf_op jit(solution)/shard_map/all_to_all | solution.py:140
  86.0 2.0 %copy-start.13 = (s32[1,8]{1,0:T(1,128)S(1)}, s32[1,8]{1,0:T(1,128)}, u32[]{:S(2)}) copy-start(s32[1,8]{1,0:T(1,128)} %param.18) | copy-start | bytes 100
  86.0 2.6 %copy-start.14 = (f32[16]{0:T(128)S(1)}, f32[16]{0:T(128)}, u32[]{:S(2)}) copy-start(f32[16]{0:T(128)} %param.25) | copy-start | bytes 196
  130.5 14.6 %copy-start.1 = (bf16[512,1536]{1,0:T(8,128)(2,1)S(1)}, bf16[512,1536]{1,0:T(8,128)(2,1)}, u32[]{:S(2)}) copy-start(bf16[512,1536]{1,0:T(8,128)(2,1)} %param.20) | copy-start | bytes 4718596
  132.3 8.9 %all-to-all-start.1 = ((bf16[4,4,1024]{2,0,1:T(4,128)(2,1)}), bf16[4,4,1024]{2,0,1:T(4,128)(2,1)S(1)}, u32[]{:S(2)}, u32[]{:S(2)}) async-start(bf16[4,4,1024]{2,0,1:T(4,128)(2,1)} %copy.75), calls=%async_computation.1 | async-start | bytes 65536 | tf_op jit(solution)/shard_map/all_to_all | solution.py:203
  136.4 7.9 %collective-permute-start.2 = (bf16[3,1,32,512]{3,2,1,0:T(8,128)(2,1)S(1)}, bf16[3,1,32,512]{3,2,1,0:T(8,128)(2,1)S(1)}, u32[]{:S(2)}, u32[]{:S(2)}) collective-permute-start(bf16[3,1,32,512]{3,2,1,0:T(8,128)(2,1)S(1)} %pad_maximum_fusion.1), channel_id=1, source_target_pairs={{0,1},{1,2},{2,3},{3,4},{4,5},{5,6},{6,7},{7,0},{8,9},{9,10},{10,1... | collective-permute-start | bytes 294920 | tf_op jit(solution)/shard_map/ppermute | solution.py:21
  136.5 7.8 %collective-permute-start.3 = (bf16[3,1,32,512]{3,2,1,0:T(8,128)(2,1)S(1)}, bf16[3,1,32,512]{3,2,1,0:T(8,128)(2,1)S(1)}, u32[]{:S(2)}, u32[]{:S(2)}) collective-permute-start(bf16[3,1,32,512]{3,2,1,0:T(8,128)(2,1)S(1)} %pad_maximum_fusion.1), channel_id=1, source_target_pairs={{1,0},{2,1},{3,2},{4,3},{5,4},{6,5},{7,6},{0,7},{9,8},{10,9},{11,1... | collective-permute-start | bytes 294920 | tf_op jit(solution)/shard_map/ppermute | solution.py:23
  141.4 4.9 %copy-start.6 = (pred[8]{0:T(512)(128)(4,1)S(1)}, pred[8]{0:T(512)(128)(4,1)}, u32[]{:S(2)}) copy-start(pred[8]{0:T(512)(128)(4,1)} %get-tuple-element.43) | copy-start | bytes 28
  146.4 1.3 copy-start.10
  147.6 1.0 copy-start.3
  148.2 1.0 copy-start.2
where the time goes:
time: 151 us; the launch traced here: 150 us
  blocking collectives  101 us (67%)
  starting transfers between devices  14 us (9%)
  matrix products  13.6 us (9%)
  local copies, waits for them, and re-layouts  12.9 us (9%)
  other arithmetic  5.87 us (4%)
  waiting for transfers between devices  2.15 us (1%)
    all_gather x1, blocking collectives, on_device(): every_pos = lax.all_gather(positions, ('rows', 'cols'), axis=1, tiled=True)  69.9 us
    all_gather x1, blocking collectives, on_device(): piece = lax.all_gather(key_vals, 'cols', axis=2, tiled=True)  31.2 us
    ppermute x2, starting transfers between devices, with_halo(): lax.ppermute(head, axis, [((i + 1) % count, i) for i in range(count)])  6.68 us
    all_to_all x1, starting transfers between devices, on_device(): lax.all_to_all(grouped, 'rows', split_axis=1, concat_axis=2, tiled=True)  3.52 us
    all_to_all x1, starting transfers between devices, on_device(): lax.all_to_all(head_out, 'rows', split_axis=1, concat_axis=0, tiled=True)  3.26 us
  transfers between devices with their start and end apart: 6, of which 1 were waited for; matrix products, arithmetic and copies ran while one was open for 16% of the time, Pallas kernels for 0%

commit v1 on v0

--- a/solution.py
+++ b/solution.py
@@ -1,8 +1,11 @@
+import functools
 import math
 
 import jax
 import jax.numpy as jnp
 from jax import lax
+from jax.experimental import pallas as pl
+from jax.experimental.pallas import tpu as pltpu
 from jax.sharding import PartitionSpec as P
 
 rbf_step = 2.0
@@ -213,9 +216,453 @@
     return updated.astype(jnp.bfloat16)
 
 
+def mm(a, b, dims):
+    return lax.dot_general(a, b, (dims, ((), ())), preferred_element_type=jnp.float32)
+
+
+def parts_of(value, count):
+    out = []
+    for _ in range(count):
+        part = value.astype(jnp.bfloat16)
+        out.append(part)
+        value = value - part.astype(jnp.float32)
+    return out
+
+
+def unit(rows, cols, dtype):
+    r = lax.broadcasted_iota(jnp.int32, (rows, cols), 0)
+    c = lax.broadcasted_iota(jnp.int32, (rows, cols), 1)
+    return (r == c).astype(dtype)
+
+
+def to_column(row):
+    count = row.shape[1]
+    r = lax.broadcasted_iota(jnp.int32, (count, count), 0)
+    c = lax.broadcasted_iota(jnp.int32, (count, count), 1)
+    return jnp.sum(jnp.where(r == c, jnp.broadcast_to(row, (count, count)), 0.0), axis=1, keepdims=True)
+
+
+def pack_kernel(feat_ref, gain_ref, pos_ref, mate_ref, out_ref, tmp_ref):
+    atoms, dim = feat_ref.shape
+    floats = feat_ref[...].astype(jnp.float32)
+    spread = jnp.mean(floats * floats, axis=-1, keepdims=True)
+    normed = floats * lax.rsqrt(spread + 1e-06) * gain_ref[...]
+    out_ref[:, :dim] = normed.astype(jnp.bfloat16)
+    tmp_ref[...] = jnp.zeros(tmp_ref.shape, jnp.float32)
+    own = parts_of(pos_ref[...], 3)
+    mate = parts_of(mate_ref[...], 3)
+    for p in range(3):
+        tmp_ref[8 * p : 8 * p + 3, :] = own[p].astype(jnp.float32)
+        tmp_ref[8 * p + 3 : 8 * p + 6, :] = mate[p].astype(jnp.float32)
+    eye = unit(atoms, atoms, jnp.bfloat16)
+    turned = mm(eye, tmp_ref[...].astype(jnp.bfloat16), ((1,), (1,)))
+    out_ref[:, dim:] = turned.astype(jnp.bfloat16)
+
+
+def query_kernel(
+    head_dim,
+    pack_ref,
+    wqkv_ref,
+    rw_ref,
+    ro_ref,
+    pw_ref,
+    qexp_ref,
+    w1_ref,
+    w2_ref,
+    off_ref,
+):
+    atoms = pack_ref.shape[0]
+    dim = wqkv_ref.shape[0]
+    groups, rows, width = qexp_ref.shape
+    per = rows // atoms
+    q = mm(pack_ref[:, :dim], wqkv_ref[:, :dim], ((1,), (0,)))
+    q = q.astype(jnp.bfloat16).astype(jnp.float32)
+    lane = lax.broadcasted_iota(jnp.int32, (per, width), 1) // head_dim
+    sub = lax.broadcasted_iota(jnp.int32, (per, width), 0)
+    keep = (lane == sub)[None]
+    for g in range(groups):
+        part = q[:, g * width : (g + 1) * width]
+        spread = jnp.broadcast_to(part[:, None, :], (atoms, per, width))
+        spread = jnp.where(keep, spread, 0.0).reshape(rows, width)
+        qexp_ref[g] = spread.astype(jnp.bfloat16)
+    h, m, l = parts_of(rw_ref[...], 3)
+    stack = jnp.concatenate([h, h, m, h, l, m], axis=0)
+    hidden = rw_ref.shape[1]
+    w1_ref[...] = mm(unit(hidden, hidden, jnp.bfloat16), stack, ((1,), (1,))).astype(jnp.bfloat16)
+    h, l = parts_of(pw_ref[...], 2)
+    stack = jnp.concatenate([h, h, l], axis=0)
+    heads = pw_ref.shape[1]
+    w2_ref[...] = mm(unit(heads, heads, jnp.bfloat16), stack, ((1,), (1,))).astype(jnp.bfloat16)
+    off_ref[...] = jnp.broadcast_to(to_column(ro_ref[...]), off_ref.shape)
+
+
+def chosen(scalars, lane):
+    out = jnp.full(lane.shape, scalars[0])
+    for e in range(1, len(scalars)):
+        out = jnp.where(lane == e, scalars[e], out)
+    return out
+
+
+def turned_positions(rows_bf):
+    r = lax.broadcasted_iota(jnp.int32, (8, 128), 0)
+    c = lax.broadcasted_iota(jnp.int32, (8, 128), 1)
+    pick = ((c % 8 == r) & (c < 24) & (r < 6)).astype(jnp.bfloat16)
+    return mm(pick, rows_bf, ((1,), (1,)))
+
+
+def own_columns(rows_bf):
+    rows = rows_bf.astype(jnp.float32)
+    return [rows[:, c : c + 1] + rows[:, c + 8 : c + 9] + rows[:, c + 16 : c + 17] for c in range(3)]
+
+
+def wave_feats(pos8):
+    angle = two_pi * pos8
+    return jnp.cos(angle), jnp.sin(angle)
+
+
+def cosine_rows(own_cols, feats):
+    cos_k, sin_k = feats
+    total = None
+    for c in range(3):
+        angle = two_pi * own_cols[c]
+        term = jnp.cos(angle) * cos_k[c : c + 1] + jnp.sin(angle) * sin_k[c : c + 1]
+        total = term if total is None else total + term
+    return total
+
+
+def attend(qexp, keys, vals, scale, bias3):
+    rows = qexp.shape[0]
+    count = keys.shape[0]
+    atoms, per, _ = bias3.shape
+    s = mm(qexp, keys, ((1,), (1,))).reshape(atoms, per, count) * scale + bias3
+    top = jnp.max(s, axis=-1, keepdims=True)
+    p = jnp.exp(s - top)
+    total = jnp.sum(p, axis=-1, keepdims=True)
+    o = mm(p.astype(jnp.bfloat16).reshape(rows, count), vals, ((1,), (0,)))
+    return top, total, o.reshape(atoms, per, vals.shape[1])
+
+
+def early_kernel(
+    head_dim,
+    slot_ref,
+    mate_ref,
+    shift_ref,
+    cell_ref,
+    pack_ref,
+    wqkv_ref,
+    qexp_ref,
+    w1_ref,
+    w2_ref,
+    off_ref,
+    str_ref,
+    kv_ref,
+    acc_ref,
+    top_ref,
+    sum_ref,
+    bias_ref,
+    feat_ref,
+    loc_ref,
+):
+    dim = wqkv_ref.shape[0]
+    atoms = acc_ref.shape[1]
+    groups, rows, width = qexp_ref.shape
+    per = rows // atoms
+    kv = mm(pack_ref[:, :dim], wqkv_ref[:, dim:], ((1,), (0,)))
+    kv_ref[...] = kv.astype(jnp.bfloat16)
+    own = own_columns(pack_ref[:atoms, dim:])
+    pos8 = turned_positions(pack_ref[:, dim:])
+    cos8, sin8 = wave_feats(pos8)
+    feat_ref[0] = cos8
+    feat_ref[1] = sin8
+    waves = cosine_rows(own, (cos8, sin8))
+    strength = to_column(str_ref[...])
+    scale = head_dim ** (-0.5)
+    for g in range(groups):
+        low, high = g * width, (g + 1) * width
+        bias3 = strength[g * per : (g + 1) * per][None] * waves[:, None, :]
+        top, total, o = attend(
+            qexp_ref[g], kv_ref[:, low:high], kv_ref[:, dim + low : dim + high], scale, bias3
+        )
+        acc_ref[g] = o
+        top_ref[g] = jnp.broadcast_to(top, top_ref.shape[1:])
+        sum_ref[g] = jnp.broadcast_to(total, sum_ref.shape[1:])
+    entries = slot_ref.shape[0]
+    for e in range(entries):
+        start = pl.multiple_of(slot_ref[e] * atoms, atoms)
+        loc_ref[e * atoms : (e + 1) * atoms, :] = pack_ref[pl.ds(start, atoms), dim:]
+    near = turned_positions(loc_ref[...])
+    listed = entries * atoms
+    lane = lax.broadcasted_iota(jnp.int32, (1, listed), 1) // atoms
+    from_mate = chosen([mate_ref[e] for e in range(entries)], lane) > 0
+    square = None
+    for c in range(3):
+        at = jnp.where(from_mate, near[c + 3 : c + 4], near[c : c + 1])
+        at = at + chosen([shift_ref[c, e] for e in range(entries)], lane).astype(jnp.float32)
+        gap = (at - own[c]) * cell_ref[c]
+        square = gap * gap if square is None else square + gap * gap
+    dist = jnp.sqrt(square + 0.25)
+    nrbf = w1_ref.shape[1] // 6
+    centers = lax.broadcasted_iota(jnp.int32, (nrbf, 1), 0).astype(jnp.float32) * rbf_step
+    offset = off_ref[:, :1]
+    step = 4
+    for i in range(0, atoms, step):
+        radial = jnp.concatenate(
+            [
+                jnp.exp(-((dist[j : j + 1] - centers) ** 2) * (0.5 / rbf_width**2))
+                for j in range(i, i + step)
+            ],
+            axis=1,
+        )
+        h, m, l = parts_of(radial, 3)
+        stack = jnp.concatenate([h, m, h, l, h, m], axis=0)
+        u = mm(w1_ref[...], stack, ((1,), (0,))) + offset
+        u = u / (1.0 + jnp.exp(-u))
+        h, l = parts_of(u, 2)
+        pair = mm(w2_ref[...], jnp.concatenate([h, l, h], axis=0), ((1,), (0,)))
+        for j in range(step):
+            for g in range(groups):
+                bias_ref[g, i + j] = pair[
+                    g * per : (g + 1) * per, j * listed : (j + 1) * listed
+                ]
+
+
+def late_kernel(
+    head_dim,
+    slot_ref,
+    valid_ref,
+    pack_ref,
+    feat_ref,
+    wqkv_ref,
+    wout_ref,
+    qexp_ref,
+    str_ref,
+    own_ref,
+    kv_ref,
+    acc_ref,
+    top_ref,
+    sum_ref,
+    bias_ref,
+    in_ref,
+    out_ref,
+    kv2_ref,
+    near_ref,
+):
+    dim = wqkv_ref.shape[0]
+    atoms = acc_ref.shape[1]
+    groups, rows, width = qexp_ref.shape
+    per = rows // atoms
+    half = kv_ref.shape[0]
+    kv2 = mm(pack_ref[:, :dim], wqkv_ref[:, dim:], ((1,), (0,)))
+    kv2_ref[half:, :] = kv2.astype(jnp.bfloat16)
+    kv2_ref[:half, :] = kv_ref[...]
+    entries = slot_ref.shape[0]
+    for e in range(entries):
+        start = pl.multiple_of(slot_ref[e] * atoms, atoms)
+        near_ref[e * atoms : (e + 1) * atoms, :] = kv2_ref[pl.ds(start, atoms), :]
+    own = own_columns(own_ref[:, dim:])
+    waves = cosine_rows(own, (feat_ref[0, 3:6], feat_ref[1, 3:6]))
+    strength = to_column(str_ref[...])
+    scale = head_dim ** (-0.5)
+    listed = entries * atoms
+    lane = lax.broadcasted_iota(jnp.int32, (1, 1, listed), 2) // atoms
+    live = chosen([valid_ref[e] for e in range(entries)], lane) > 0
+    block = lax.broadcasted_iota(jnp.int32, (1, per, width), 2) // head_dim
+    keep = block == lax.broadcasted_iota(jnp.int32, (1, per, width), 1)
+    pieces = []
+    for g in range(groups):
+        low, high = g * width, (g + 1) * width
+        bias3 = strength[g * per : (g + 1) * per][None] * waves[:, None, :]
+        top, total, o = attend(
+            qexp_ref[g],
+            kv2_ref[half:, low:high],
+            kv2_ref[half:, dim + low : dim + high],
+            scale,
+            bias3,
+        )
+        top1 = top_ref[g][:, :, :1]
+        best = jnp.maximum(top, top1)
+        a, b = jnp.exp(top1 - best), jnp.exp(top - best)
+        denom = a * sum_ref[g][:, :, :1] + b * total
+        far = (a / denom) * acc_ref[g] + (b / denom) * o
+        far = jnp.sum(jnp.where(keep, far, 0.0), axis=1).astype(jnp.bfloat16)
+        s = mm(qexp_ref[g], near_ref[:, low:high], ((1,), (1,)))
+        s = s.reshape(atoms, per, listed) * scale + bias_ref[g]
+        s = jnp.where(live, s, -1e30)
+        p = jnp.exp(s - jnp.max(s, axis=-1, keepdims=True))
+        total = jnp.sum(p, axis=-1, keepdims=True)
+        o = mm(
+            p.astype(jnp.bfloat16).reshape(rows, listed),
+            near_ref[:, dim + low : dim + high],
+            ((1,), (0,)),
+        )
+        o = o.reshape(atoms, per, width) / total
+        close = jnp.sum(jnp.where(keep, o, 0.0), axis=1).astype(jnp.bfloat16)
+        pieces.append((close.astype(jnp.float32) + far.astype(jnp.float32)).astype(jnp.bfloat16))
+    combined = jnp.concatenate(pieces, axis=1)
+    moved = mm(combined, wout_ref[...], ((1,), (0,)))
+    out_ref[...] = (in_ref[...].astype(jnp.float32) + moved).astype(jnp.bfloat16)
+
+
+def call(kernel, outs, scratch, smem, args):
+    specs = [pl.BlockSpec(memory_space=pltpu.SMEM)] * smem
+    specs += [pl.BlockSpec(memory_space=pltpu.VMEM)] * (len(args) - smem)
+    many = isinstance(outs, list)
+    vmem = pl.BlockSpec(memory_space=pltpu.VMEM)
+    return pl.pallas_call(
+        kernel,
+        out_shape=outs,
+        in_specs=specs,
+        out_specs=[vmem] * len(outs) if many else vmem,
+        scratch_shapes=scratch,
+    )(*args)
+
+
+def xor_phases(row_count, col_count):
+    col_bits = col_count.bit_length() - 1
+    row_bits = row_count.bit_length() - 1
+    first = list(range(1, col_bits))
+    second = [0] + list(range(col_bits + 1, col_bits + row_bits))
+    return first, second, [col_bits]
+
+
+def spread_bits(number, bits):
+    return sum(((number >> k) & 1) << bit for k, bit in enumerate(bits))
+
+
+def on_device_small(
+    features,
+    positions,
+    cell_lengths,
+    block_lists,
+    image_offsets,
+    block_valid,
+    norm_gain,
+    w_qkv,
+    w_out,
+    rbf_weight,
+    rbf_offset,
+    pair_weight,
+    cosine_scale,
+):
+    atoms, dim = features.shape
+    heads = pair_weight.shape[1]
+    hidden = pair_weight.shape[0]
+    nrbf = rbf_weight.shape[0]
+    head_dim = dim // heads
+    row_count = lax.axis_size("rows")
+    col_count = lax.axis_size("cols")
+    total = row_count * col_count
+    axes = ("rows", "cols")
+    me = lax.axis_index("rows") * col_count + lax.axis_index("cols")
+    phases = xor_phases(row_count, col_count)
+    entries = block_lists.shape[1]
+    width = 256
+    per = width // head_dim
+    groups = heads // per
+    rows = atoms * per
+    half = total // 2 * atoms
+    f32, bf16 = jnp.float32, jnp.bfloat16
+    shape = jax.ShapeDtypeStruct
+
+    def swap(array, mask):
+        return lax.ppermute(array, axes, [(i, i ^ mask) for i in range(total)])
+
+    def gathered(array, bits):
+        got = [swap(array, spread_bits(d, bits)) for d in range(1, 1 << len(bits))]
+        return jnp.concatenate([array] + got, axis=0)
+
+    rel = block_lists[0] ^ me
+    slot = jnp.zeros_like(rel)
+    stride = 1
+    for bits in phases[:2]:
+        for bit in bits:
+            slot = slot + ((rel >> bit) & 1) * stride
+            stride = stride * 2
+    from_mate = (rel >> phases[2][0]) & 1
+    full_slot = slot + from_mate * stride
+    mate = swap(positions, 1 << phases[2][0])
+    pack = call(
+        pack_kernel,
+        shape((atoms, dim + 128), bf16),
+        [pltpu.VMEM((128, atoms), f32)],
+        0,
+        (features, norm_gain[None], positions, mate),
+    )
+    near = gathered(pack, phases[0])
+    qexp, w1, w2, off = call(
+        functools.partial(query_kernel, head_dim),
+        [
+            shape((groups, rows, width), bf16),
+            shape((hidden, 6 * nrbf), bf16),
+            shape((heads, 3 * hidden), bf16),
+            shape((hidden, 128), f32),
+        ],
+        [],
+        0,
+        (pack, w_qkv, rbf_weight, rbf_offset[None], pair_weight),
+    )
+    mine = gathered(near, phases[1])
+    other = swap(mine, 1 << phases[2][0])
+    kv, acc, top, summed, bias, feats = call(
+        functools.partial(early_kernel, head_dim),
+        [
+            shape((half, 2 * dim), bf16),
+            shape((groups, atoms, per, width), f32),
+            shape((groups, atoms, per, 128), f32),
+            shape((groups, atoms, per, 128), f32),
+            shape((groups, atoms, per, entries * atoms), f32),
+            shape((2, 8, half), f32),
+        ],
+        [pltpu.VMEM((entries * atoms, 128), bf16)],
+        4,
+        (
+            slot,
+            from_mate,
+            image_offsets[:, 0, :],
+            cell_lengths,
+            mine,
+            w_qkv,
+            qexp,
+            w1,
+            w2,
+            off,
+            cosine_scale[None],
+        ),
+    )
+    return call(
+        functools.partial(late_kernel, head_dim),
+        shape((atoms, dim), bf16),
+        [
+            pltpu.VMEM((2 * half, 2 * dim), bf16),
+            pltpu.VMEM((entries * atoms, 2 * dim), bf16),
+        ],
+        2,
+        (
+            full_slot,
+            block_valid[0],
+            other,
+            feats,
+            w_qkv,
+            w_out,
+            qexp,
+            cosine_scale[None],
+            pack,
+            kv,
+            acc,
+            top,
+            summed,
+            bias,
+            features,
+        ),
+    )
+
+
 def solution(mesh):
+    row_count, col_count = mesh.shape["rows"], mesh.shape["cols"]
+    small = row_count * col_count <= 64
+    body = on_device_small if small else on_device
     return jax.shard_map(
-        on_device,
+        body,
         mesh=mesh,
         in_specs=(
             P(("rows", "cols"), None),

time: 151 us -> 42.7 us (0.28)
  blocking collectives: 101 us -> 0 us
  Pallas kernels: 0 us -> 15.2 us
  matrix products: 13.6 us -> 0 us
  waiting for transfers between devices: 2.15 us -> 12.3 us
  local copies, waits for them, and re-layouts: 12.9 us -> 3.71 us
  other arithmetic: 5.87 us -> 1.37 us
  starting transfers between devices: 14 us -> 9.68 us
    all_gather x2 -> x0, blocking collectives: 101 us -> none  [the longest x1 69.9 us: on_device(): every_pos = lax.all_gather(positions, ('rows', 'cols'), axis=1, tiled=True)]
    pallas_call x0 -> x4, Pallas kernels: none -> 15.2 us  [call(): pl.pallas_call(kernel, out_shape=outs, in_specs=specs, out_specs=[vmem] *...]
    dot_general x10 -> x0, matrix products: 13.6 us -> none  [the longest x1 2.4 us: update(): jnp.einsum('hqk,hkd->hdq', prob_bf, kv_block[1], preferred_element_type=j...]
    ppermute x4 -> x8, waiting for transfers between devices: 2.15 us -> 12.3 us  [swap(): return lax.ppermute(array, axes, [(i, i ^ mask) for i in range(total)])]
    all_to_all x2 -> x0, starting transfers between devices: 6.78 us -> none  [the longest x1 3.52 us: on_device(): lax.all_to_all(grouped, 'rows', split_axis=1, concat_axis=2, tiled=True)]
    unnamed x34 -> x20, local copies, waits for them, and re-layouts: 0.45 us -> 3.69 us
    squeeze x2 -> x0, local copies, waits for them, and re-layouts: 3.13 us -> none  [the longest x1 1.56 us: update(): kv_block[1]]
    reshape x12 -> x0, local copies, waits for them, and re-layouts: 3.09 us -> none  [the longest x2 1.14 us: on_device(): grouped = packed.reshape(atom_count, 3, head_count, head_dim).transpose(1...]
  transfers between devices with their start and end apart: 6 -> 8, of which waited for: 1 -> 6; matrix products, arithmetic and copies ran while one was open for 16% -> 7% of each run, Pallas kernels for 0% -> 19%
where the time goes in v1:
time: 42.7 us; the launch traced here: 42.3 us
  Pallas kernels  15.2 us (36%)
  waiting for transfers between devices  12.3 us (29%)
  starting transfers between devices  9.68 us (23%)
  local copies, waits for them, and re-layouts  3.71 us (9%)
  other arithmetic  1.37 us (3%)
    pallas_call x4, Pallas kernels, call(): pl.pallas_call(kernel, out_shape=outs, in_specs=specs, out_specs=[vmem] *...  15.2 us
    ppermute x8, waiting for transfers between devices, swap(): return lax.ppermute(array, axes, [(i, i ^ mask) for i in range(total)])  12.3 us
    ppermute x8, starting transfers between devices, swap(): return lax.ppermute(array, axes, [(i, i ^ mask) for i in range(total)])  9.68 us
    unnamed x20, local copies, waits for them, and re-layouts  3.69 us
  transfers between devices with their start and end apart: 8, of which 6 were waited for; matrix products, arithmetic and copies ran while one was open for 7% of the time, Pallas kernels for 19%

profile of v1, /device:TPU:0, one launch (start us, length us, event | category | flops | bytes accessed | tf_op | source)
XLA Modules:
  0.0 42.3 jit_solution(17713122486611551648)
XLA Ops:
  0.0 0.0 copy-start.2
  0.0 0.0 copy-start.4
  0.0 0.0 copy-start.5
  0.0 0.6 %collective-permute-start = (f32[3,32]{1,0:T(4,128)}, f32[3,32]{1,0:T(4,128)S(1)}, u32[]{:S(2)}, u32[]{:S(2)}) collective-permute-start(f32[3,32]{1,0:T(4,128)} %pos_ref.1), channel_id=1, source_target_pairs={{0,8},{1,9},{2,10},{3,11},{4,12},{5,13},{6,14},{7,15},{8,0},{9,1},... | collective-permute-start | bytes 1160 | tf_op jit(solution)/shard_map/ppermute | solution.py:568
  0.6 1.0 %collective-permute-done.mate_ref = f32[3,32]{1,0:T(4,128)S(1)} collective-permute-done((f32[3,32]{1,0:T(4,128)}, f32[3,32]{1,0:T(4,128)S(1)}, u32[]{:S(2)}, u32[]{:S(2)}) %collective-permute-start) | collective-permute-done | bytes 416 | tf_op jit(solution)/shard_map/ppermute | solution.py:568
  1.6 0.0 copy-start.3
  1.6 0.6 %copy-done.3 = f32[3,32]{1,0:T(4,128)} copy-done((f32[3,32]{1,0:T(4,128)}, f32[3,32]{1,0:T(4,128)S(1)}, u32[]{:S(2)}) %copy-start.3) | copy-done | bytes 408
  2.2 1.6 %shard_map.127.pack_ref.own_ref = bf16[32,640]{1,0:T(8,128)(2,1)} custom-call(bf16[32,512]{1,0:T(8,128)(2,1)} %in_ref.1, f32[1,512]{1,0:T(1,128)} %bitcast.16, f32[3,32]{1,0:T(4,128)} %pos_ref.1, f32[3,32]{1,0:T(4,128)} %copy-done.3), custom_call_target="tpu_custom_call" | custom-call | tf_op jit(solution)/shard_map/pallas_call | solution.py:511
  3.7 2.9 %collective-permute-start.1 = (bf16[32,640]{1,0:T(8,128)(2,1)}, bf16[32,640]{1,0:T(8,128)(2,1)S(1)}, u32[]{:S(2)}, u32[]{:S(2)}) collective-permute-start(bf16[32,640]{1,0:T(8,128)(2,1)} %shard_map.127.pack_ref.own_ref), channel_id=1, source_target_pairs={{0,2},{1,3},{2,0},{3,1},{4,6},{5,7},{6,4},{7,5},{8,10},{9,11},{10,... | collective-permute-start | bytes 122888 | tf_op jit(solution)/shard_map/ppermute | solution.py:568
  6.6 2.6 %collective-permute-start.2 = (bf16[32,640]{1,0:T(8,128)(2,1)}, bf16[32,640]{1,0:T(8,128)(2,1)S(1)}, u32[]{:S(2)}, u32[]{:S(2)}) collective-permute-start(bf16[32,640]{1,0:T(8,128)(2,1)} %shard_map.127.pack_ref.own_ref), channel_id=1, source_target_pairs={{0,4},{1,5},{2,6},{3,7},{4,0},{5,1},{6,2},{7,3},{8,12},{9,13},{10,... | collective-permute-start | bytes 122888 | tf_op jit(solution)/shard_map/ppermute | solution.py:568
  9.2 0.0 collective-permute-start.3
  9.2 0.8 %constant_dynamic-update-slice_fusion.6 = bf16[512,640]{1,0:T(8,128)(2,1)S(1)} fusion(bf16[32,640]{1,0:T(8,128)(2,1)} %shard_map.127.pack_ref.own_ref), kind=kLoop, calls=%fused_computation.7 | loop fusion | bytes 81920
  10.1 0.0 collective-permute-done.1
  10.1 2.5 %collective-permute-done.2 = bf16[32,640]{1,0:T(8,128)(2,1)S(1)} collective-permute-done((bf16[32,640]{1,0:T(8,128)(2,1)}, bf16[32,640]{1,0:T(8,128)(2,1)S(1)}, u32[]{:S(2)}, u32[]{:S(2)}) %collective-permute-start.2) | collective-permute-done | bytes 40992 | tf_op jit(solution)/shard_map/ppermute | solution.py:568
  12.6 2.7 %collective-permute-done.3 = bf16[32,640]{1,0:T(8,128)(2,1)S(1)} collective-permute-done((bf16[32,640]{1,0:T(8,128)(2,1)}, bf16[32,640]{1,0:T(8,128)(2,1)S(1)}, u32[]{:S(2)}, u32[]{:S(2)}) %collective-permute-start.3) | collective-permute-done | bytes 40992 | tf_op jit(solution)/shard_map/ppermute | solution.py:568
  15.2 0.8 %pad_maximum_fusion = bf16[128,640]{1,0:T(8,128)(2,1)S(1)} fusion(bf16[32,640]{1,0:T(8,128)(2,1)S(1)} %collective-permute-done.3, bf16[32,640]{1,0:T(8,128)(2,1)S(1)} %collective-permute-done.2, bf16[32,640]{1,0:T(8,128)(2,1)S(1)} %collective-permute-done.1, bf16[32,640]{1,0:T(8,128)(2,1)} %shard_map.127.pack_ref.own_ref), kind=kLoop, calls=%fused_computation | loop fusion | flops 655360 | bytes 327680 | tf_op jit(solution)/shard_map/concatenate | solution.py:572
  16.0 1.6 %collective-permute-start.4 = (bf16[128,640]{1,0:T(8,128)(2,1)S(1)}, bf16[128,640]{1,0:T(8,128)(2,1)S(1)}, u32[]{:S(2)}, u32[]{:S(2)}) collective-permute-start(bf16[128,640]{1,0:T(8,128)(2,1)S(1)} %pad_maximum_fusion), channel_id=1, source_target_pairs={{0,1},{1,0},{2,3},{3,2},{4,5},{5,4},{6,7},{7,6},{8,9},{9,8},{10,11... | collective-permute-start | bytes 491528 | tf_op jit(solution)/shard_map/ppermute | solution.py:568
  17.6 1.5 %collective-permute-start.5 = (bf16[128,640]{1,0:T(8,128)(2,1)S(1)}, bf16[128,640]{1,0:T(8,128)(2,1)S(1)}, u32[]{:S(2)}, u32[]{:S(2)}) collective-permute-start(bf16[128,640]{1,0:T(8,128)(2,1)S(1)} %pad_maximum_fusion), channel_id=1, source_target_pairs={{0,16},{1,17},{2,18},{3,19},{4,20},{5,21},{6,22},{7,23},{8,24},{9,... | collective-permute-start | bytes 491528 | tf_op jit(solution)/shard_map/ppermute | solution.py:568
  19.1 0.5 %collective-permute-start.6 = (bf16[128,640]{1,0:T(8,128)(2,1)S(1)}, bf16[128,640]{1,0:T(8,128)(2,1)S(1)}, u32[]{:S(2)}, u32[]{:S(2)}) collective-permute-start(bf16[128,640]{1,0:T(8,128)(2,1)S(1)} %pad_maximum_fusion), channel_id=1, source_target_pairs={{0,17},{1,16},{2,19},{3,18},{4,21},{5,20},{6,23},{7,22},{8,25},{9,... | collective-permute-start | bytes 491528 | tf_op jit(solution)/shard_map/ppermute | solution.py:568
  19.6 3.3 %collective-permute-done.4 = bf16[128,640]{1,0:T(8,128)(2,1)S(1)} collective-permute-done((bf16[128,640]{1,0:T(8,128)(2,1)S(1)}, bf16[128,640]{1,0:T(8,128)(2,1)S(1)}, u32[]{:S(2)}, u32[]{:S(2)}) %collective-permute-start.4) | collective-permute-done | bytes 163872 | tf_op jit(solution)/shard_map/ppermute | solution.py:568
  23.0 0.7 %collective-permute-done.5 = bf16[128,640]{1,0:T(8,128)(2,1)S(1)} collective-permute-done((bf16[128,640]{1,0:T(8,128)(2,1)S(1)}, bf16[128,640]{1,0:T(8,128)(2,1)S(1)}, u32[]{:S(2)}, u32[]{:S(2)}) %collective-permute-start.5) | collective-permute-done | bytes 163872 | tf_op jit(solution)/shard_map/ppermute | solution.py:568
  23.7 2.0 %collective-permute-done.6 = bf16[128,640]{1,0:T(8,128)(2,1)S(1)} collective-permute-done((bf16[128,640]{1,0:T(8,128)(2,1)S(1)}, bf16[128,640]{1,0:T(8,128)(2,1)S(1)}, u32[]{:S(2)}, u32[]{:S(2)}) %collective-permute-start.6) | collective-permute-done | bytes 163872 | tf_op jit(solution)/shard_map/ppermute | solution.py:568
  25.8 0.0 copy-start
  25.8 0.1 collective-permute-start.7
  25.9 0.0 copy-done.2
  25.9 0.7 %copy.14.pw_ref = f32[64,16]{1,0:T(8,128)} copy(f32[64,16]{0,1:T(8,128)S(1)} %copy-done.2) | data formatting | bytes 8192 | tf_op args[11]
  26.6 0.0 copy-done.4
  26.6 0.6 %copy.17 = s32[3,1,8]{2,0,1:T(4,128)} copy(s32[3,1,8]{2,1,0:T(1,128)S(1)} %copy-done.4) | data formatting | bytes 192
  27.2 0.0 copy-done.5
  27.2 0.6 %multiply_add_fusion = (s32[8]{0:T(128)}, s32[8]{0:T(128)}, s32[8]{0:T(128)}) fusion(s32[1,8]{1,0:T(1,128)S(1)} %copy-done.5, s32[]{:T(128)S(6)} %add.15), kind=kLoop, calls=%fused_computation.10 | loop fusion | flops 152 | bytes 132 | tf_op jit(solution)/shard_map/add | solution.py:582
  27.8 2.4 %shard_map.128 = (bf16[2,256,256]{2,1,0:T(8,128)(2,1)}, bf16[64,96]{1,0:T(8,128)(2,1)}, bf16[16,192]{1,0:T(8,128)(2,1)}, f32[64,128]{1,0:T(8,128)}) custom-call(bf16[32,640]{1,0:T(8,128)(2,1)} %shard_map.127.pack_ref.own_ref, bf16[512,1536]{1,0:T(8,128)(2,1)} %wqkv_ref.5, f32[16,64]{1,0:T(8,128)} %rw_ref.1, f32[1,64]{1,0:T(1,128)} %bitcast.17, ...), custom_call_target="tpu_custom_call" | custom-call | tf_op jit(solution)/shard_map/pallas_call | solution.py:511
  30.2 0.0 copy-done
  30.2 5.7 %shard_map.129 = (bf16[512,1024]{1,0:T(8,128)(2,1)}, f32[2,32,8,256]{3,2,1,0:T(8,128)}, f32[2,32,8,128]{3,2,1,0:T(8,128)}, f32[2,32,8,128]{3,2,1,0:T(8,128)}, f3...) custom-call(s32[8]{0:T(128)} %get-tuple-element.27.slot_ref, s32[8]{0:T(128)} %get-tuple-element.26.mate_ref, ...), custom_call_target="tpu_custom_call" | custom-call | tf_op jit(solution)/shard_map/pallas_call | solution.py:511
  35.9 0.0 collective-permute-done.7.pack_ref
  35.9 0.0 copy-start.1
  35.9 0.9 %copy-done.1 = bf16[512,640]{1,0:T(8,128)(2,1)} copy-done((bf16[512,640]{1,0:T(8,128)(2,1)}, bf16[512,640]{1,0:T(8,128)(2,1)S(1)}, u32[]{:S(2)}) %copy-start.1) | copy-done | bytes 655384
  36.8 5.6 %shard_map.130 = bf16[32,512]{1,0:T(8,128)(2,1)} custom-call(s32[8]{0:T(128)} %get-tuple-element.25.slot_ref, s32[8]{0:T(128)} %bitcast.18, bf16[512,640]{1,0:T(8,128)(2,1)} %copy-done.1, f32[2,8,512]{2,1,0:T(8,128)} %get-tuple-element.19.feat_ref, bf16[512,1536]{1,0:T(8,128)(2,1)} %wqkv_ref.5, bf16[512,512]{1,0:T(8,128)(2,1)} %wout_ref.1, ...), custom_call_target="tpu_custom_call" | custom-call | tf_op jit(solution)/shard_map/pallas_call | solution.py:511
  (6 shorter events, 0.1 us)
Async XLA Ops:
  0.0 25.9 %copy-start.2 = (f32[64,16]{0,1:T(8,128)S(1)}, f32[64,16]{0,1:T(8,128)}, u32[]{:S(2)}) copy-start(f32[64,16]{0,1:T(8,128)} %param.24) | copy-start | bytes 12292
  0.0 26.6 %copy-start.4 = (s32[3,1,8]{2,1,0:T(1,128)S(1)}, s32[3,1,8]{2,1,0:T(1,128)}, u32[]{:S(2)}) copy-start(s32[3,1,8]{2,1,0:T(1,128)} %param.17) | copy-start | bytes 292
  0.0 27.2 %copy-start.5 = (s32[1,8]{1,0:T(1,128)S(1)}, s32[1,8]{1,0:T(1,128)}, u32[]{:S(2)}) copy-start(s32[1,8]{1,0:T(1,128)} %param.16) | copy-start | bytes 100
  0.0 1.6 %collective-permute-start = (f32[3,32]{1,0:T(4,128)}, f32[3,32]{1,0:T(4,128)S(1)}, u32[]{:S(2)}, u32[]{:S(2)}) collective-permute-start(f32[3,32]{1,0:T(4,128)} %pos_ref.1), channel_id=1, source_target_pairs={{0,8},{1,9},{2,10},{3,11},{4,12},{5,13},{6,14},{7,15},{8,0},{9,1},... | collective-permute-start | bytes 1160 | tf_op jit(solution)/shard_map/ppermute | solution.py:568
  1.6 0.6 %copy-start.3 = (f32[3,32]{1,0:T(4,128)}, f32[3,32]{1,0:T(4,128)S(1)}, u32[]{:S(2)}) copy-start(f32[3,32]{1,0:T(4,128)S(1)} %collective-permute-done.mate_ref) | copy-start | bytes 1156
  3.7 6.3 %collective-permute-start.1 = (bf16[32,640]{1,0:T(8,128)(2,1)}, bf16[32,640]{1,0:T(8,128)(2,1)S(1)}, u32[]{:S(2)}, u32[]{:S(2)}) collective-permute-start(bf16[32,640]{1,0:T(8,128)(2,1)} %shard_map.127.pack_ref.own_ref), channel_id=1, source_target_pairs={{0,2},{1,3},{2,0},{3,1},{4,6},{5,7},{6,4},{7,5},{8,10},{9,11},{10,... | collective-permute-start | bytes 122888 | tf_op jit(solution)/shard_map/ppermute | solution.py:568
  6.6 5.9 %collective-permute-start.2 = (bf16[32,640]{1,0:T(8,128)(2,1)}, bf16[32,640]{1,0:T(8,128)(2,1)S(1)}, u32[]{:S(2)}, u32[]{:S(2)}) collective-permute-start(bf16[32,640]{1,0:T(8,128)(2,1)} %shard_map.127.pack_ref.own_ref), channel_id=1, source_target_pairs={{0,4},{1,5},{2,6},{3,7},{4,0},{5,1},{6,2},{7,3},{8,12},{9,13},{10,... | collective-permute-start | bytes 122888 | tf_op jit(solution)/shard_map/ppermute | solution.py:568
  9.2 6.0 %collective-permute-start.3 = (bf16[32,640]{1,0:T(8,128)(2,1)}, bf16[32,640]{1,0:T(8,128)(2,1)S(1)}, u32[]{:S(2)}, u32[]{:S(2)}) collective-permute-start(bf16[32,640]{1,0:T(8,128)(2,1)} %shard_map.127.pack_ref.own_ref), channel_id=1, source_target_pairs={{0,6},{1,7},{2,4},{3,5},{4,2},{5,3},{6,0},{7,1},{8,14},{9,15},{10,... | collective-permute-start | bytes 122888 | tf_op jit(solution)/shard_map/ppermute | solution.py:568
  16.0 6.9 %collective-permute-start.4 = (bf16[128,640]{1,0:T(8,128)(2,1)S(1)}, bf16[128,640]{1,0:T(8,128)(2,1)S(1)}, u32[]{:S(2)}, u32[]{:S(2)}) collective-permute-start(bf16[128,640]{1,0:T(8,128)(2,1)S(1)} %pad_maximum_fusion), channel_id=1, source_target_pairs={{0,1},{1,0},{2,3},{3,2},{4,5},{5,4},{6,7},{7,6},{8,9},{9,8},{10,11... | collective-permute-start | bytes 491528 | tf_op jit(solution)/shard_map/ppermute | solution.py:568
  17.6 6.1 %collective-permute-start.5 = (bf16[128,640]{1,0:T(8,128)(2,1)S(1)}, bf16[128,640]{1,0:T(8,128)(2,1)S(1)}, u32[]{:S(2)}, u32[]{:S(2)}) collective-permute-start(bf16[128,640]{1,0:T(8,128)(2,1)S(1)} %pad_maximum_fusion), channel_id=1, source_target_pairs={{0,16},{1,17},{2,18},{3,19},{4,20},{5,21},{6,22},{7,23},{8,24},{9,... | collective-permute-start | bytes 491528 | tf_op jit(solution)/shard_map/ppermute | solution.py:568
  19.1 6.7 %collective-permute-start.6 = (bf16[128,640]{1,0:T(8,128)(2,1)S(1)}, bf16[128,640]{1,0:T(8,128)(2,1)S(1)}, u32[]{:S(2)}, u32[]{:S(2)}) collective-permute-start(bf16[128,640]{1,0:T(8,128)(2,1)S(1)} %pad_maximum_fusion), channel_id=1, source_target_pairs={{0,17},{1,16},{2,19},{3,18},{4,21},{5,20},{6,23},{7,22},{8,25},{9,... | collective-permute-start | bytes 491528 | tf_op jit(solution)/shard_map/ppermute | solution.py:568
  25.8 4.4 %copy-start = (bf16[512,640]{1,0:T(8,128)(2,1)}, bf16[512,640]{1,0:T(8,128)(2,1)S(1)}, u32[]{:S(2)}) copy-start(bf16[512,640]{1,0:T(8,128)(2,1)S(1)} %constant_dynamic-update-slice_fusion.pack_ref) | copy-start | bytes 1966084
  25.8 10.1 %collective-permute-start.7 = (bf16[512,640]{1,0:T(8,128)(2,1)S(1)}, bf16[512,640]{1,0:T(8,128)(2,1)S(1)}, u32[]{:S(2)}, u32[]{:S(2)}) collective-permute-start(bf16[512,640]{1,0:T(8,128)(2,1)S(1)} %constant_dynamic-update-slice_fusion.pack_ref), channel_id=1, source_target_pairs={{0,8},{1,9},{2,10},{3,11},{4,12},{5,13},{6,14},{7,15},{8,0},{9,1},... | collective-permute-start | bytes 1966088 | tf_op jit(solution)/shard_map/ppermute | solution.py:568
  35.9 0.9 %copy-start.1 = (bf16[512,640]{1,0:T(8,128)(2,1)}, bf16[512,640]{1,0:T(8,128)(2,1)S(1)}, u32[]{:S(2)}) copy-start(bf16[512,640]{1,0:T(8,128)(2,1)S(1)} %collective-permute-done.7.pack_ref) | copy-start | bytes 1966084

commit v2 on v0

--- a/solution.py
+++ b/solution.py
@@ -1,9 +1,13 @@
+import functools
 import math
 
 import jax
 import jax.numpy as jnp
 from jax import lax
+from jax.experimental import pallas as pl
+from jax.experimental.pallas import tpu as pltpu
 from jax.sharding import PartitionSpec as P
+
 
 rbf_step = 2.0
 rbf_width = 2.0
@@ -193,7 +197,7 @@
         return (update(state, kv_block, key_start, block_len), None)
 
     state, _ = lax.scan(one_block, initial, (kv_blocks, block_starts))
-    run_max, run_sum, accum = state
+    _, run_sum, accum = state
     head_out = (
         (accum / run_sum[:, None, :])
         .transpose(0, 2, 1)
@@ -213,9 +217,521 @@
     return updated.astype(jnp.bfloat16)
 
 
+def mm(a, b, dims):
+    return lax.dot_general(a, b, (dims, ((), ())), preferred_element_type=jnp.float32)
+
+
+def parts_of(value, count):
+    out = []
+    for _ in range(count):
+        part = value.astype(jnp.bfloat16)
+        out.append(part)
+        value = value - part.astype(jnp.float32)
+    return out
+
+
+def unit(rows, cols, dtype):
+    r = lax.broadcasted_iota(jnp.int32, (rows, cols), 0)
+    c = lax.broadcasted_iota(jnp.int32, (rows, cols), 1)
+    return (r == c).astype(dtype)
+
+
+def to_column(row):
+    count = row.shape[1]
+    r = lax.broadcasted_iota(jnp.int32, (count, count), 0)
+    c = lax.broadcasted_iota(jnp.int32, (count, count), 1)
+    return jnp.sum(jnp.where(r == c, jnp.broadcast_to(row, (count, count)), 0.0), axis=1, keepdims=True)
+
+
+def fetch(pairs, sems):
+    copies = [pltpu.make_async_copy(src, dst, sems.at[k]) for k, (src, dst) in enumerate(pairs)]
+    for copy in copies:
+        copy.start()
+    for copy in copies:
+        copy.wait()
+
+
+def pack_kernel(feat_hbm, gain_hbm, pos_hbm, out_ref, feat_ref, gain_ref, pos_ref, tmp_ref, sems):
+    fetch(((feat_hbm, feat_ref), (gain_hbm, gain_ref), (pos_hbm, pos_ref)), sems)
+    atoms, dim = feat_ref.shape
+    floats = feat_ref[...].astype(jnp.float32)
+    spread = jnp.mean(floats * floats, axis=-1, keepdims=True)
+    normed = floats * lax.rsqrt(spread + 1e-06) * gain_ref[...]
+    out_ref[:, :dim] = normed.astype(jnp.bfloat16)
+    tmp_ref[...] = jnp.zeros(tmp_ref.shape, jnp.float32)
+    for p, part in enumerate(parts_of(pos_ref[...], 3)):
+        tmp_ref[8 * p : 8 * p + 3, :] = part.astype(jnp.float32)
+    eye = unit(atoms, atoms, jnp.bfloat16)
+    turned = mm(eye, tmp_ref[...].astype(jnp.bfloat16), ((1,), (1,)))
+    out_ref[:, dim:] = turned.astype(jnp.bfloat16)
+
+
+def query_kernel(
+    head_dim,
+    wqkv_hbm,
+    rw_hbm,
+    ro_hbm,
+    pw_hbm,
+    cs_hbm,
+    pack_ref,
+    qexp_ref,
+    w1_ref,
+    w2_ref,
+    off_ref,
+    str_ref,
+    own_ref,
+    wq_ref,
+    rw_ref,
+    ro_ref,
+    pw_ref,
+    cs_ref,
+    sems,
+):
+    atoms = pack_ref.shape[0]
+    dim = wq_ref.shape[0]
+    fetch(
+        (
+            (wqkv_hbm.at[:, pl.ds(0, dim)], wq_ref),
+            (rw_hbm, rw_ref),
+            (ro_hbm, ro_ref),
+            (pw_hbm, pw_ref),
+            (cs_hbm, cs_ref),
+        ),
+        sems,
+    )
+    groups, rows, width = qexp_ref.shape
+    per = rows // atoms
+    q = mm(pack_ref[:, :dim], wq_ref[...], ((1,), (0,)))
+    q = q.astype(jnp.bfloat16).astype(jnp.float32)
+    lane = lax.broadcasted_iota(jnp.int32, (per, width), 1) // head_dim
+    sub = lax.broadcasted_iota(jnp.int32, (per, width), 0)
+    keep = (lane == sub)[None]
+    for g in range(groups):
+        part = q[:, g * width : (g + 1) * width]
+        spread = jnp.broadcast_to(part[:, None, :], (atoms, per, width))
+        spread = jnp.where(keep, spread, 0.0).reshape(rows, width)
+        qexp_ref[g] = spread.astype(jnp.bfloat16)
+    h, m, l = parts_of(rw_ref[...], 3)
+    stack = jnp.concatenate([h, h, m, h, l, m], axis=0)
+    hidden = rw_ref.shape[1]
+    w1_ref[...] = mm(unit(hidden, hidden, jnp.bfloat16), stack, ((1,), (1,))).astype(jnp.bfloat16)
+    h, l = parts_of(pw_ref[...], 2)
+    w2_ref[...] = jnp.concatenate([h, h, l], axis=1)
+    off_ref[...] = jnp.broadcast_to(to_column(ro_ref[...]), off_ref.shape)
+    str_ref[...] = jnp.broadcast_to(to_column(cs_ref[...]), str_ref.shape)
+    pos = pack_ref[:, dim:].astype(jnp.float32)
+    pos = pos + pltpu.roll(pos, 120, 1) + pltpu.roll(pos, 112, 1)
+    own_ref[0] = pos
+    own_ref[1] = jnp.cos(two_pi * pos)
+    own_ref[2] = jnp.sin(two_pi * pos)
+
+
+def repack_kernel(*refs):
+    blocks, out_ref = refs[:-1], refs[-1]
+    atoms = blocks[0].shape[0]
+    dim = out_ref.shape[1]
+    count = atoms * len(blocks)
+    for k, block in enumerate(blocks):
+        out_ref[k * atoms : (k + 1) * atoms, :] = block[:, :dim]
+    pos = jnp.concatenate([block[:, dim:] for block in blocks], axis=0)
+    r = lax.broadcasted_iota(jnp.int32, (8, 128), 0)
+    c = lax.broadcasted_iota(jnp.int32, (8, 128), 1)
+    tail = []
+    for p in range(3):
+        pick = ((c == 8 * p + r) & (r < 3)).astype(jnp.bfloat16)
+        tail.append(mm(pick, pos, ((1,), (1,))))
+    tail.append(jnp.zeros((8, dim - 3 * count), jnp.float32))
+    out_ref[count:, :] = jnp.concatenate(tail, axis=1).astype(jnp.bfloat16)
+
+
+def piece_positions(piece_ref, count):
+    tail = piece_ref[count:, :].astype(jnp.float32)
+    return tail[:, :count] + tail[:, count : 2 * count] + tail[:, 2 * count : 3 * count]
+
+
+def attend(qexp, keys, vals, scale, bias3):
+    rows = qexp.shape[0]
+    count = keys.shape[0]
+    atoms, per, _ = bias3.shape
+    s = mm(qexp, keys, ((1,), (1,))).reshape(atoms, per, count) * scale + bias3
+    top = jnp.max(s, axis=-1, keepdims=True)
+    p = jnp.exp(s - top)
+    total = jnp.sum(p, axis=-1, keepdims=True)
+    o = mm(p.astype(jnp.bfloat16).reshape(rows, count), vals, ((1,), (0,)))
+    return top, total, o.reshape(atoms, per, vals.shape[1])
+
+
+def absorb(head_dim, places, pieces, wqkv_ref, qexp_ref, str_ref, own_ref, kv_ref):
+    dim = wqkv_ref.shape[0]
+    atoms = own_ref.shape[1]
+    groups, rows, width = qexp_ref.shape
+    per = rows // atoms
+    count = pieces[0].shape[0] - 8
+    rows_in = jnp.concatenate([piece[:count, :] for piece in pieces], axis=0)
+    kv = mm(rows_in, wqkv_ref[:, dim:], ((1,), (0,))).astype(jnp.bfloat16)
+    for k, place in enumerate(places):
+        kv_ref[place * count : (place + 1) * count, :] = kv[k * count : (k + 1) * count]
+    pos8 = jnp.concatenate([piece_positions(piece, count) for piece in pieces], axis=1)
+    cos_k, sin_k = jnp.cos(two_pi * pos8), jnp.sin(two_pi * pos8)
+    waves = None
+    for c in range(3):
+        term = own_ref[1, :, c : c + 1] * cos_k[c : c + 1] + own_ref[2, :, c : c + 1] * sin_k[c : c + 1]
+        waves = term if waves is None else waves + term
+    out = []
+    for g in range(groups):
+        low, high = g * width, (g + 1) * width
+        bias3 = str_ref[g * per : (g + 1) * per, :1][None] * waves[:, None, :]
+        out.append(
+            attend(
+                qexp_ref[g],
+                kv[:, low:high],
+                kv[:, dim + low : dim + high],
+                head_dim ** (-0.5),
+                bias3,
+            )
+        )
+    return out
+
+
+def widen(column, lanes):
+    return jnp.broadcast_to(column, column.shape[:-1] + (lanes,))
+
+
+def repeat_lanes(array, lanes):
+    return jnp.concatenate([array] * (lanes // array.shape[-1]), axis=-1)
+
+
+def first_kernel(head_dim, places, *refs):
+    pieces = refs[: len(places)]
+    wqkv_ref, qexp_ref, str_ref, own_ref = refs[len(places) : -4]
+    kv_ref, acc_ref, top_ref, sum_ref = refs[-4:]
+    got = absorb(head_dim, places, pieces, wqkv_ref, qexp_ref, str_ref, own_ref, kv_ref)
+    for g, (top, total, o) in enumerate(got):
+        acc_ref[g] = o
+        top_ref[g] = widen(top, 128)
+        sum_ref[g] = widen(total, 128)
+
+
+def merge(got, g, acc_ref, top_ref, sum_ref):
+    top, total, o = got[g]
+    width = o.shape[-1]
+    best = jnp.maximum(widen(top, 128), top_ref[g])
+    a, b = jnp.exp(top_ref[g] - best), jnp.exp(widen(top, 128) - best)
+    summed = a * sum_ref[g] + b * widen(total, 128)
+    acc = repeat_lanes(a, width) * acc_ref[g] + repeat_lanes(b, width) * o
+    return best, summed, acc
+
+
+def next_kernel(head_dim, places, *refs):
+    pieces = refs[: len(places)]
+    wqkv_ref, qexp_ref, str_ref, own_ref = refs[len(places) : len(places) + 4]
+    _, acc_in, top_in, sum_in, kv_ref, acc_ref, top_ref, sum_ref = refs[len(places) + 4 :]
+    got = absorb(head_dim, places, pieces, wqkv_ref, qexp_ref, str_ref, own_ref, kv_ref)
+    for g in range(len(got)):
+        best, summed, acc = merge(got, g, acc_in, top_in, sum_in)
+        acc_ref[g] = acc
+        top_ref[g] = best
+        sum_ref[g] = summed
+
+
+def chosen(scalars, lane):
+    out = jnp.full(lane.shape, scalars[0])
+    for e in range(1, len(scalars)):
+        out = jnp.where(lane == e, scalars[e], out)
+    return out
+
+
+def last_kernel(head_dim, locate, col_count, list_ref, valid_ref, shift_ref, cell_ref, *refs):
+    piece_refs = refs[:8]
+    (
+        wqkv_ref,
+        qexp_ref,
+        str_ref,
+        own_ref,
+        w1_ref,
+        w2_ref,
+        off_ref,
+        wout_ref,
+        in_ref,
+        _,
+        acc_in,
+        top_in,
+        sum_in,
+        out_ref,
+        kv_ref,
+        near_ref,
+        pos_ref,
+        bias_ref,
+    ) = refs[8:]
+    dim = wqkv_ref.shape[0]
+    atoms = own_ref.shape[1]
+    groups, rows, width = qexp_ref.shape
+    per = rows // atoms
+    count = piece_refs[0].shape[0] - 8
+    got = absorb(head_dim, (7,), piece_refs[7:], wqkv_ref, qexp_ref, str_ref, own_ref, kv_ref)
+    for k in range(8):
+        pos_ref[k] = piece_positions(piece_refs[k], count)
+    me = lax.axis_index("rows") * col_count + lax.axis_index("cols")
+    entries = list_ref.shape[1]
+    listed = entries * atoms
+    lane = lax.broadcasted_iota(jnp.int32, (1, listed), 1) // atoms
+    in_tile = lax.broadcasted_iota(jnp.int32, (1, count), 1) // atoms
+    a_tile = count // atoms
+    tiles = []
+    for e in range(entries):
+        up, across, turn = locate(list_ref[0, e] ^ me)
+        place = across + 4 * turn
+        start = pl.multiple_of((place * a_tile + up) * atoms, atoms)
+        near_ref[e * atoms : (e + 1) * atoms, :] = kv_ref[pl.ds(start, atoms), :]
+        into = e % a_tile
+        moved = pltpu.roll(pos_ref[place], (into - up + a_tile) % a_tile * atoms, 1)
+        if into == 0:
+            tiles.append(moved)
+        else:
+            tiles[-1] = jnp.where(in_tile == into, moved, tiles[-1])
+    near = jnp.concatenate(tiles, axis=1)
+    square = None
+    for c in range(3):
+        at = near[c : c + 1] + chosen([shift_ref[c, 0, e] for e in range(entries)], lane).astype(jnp.float32)
+        gap = (at - own_ref[0, :, c : c + 1]) * cell_ref[c]
+        square = gap * gap if square is None else square + gap * gap
+    dist = jnp.sqrt(square + 0.25)
+    nrbf = w1_ref.shape[1] // 6
+    centers = lax.broadcasted_iota(jnp.int32, (nrbf, 1), 0).astype(jnp.float32) * rbf_step
+    offset = off_ref[:, :1]
+    step = 4
+    for i in range(0, atoms, step):
+        radial = jnp.concatenate(
+            [
+                jnp.exp(-((dist[j : j + 1] - centers) ** 2) * (0.5 / rbf_width**2))
+                for j in range(i, i + step)
+            ],
+            axis=1,
+        )
+        h, m, l = parts_of(radial, 3)
+        stack = jnp.concatenate([h, m, h, l, h, m], axis=0)
+        u = mm(w1_ref[...], stack, ((1,), (0,))) + offset
+        u = u / (1.0 + jnp.exp(-u))
+        h, l = parts_of(u, 2)
+        pair = mm(w2_ref[...], jnp.concatenate([h, l, h], axis=0), ((1,), (0,)))
+        for j in range(step):
+            for g in range(groups):
+                bias_ref[g, i + j] = pair[g * per : (g + 1) * per, j * listed : (j + 1) * listed]
+    lane3 = lax.broadcasted_iota(jnp.int32, (1, 1, listed), 2) // atoms
+    live = chosen([valid_ref[0, e] for e in range(entries)], lane3) > 0
+    block = lax.broadcasted_iota(jnp.int32, (1, per, width), 2) // head_dim
+    keep = block == lax.broadcasted_iota(jnp.int32, (1, per, width), 1)
+    pieces = []
+    for g in range(groups):
+        low, high = g * width, (g + 1) * width
+        _, summed, far = merge(got, g, acc_in, top_in, sum_in)
+        far = far / repeat_lanes(summed, width)
+        far = jnp.sum(jnp.where(keep, far, 0.0), axis=1).astype(jnp.bfloat16)
+        s = mm(qexp_ref[g], near_ref[:, low:high], ((1,), (1,)))
+        s = s.reshape(atoms, per, listed) * head_dim ** (-0.5) + bias_ref[g]
+        s = jnp.where(live, s, -1e30)
+        p = jnp.exp(s - jnp.max(s, axis=-1, keepdims=True))
+        summed = jnp.sum(p, axis=-1, keepdims=True)
+        o = mm(
+            p.astype(jnp.bfloat16).reshape(rows, listed),
+            near_ref[:, dim + low : dim + high],
+            ((1,), (0,)),
+        )
+        o = o.reshape(atoms, per, width) / summed
+        close = jnp.sum(jnp.where(keep, o, 0.0), axis=1).astype(jnp.bfloat16)
+        pieces.append((close.astype(jnp.float32) + far.astype(jnp.float32)).astype(jnp.bfloat16))
+    combined = jnp.concatenate(pieces, axis=1)
+    moved = mm(combined, wout_ref[...], ((1,), (0,)))
+    out_ref[...] = (in_ref[...].astype(jnp.float32) + moved).astype(jnp.bfloat16)
+
+
+def call(kernel, outs, scratch, smem, args, aliases=None, hbm=0):
+    vmem = pl.BlockSpec(memory_space=pltpu.VMEM)
+    first = smem + hbm
+    specs = [pl.BlockSpec(memory_space=pltpu.SMEM)] * smem
+    specs += [pl.BlockSpec(memory_space=pltpu.HBM)] * hbm + [vmem] * (len(args) - first)
+    placed = [pltpu.with_memory_space_constraint(a, pltpu.HBM) for a in args[smem:first]]
+    placed += [pltpu.with_memory_space_constraint(a, pltpu.VMEM) for a in args[first:]]
+    many = isinstance(outs, list)
+    return pl.pallas_call(
+        kernel,
+        out_shape=outs,
+        in_specs=specs,
+        out_specs=[vmem] * len(outs) if many else vmem,
+        scratch_shapes=scratch,
+        input_output_aliases=aliases or {},
+        compiler_params=pltpu.CompilerParams(vmem_limit_bytes=24 << 20),
+    )(*args[:smem], *placed)
+
+
+def on_device_small(
+    features,
+    positions,
+    cell_lengths,
+    block_lists,
+    image_offsets,
+    block_valid,
+    norm_gain,
+    w_qkv,
+    w_out,
+    rbf_weight,
+    rbf_offset,
+    pair_weight,
+    cosine_scale,
+):
+    atoms, dim = features.shape
+    heads = pair_weight.shape[1]
+    hidden = pair_weight.shape[0]
+    nrbf = rbf_weight.shape[0]
+    head_dim = dim // heads
+    row_count = lax.axis_size("rows")
+    col_count = lax.axis_size("cols")
+    total = row_count * col_count
+    axes = ("rows", "cols")
+    col_bits = col_count.bit_length() - 1
+    flip = 1 << col_bits
+    across_bits = (0, col_bits + 1)
+    entries = block_lists.shape[1]
+    width = 256
+    per = width // head_dim
+    groups = heads // per
+    rows = atoms * per
+    f32, bf16 = jnp.float32, jnp.bfloat16
+    vm = pltpu.VMEM
+
+    def swap(array, mask):
+        return lax.ppermute(array, axes, [(i, i ^ mask) for i in range(total)])
+
+    def locate(rel):
+        up = (rel >> 1) & 3
+        across = (rel & 1) + 2 * ((rel >> across_bits[1]) & 1)
+        turn = (rel >> col_bits) & 1
+        turn = turn ^ jnp.minimum(up, 1) ^ jnp.minimum(across, 1)
+        return up, across, turn
+
+    tied = lax.optimization_barrier
+    pack = call(
+        pack_kernel,
+        vm((atoms, dim + 128), bf16),
+        [
+            vm((atoms, dim), bf16),
+            vm((1, dim), f32),
+            vm(positions.shape, f32),
+            vm((128, atoms), f32),
+            pltpu.SemaphoreType.DMA((3,)),
+        ],
+        0,
+        (features, norm_gain[None], positions),
+        hbm=3,
+    )
+    ups = [swap(pack, (d << 1) | flip) for d in (1, 2, 3)]
+    ready = call(
+        functools.partial(query_kernel, head_dim),
+        [
+            vm((groups, rows, width), bf16),
+            vm((hidden, 6 * nrbf), bf16),
+            vm((heads, 3 * hidden), bf16),
+            vm((hidden, 128), f32),
+            vm((heads, 128), f32),
+            vm((3, atoms, 128), f32),
+        ],
+        [
+            vm((dim, dim), bf16),
+            vm((nrbf, hidden), f32),
+            vm((1, hidden), f32),
+            vm((heads, hidden), f32),
+            vm((1, heads), f32),
+            pltpu.SemaphoreType.DMA((5,)),
+        ],
+        0,
+        (w_qkv, rbf_weight, rbf_offset[None], pair_weight.T, cosine_scale[None], pack),
+        hbm=5,
+    )
+    ups, ready = tied((ups, ready))
+    qexp, w1, w2, off, strength, own = ready
+    count = 4 * atoms
+    base = call(repack_kernel, vm((count + 8, dim), bf16), [], 0, (pack, *ups))
+    east = swap(base, 1 | flip)
+    north = swap(base, (1 << across_bits[1]) | flip)
+    diag = swap(base, 1 | (1 << across_bits[1]) | flip)
+    state_shapes = [
+        vm((8 * count, 2 * dim), bf16),
+        vm((groups, atoms, per, width), f32),
+        vm((groups, atoms, per, 128), f32),
+        vm((groups, atoms, per, 128), f32),
+    ]
+    common = (w_qkv, qexp, strength, own)
+
+    def step(places, pieces, state):
+        if state is None:
+            return call(
+                functools.partial(first_kernel, head_dim, places),
+                state_shapes,
+                [],
+                0,
+                (*pieces, *common),
+            )
+        at = len(pieces) + len(common)
+        return call(
+            functools.partial(next_kernel, head_dim, places),
+            state_shapes,
+            [],
+            0,
+            (*pieces, *common, *state),
+            {at + k: k for k in range(4)},
+        )
+
+    state = step((0,), (base,), None)
+    base_late, state = tied((base, state))
+    base2 = swap(base_late, flip)
+    east, north, base2, state = tied((east, north, base2, state))
+    east2, north2 = swap(east, flip), swap(north, flip)
+    state = step((1, 2, 4), (east, north, base2), state)
+    diag, east2, north2, state = tied((diag, east2, north2, state))
+    diag2 = swap(diag, flip)
+    state = step((3, 5, 6), (diag, east2, north2), state)
+    diag2, state = tied((diag2, state))
+    updated, _ = call(
+        functools.partial(last_kernel, head_dim, locate, col_count),
+        [jax.ShapeDtypeStruct((atoms, dim), bf16), state_shapes[0]],
+        [
+            vm((entries * atoms, 2 * dim), bf16),
+            vm((8, 8, count), f32),
+            vm((groups, atoms, per, entries * atoms), f32),
+        ],
+        4,
+        (
+            block_lists,
+            block_valid,
+            image_offsets,
+            cell_lengths,
+            base,
+            east,
+            north,
+            diag,
+            base2,
+            east2,
+            north2,
+            diag2,
+            *common,
+            w1,
+            w2,
+            off,
+            w_out,
+            features,
+            *state,
+        ),
+        {4 + 8 + len(common) + 5: 1},
+    )
+    return updated
+
+
 def solution(mesh):
+    row_count, col_count = mesh.shape["rows"], mesh.shape["cols"]
+    small = (row_count, col_count) == (4, 8)
+    body = on_device_small if small else on_device
     return jax.shard_map(
-        on_device,
+        body,
         mesh=mesh,
         in_specs=(
             P(("rows", "cols"), None),

time: 151 us -> 28.3 us (0.19)
  blocking collectives: 101 us -> 0 us
  matrix products: 13.6 us -> 0 us
  local copies, waits for them, and re-layouts: 12.9 us -> 0.04 us
  Pallas kernels: 0 us -> 10.7 us
  other arithmetic: 5.87 us -> 0 us
  waiting for transfers between devices: 2.15 us -> 7.69 us
  starting transfers between devices: 14 us -> 9.51 us
    all_gather x2 -> x0, blocking collectives: 101 us -> none  [the longest x1 69.9 us: on_device(): every_pos = lax.all_gather(positions, ('rows', 'cols'), axis=1, tiled=True)]
    dot_general x10 -> x0, matrix products: 13.6 us -> none  [the longest x1 2.4 us: update(): jnp.einsum('hqk,hkd->hdq', prob_bf, kv_block[1], preferred_element_type=j...]
    pallas_call x0 -> x7, Pallas kernels: none -> 10.7 us  [call(): pl.pallas_call(kernel, out_shape=outs, in_specs=specs, out_specs=[vmem] *...]
    all_to_all x2 -> x0, starting transfers between devices: 6.78 us -> none  [the longest x1 3.52 us: on_device(): lax.all_to_all(grouped, 'rows', split_axis=1, concat_axis=2, tiled=True)]
    ppermute x4 -> x10, waiting for transfers between devices: 2.15 us -> 7.69 us  [swap(): return lax.ppermute(array, axes, [(i, i ^ mask) for i in range(total)])]
    squeeze x2 -> x0, local copies, waits for them, and re-layouts: 3.13 us -> none  [the longest x1 1.56 us: update(): kv_block[1]]
    reshape x12 -> x0, local copies, waits for them, and re-layouts: 3.09 us -> none  [the longest x2 1.14 us: on_device(): grouped = packed.reshape(atom_count, 3, head_count, head_dim).transpose(1...]
    ppermute x4 -> x10, starting transfers between devices: 7.24 us -> 9.51 us  [swap(): return lax.ppermute(array, axes, [(i, i ^ mask) for i in range(total)])]
  transfers between devices with their start and end apart: 6 -> 10, of which waited for: 1 -> 3; matrix products, arithmetic and copies ran while one was open for 16% -> 0% of each run, Pallas kernels for 0% -> 18%
where the time goes in v2:
time: 28.3 us; the launch traced here: 28.2 us
  Pallas kernels  10.7 us (38%)
  starting transfers between devices  9.51 us (34%)
  waiting for transfers between devices  7.69 us (27%)
    pallas_call x7, Pallas kernels, call(): pl.pallas_call(kernel, out_shape=outs, in_specs=specs, out_specs=[vmem] *...  10.7 us
    ppermute x10, starting transfers between devices, swap(): return lax.ppermute(array, axes, [(i, i ^ mask) for i in range(total)])  9.51 us
    ppermute x10, waiting for transfers between devices, swap(): return lax.ppermute(array, axes, [(i, i ^ mask) for i in range(total)])  7.69 us
  transfers between devices with their start and end apart: 10, of which 3 were waited for; matrix products, arithmetic and copies ran while one was open for 0% of the time, Pallas kernels for 18%

profile of v2, /device:TPU:0, one launch (start us, length us, event | category | flops | bytes accessed | tf_op | source)
XLA Modules:
  0.0 28.2 jit_solution(1603536066274291886)
XLA Ops:
  0.0 0.0 copy-start
  0.0 1.1 %shard_map.127.pack_ref.refs_0_ = bf16[32,640]{1,0:T(8,128)(2,1)S(1)} custom-call(bf16[32,512]{1,0:T(8,128)(2,1)} %refs_16_.1, f32[1,512]{1,0:T(1,128)} %bitcast.5, f32[3,32]{1,0:T(4,128)} %pos_hbm.1), custom_call_target="tpu_custom_call" | custom-call | tf_op jit(solution)/shard_map/pallas_call | solution.py:556
  1.1 4.6 %collective-permute-start.2 = (bf16[32,640]{1,0:T(8,128)(2,1)S(1)}, bf16[32,640]{1,0:T(8,128)(2,1)S(1)}, u32[]{:S(2)}, u32[]{:S(2)}) collective-permute-start(bf16[32,640]{1,0:T(8,128)(2,1)S(1)} %shard_map.127.pack_ref.refs_0_), channel_id=1, source_target_pairs={{0,14},{1,15},{2,12},{3,13},{4,10},{5,11},{6,8},{7,9},{8,6},{9,7},... | collective-permute-start | bytes 122888 | tf_op jit(solution)/shard_map/ppermute | solution.py:603
  5.7 0.0 collective-permute-start.1
  5.7 0.9 %collective-permute-start = (bf16[32,640]{1,0:T(8,128)(2,1)S(1)}, bf16[32,640]{1,0:T(8,128)(2,1)S(1)}, u32[]{:S(2)}, u32[]{:S(2)}) collective-permute-start(bf16[32,640]{1,0:T(8,128)(2,1)S(1)} %shard_map.127.pack_ref.refs_0_), channel_id=1, source_target_pairs={{0,10},{1,11},{2,8},{3,9},{4,14},{5,15},{6,12},{7,13},{8,2},{9,3},... | collective-permute-start | bytes 122888 | tf_op jit(solution)/shard_map/ppermute | solution.py:603
  6.6 1.4 %shard_map.128 = (bf16[2,256,256]{2,1,0:T(8,128)(2,1)S(1)}, bf16[64,96]{1,0:T(8,128)(2,1)S(1)}, bf16[16,192]{1,0:T(8,128)(2,1)S(1)}, f32[64,128]{1,0:T(8,128)S(1...) custom-call(bf16[512,1536]{1,0:T(8,128)(2,1)} %refs_8_.1, f32[16,64]{1,0:T(8,128)} %rw_hbm.1, f32[1,64]{1,0:T(1,128)} %bitcast.6, ...), custom_call_target="tpu_custom_call" | custom-call | tf_op jit(solution)/shard_map/pallas_call | solution.py:556
  8.0 0.0 collective-permute-done.2.refs_3_
  8.0 2.4 %collective-permute-done.1.refs_2_ = bf16[32,640]{1,0:T(8,128)(2,1)S(1)} collective-permute-done((bf16[32,640]{1,0:T(8,128)(2,1)S(1)}, bf16[32,640]{1,0:T(8,128)(2,1)S(1)}, u32[]{:S(2)}, u32[]{:S(2)}) %collective-permute-start.1) | collective-permute-done | bytes 40992 | tf_op jit(solution)/shard_map/ppermute | solution.py:603
  10.4 0.0 collective-permute-done.refs_1_
  10.4 0.2 shard_map.129.refs_0_
  10.5 1.4 %collective-permute-start.4 = (bf16[136,512]{1,0:T(8,128)(2,1)S(1)}, bf16[136,512]{1,0:T(8,128)(2,1)S(1)}, u32[]{:S(2)}, u32[]{:S(2)}) collective-permute-start(bf16[136,512]{1,0:T(8,128)(2,1)S(1)} %shard_map.129.refs_0_), channel_id=1, source_target_pairs={{0,24},{1,25},{2,26},{3,27},{4,28},{5,29},{6,30},{7,31},{8,16},{9,... | collective-permute-start | bytes 417800 | tf_op jit(solution)/shard_map/ppermute | solution.py:603
  12.0 1.3 %collective-permute-start.3 = (bf16[136,512]{1,0:T(8,128)(2,1)S(1)}, bf16[136,512]{1,0:T(8,128)(2,1)S(1)}, u32[]{:S(2)}, u32[]{:S(2)}) collective-permute-start(bf16[136,512]{1,0:T(8,128)(2,1)S(1)} %shard_map.129.refs_0_), channel_id=1, source_target_pairs={{0,9},{1,8},{2,11},{3,10},{4,13},{5,12},{6,15},{7,14},{8,1},{9,0},... | collective-permute-start | bytes 417800 | tf_op jit(solution)/shard_map/ppermute | solution.py:603
  13.3 0.0 copy-done
  13.3 0.8 %shard_map.130 = (bf16[1024,1024]{1,0:T(8,128)(2,1)S(1)}, f32[2,32,8,256]{3,2,1,0:T(8,128)S(1)}, f32[2,32,8,128]{3,2,1,0:T(8,128)S(1)}, f32[2,32,8,128]{3,2,1,0:T(8,128)S(1)}) custom-call(bf16[136,512]{1,0:T(8,128)(2,1)S(1)} %shard_map.129.refs_0_, bf16[512,1536]{1,0:T(8,128)(2,1)S(1)} %copy-done, ...), custom_call_target="tpu_custom_call" | custom-call | tf_op jit(solution)/shard_map/pallas_call | solution.py:556
  14.1 0.4 %collective-permute-start.5 = (bf16[136,512]{1,0:T(8,128)(2,1)S(1)}, bf16[136,512]{1,0:T(8,128)(2,1)S(1)}, u32[]{:S(2)}, u32[]{:S(2)}) collective-permute-start(bf16[136,512]{1,0:T(8,128)(2,1)S(1)} %shard_map.129.refs_0_), channel_id=1, source_target_pairs={{0,8},{1,9},{2,10},{3,11},{4,12},{5,13},{6,14},{7,15},{8,0},{9,1},... | collective-permute-start | bytes 417800 | tf_op jit(solution)/shard_map/ppermute | solution.py:603
  14.4 0.3 %collective-permute-start.6 = (bf16[136,512]{1,0:T(8,128)(2,1)S(1)}, bf16[136,512]{1,0:T(8,128)(2,1)S(1)}, u32[]{:S(2)}, u32[]{:S(2)}) collective-permute-start(bf16[136,512]{1,0:T(8,128)(2,1)S(1)} %shard_map.129.refs_0_), channel_id=1, source_target_pairs={{0,25},{1,24},{2,27},{3,26},{4,29},{5,28},{6,31},{7,30},{8,17},{9,... | collective-permute-start | bytes 417800 | tf_op jit(solution)/shard_map/ppermute | solution.py:603
  14.7 1.3 %collective-permute-done.4.refs_1_.refs_2_ = bf16[136,512]{1,0:T(8,128)(2,1)S(1)} collective-permute-done((bf16[136,512]{1,0:T(8,128)(2,1)S(1)}, bf16[136,512]{1,0:T(8,128)(2,1)S(1)}, u32[]{:S(2)}, u32[]{:S(2)}) %collective-permute-start.4) | collective-permute-done | bytes 139296 | tf_op jit(solution)/shard_map/ppermute | solution.py:603
  16.1 3.9 %collective-permute-done.3.refs_0_.refs_1_ = bf16[136,512]{1,0:T(8,128)(2,1)S(1)} collective-permute-done((bf16[136,512]{1,0:T(8,128)(2,1)S(1)}, bf16[136,512]{1,0:T(8,128)(2,1)S(1)}, u32[]{:S(2)}, u32[]{:S(2)}) %collective-permute-start.3) | collective-permute-done | bytes 139296 | tf_op jit(solution)/shard_map/ppermute | solution.py:603
  20.0 0.0 collective-permute-done.5.refs_2_.refs_4_
  20.0 0.0 collective-permute-start.7
  20.0 0.5 %collective-permute-start.8 = (bf16[136,512]{1,0:T(8,128)(2,1)S(1)}, bf16[136,512]{1,0:T(8,128)(2,1)S(1)}, u32[]{:S(2)}, u32[]{:S(2)}) collective-permute-start(bf16[136,512]{1,0:T(8,128)(2,1)S(1)} %collective-permute-done.4.refs_1_.refs_2_), channel_id=1, source_target_pairs={{0,8},{1,9},{2,10},{3,11},{4,12},{5,13},{6,14},{7,15},{8,0},{9,1},... | collective-permute-start | bytes 417800 | tf_op jit(solution)/shard_map/ppermute | solution.py:603
  20.5 1.4 %shard_map.131 = (bf16[1024,1024]{1,0:T(8,128)(2,1)S(1)}, f32[2,32,8,256]{3,2,1,0:T(8,128)S(1)}, f32[2,32,8,128]{3,2,1,0:T(8,128)S(1)}, f32[2,32,8,128]{3,2,1,0:T(8,128)S(1)}) custom-call(bf16[136,512]{1,0:T(8,128)(2,1)S(1)} %collective-permute-done.3.refs_0_.refs_1_, ...), custom_call_target="tpu_custom_call", output_to_operand_aliasing={{0}: (7, {}), {1}: (8, {}), {2}: (9, {}), {3}: (10, {})} | custom-call | tf_op jit(solution)/shard_map/pallas_call | solution.py:556
  21.9 0.0 collective-permute-done.6.refs_0_.refs_3_
  21.9 0.0 collective-permute-done.7.refs_1_.refs_5_
  21.9 0.0 collective-permute-done.8.refs_2_.refs_6_
  21.9 0.0 copy-start.1
  22.0 0.0 copy-start.2
  22.0 0.0 copy-start.3
  22.0 0.0 copy-start.4
  22.0 0.0 copy-start.5
  22.0 0.0 copy-start.6
  22.0 0.1 collective-permute-start.9
  22.1 1.4 %shard_map.132 = (bf16[1024,1024]{1,0:T(8,128)(2,1)S(1)}, f32[2,32,8,256]{3,2,1,0:T(8,128)S(1)}, f32[2,32,8,128]{3,2,1,0:T(8,128)S(1)}, f32[2,32,8,128]{3,2,1,0:T(8,128)S(1)}) custom-call(bf16[136,512]{1,0:T(8,128)(2,1)S(1)} %collective-permute-done.6.refs_0_.refs_3_, ...), custom_call_target="tpu_custom_call", output_to_operand_aliasing={{0}: (7, {}), {1}: (8, {}), {2}: (9, {}), {3}: (10, {})} | custom-call | tf_op jit(solution)/shard_map/pallas_call | solution.py:556
  23.5 0.0 collective-permute-done.9.refs_7_
  23.5 0.0 copy-done.1
  23.5 0.0 copy-done.2
  23.5 0.0 copy-done.3
  23.6 0.0 copy-done.4
  23.6 0.0 copy-done.5
  23.6 0.0 copy-done.6
  23.6 4.6 %shard_map.133 = (bf16[32,512]{1,0:T(8,128)(2,1)}, bf16[1024,1024]{1,0:T(8,128)(2,1)S(1)}) custom-call(s32[1,8]{1,0:T(1,128)S(1)} %copy-done.4, s32[1,8]{1,0:T(1,128)S(1)} %copy-done.5, s32[3,1,8]{2,1,0:T(1,128)S(1)} %copy-done.3, f32[3]{0:T(128)S(1)} %copy-done.6, bf16[136,512]{1,0:T(8,128)(2,1)S(1)} %shard_map.129.refs_0_, ...), custom_call_target="tpu_custom_call", output_to_operand_aliasing={{1}: (21, {})} | custom-call | tf_op jit(solution)/shard_map/pallas_call | solution.py:556
Async XLA Ops:
  0.0 13.3 %copy-start = (bf16[512,1536]{1,0:T(8,128)(2,1)S(1)}, bf16[512,1536]{1,0:T(8,128)(2,1)}, u32[]{:S(2)}) copy-start(bf16[512,1536]{1,0:T(8,128)(2,1)} %refs_8_.1) | copy-start | bytes 4718596
  1.1 6.9 %collective-permute-start.2 = (bf16[32,640]{1,0:T(8,128)(2,1)S(1)}, bf16[32,640]{1,0:T(8,128)(2,1)S(1)}, u32[]{:S(2)}, u32[]{:S(2)}) collective-permute-start(bf16[32,640]{1,0:T(8,128)(2,1)S(1)} %shard_map.127.pack_ref.refs_0_), channel_id=1, source_target_pairs={{0,14},{1,15},{2,12},{3,13},{4,10},{5,11},{6,8},{7,9},{8,6},{9,7},... | collective-permute-start | bytes 122888 | tf_op jit(solution)/shard_map/ppermute | solution.py:603
  5.7 4.7 %collective-permute-start.1 = (bf16[32,640]{1,0:T(8,128)(2,1)S(1)}, bf16[32,640]{1,0:T(8,128)(2,1)S(1)}, u32[]{:S(2)}, u32[]{:S(2)}) collective-permute-start(bf16[32,640]{1,0:T(8,128)(2,1)S(1)} %shard_map.127.pack_ref.refs_0_), channel_id=1, source_target_pairs={{0,12},{1,13},{2,14},{3,15},{4,8},{5,9},{6,10},{7,11},{8,4},{9,5},... | collective-permute-start | bytes 122888 | tf_op jit(solution)/shard_map/ppermute | solution.py:603
  5.7 4.7 %collective-permute-start = (bf16[32,640]{1,0:T(8,128)(2,1)S(1)}, bf16[32,640]{1,0:T(8,128)(2,1)S(1)}, u32[]{:S(2)}, u32[]{:S(2)}) collective-permute-start(bf16[32,640]{1,0:T(8,128)(2,1)S(1)} %shard_map.127.pack_ref.refs_0_), channel_id=1, source_target_pairs={{0,10},{1,11},{2,8},{3,9},{4,14},{5,15},{6,12},{7,13},{8,2},{9,3},... | collective-permute-start | bytes 122888 | tf_op jit(solution)/shard_map/ppermute | solution.py:603
  10.5 5.5 %collective-permute-start.4 = (bf16[136,512]{1,0:T(8,128)(2,1)S(1)}, bf16[136,512]{1,0:T(8,128)(2,1)S(1)}, u32[]{:S(2)}, u32[]{:S(2)}) collective-permute-start(bf16[136,512]{1,0:T(8,128)(2,1)S(1)} %shard_map.129.refs_0_), channel_id=1, source_target_pairs={{0,24},{1,25},{2,26},{3,27},{4,28},{5,29},{6,30},{7,31},{8,16},{9,... | collective-permute-start | bytes 417800 | tf_op jit(solution)/shard_map/ppermute | solution.py:603
  12.0 8.0 %collective-permute-start.3 = (bf16[136,512]{1,0:T(8,128)(2,1)S(1)}, bf16[136,512]{1,0:T(8,128)(2,1)S(1)}, u32[]{:S(2)}, u32[]{:S(2)}) collective-permute-start(bf16[136,512]{1,0:T(8,128)(2,1)S(1)} %shard_map.129.refs_0_), channel_id=1, source_target_pairs={{0,9},{1,8},{2,11},{3,10},{4,13},{5,12},{6,15},{7,14},{8,1},{9,0},... | collective-permute-start | bytes 417800 | tf_op jit(solution)/shard_map/ppermute | solution.py:603
  14.1 5.9 %collective-permute-start.5 = (bf16[136,512]{1,0:T(8,128)(2,1)S(1)}, bf16[136,512]{1,0:T(8,128)(2,1)S(1)}, u32[]{:S(2)}, u32[]{:S(2)}) collective-permute-start(bf16[136,512]{1,0:T(8,128)(2,1)S(1)} %shard_map.129.refs_0_), channel_id=1, source_target_pairs={{0,8},{1,9},{2,10},{3,11},{4,12},{5,13},{6,14},{7,15},{8,0},{9,1},... | collective-permute-start | bytes 417800 | tf_op jit(solution)/shard_map/ppermute | solution.py:603
  14.4 7.5 %collective-permute-start.6 = (bf16[136,512]{1,0:T(8,128)(2,1)S(1)}, bf16[136,512]{1,0:T(8,128)(2,1)S(1)}, u32[]{:S(2)}, u32[]{:S(2)}) collective-permute-start(bf16[136,512]{1,0:T(8,128)(2,1)S(1)} %shard_map.129.refs_0_), channel_id=1, source_target_pairs={{0,25},{1,24},{2,27},{3,26},{4,29},{5,28},{6,31},{7,30},{8,17},{9,... | collective-permute-start | bytes 417800 | tf_op jit(solution)/shard_map/ppermute | solution.py:603
  20.0 1.9 %collective-permute-start.7 = (bf16[136,512]{1,0:T(8,128)(2,1)S(1)}, bf16[136,512]{1,0:T(8,128)(2,1)S(1)}, u32[]{:S(2)}, u32[]{:S(2)}) collective-permute-start(bf16[136,512]{1,0:T(8,128)(2,1)S(1)} %collective-permute-done.3.refs_0_.refs_1_), channel_id=1, source_target_pairs={{0,8},{1,9},{2,10},{3,11},{4,12},{5,13},{6,14},{7,15},{8,0},{9,1},... | collective-permute-start | bytes 417800 | tf_op jit(solution)/shard_map/ppermute | solution.py:603
  20.0 1.9 %collective-permute-start.8 = (bf16[136,512]{1,0:T(8,128)(2,1)S(1)}, bf16[136,512]{1,0:T(8,128)(2,1)S(1)}, u32[]{:S(2)}, u32[]{:S(2)}) collective-permute-start(bf16[136,512]{1,0:T(8,128)(2,1)S(1)} %collective-permute-done.4.refs_1_.refs_2_), channel_id=1, source_target_pairs={{0,8},{1,9},{2,10},{3,11},{4,12},{5,13},{6,14},{7,15},{8,0},{9,1},... | collective-permute-start | bytes 417800 | tf_op jit(solution)/shard_map/ppermute | solution.py:603
  21.9 1.6 %copy-start.1 = (bf16[512,512]{1,0:T(8,128)(2,1)S(1)}, bf16[512,512]{1,0:T(8,128)(2,1)}, u32[]{:S(2)}) copy-start(bf16[512,512]{1,0:T(8,128)(2,1)} %refs_15_.1) | copy-start | bytes 1572868
  22.0 1.6 %copy-start.2 = (bf16[32,512]{1,0:T(8,128)(2,1)S(1)}, bf16[32,512]{1,0:T(8,128)(2,1)}, u32[]{:S(2)}) copy-start(bf16[32,512]{1,0:T(8,128)(2,1)} %refs_16_.1) | copy-start | bytes 98308
  22.0 1.6 %copy-start.3 = (s32[3,1,8]{2,1,0:T(1,128)S(1)}, s32[3,1,8]{2,1,0:T(1,128)}, u32[]{:S(2)}) copy-start(s32[3,1,8]{2,1,0:T(1,128)} %shift_ref.1) | copy-start | bytes 292
  22.0 1.6 %copy-start.4 = (s32[1,8]{1,0:T(1,128)S(1)}, s32[1,8]{1,0:T(1,128)}, u32[]{:S(2)}) copy-start(s32[1,8]{1,0:T(1,128)} %list_ref.1) | copy-start | bytes 100
  22.0 1.6 %copy-start.5 = (s32[1,8]{1,0:T(1,128)S(1)}, s32[1,8]{1,0:T(1,128)}, u32[]{:S(2)}) copy-start(s32[1,8]{1,0:T(1,128)} %valid_ref.1) | copy-start | bytes 100
  22.0 1.6 %copy-start.6 = (f32[3]{0:T(128)S(1)}, f32[3]{0:T(128)}, u32[]{:S(2)}) copy-start(f32[3]{0:T(128)} %cell_ref.1) | copy-start | bytes 40
  22.0 1.5 %collective-permute-start.9 = (bf16[136,512]{1,0:T(8,128)(2,1)S(1)}, bf16[136,512]{1,0:T(8,128)(2,1)S(1)}, u32[]{:S(2)}, u32[]{:S(2)}) collective-permute-start(bf16[136,512]{1,0:T(8,128)(2,1)S(1)} %collective-permute-done.6.refs_0_.refs_3_), channel_id=1, source_target_pairs={{0,8},{1,9},{2,10},{3,11},{4,12},{5,13},{6,14},{7,15},{8,0},{9,1},... | collective-permute-start | bytes 417800 | tf_op jit(solution)/shard_map/ppermute | solution.py:603

commit v3 on v2

--- a/solution.py
+++ b/solution.py
@@ -277,7 +277,6 @@
     qexp_ref,
     w1_ref,
     w2_ref,
-    off_ref,
     str_ref,
     own_ref,
     wq_ref,
@@ -311,13 +310,16 @@
         spread = jnp.broadcast_to(part[:, None, :], (atoms, per, width))
         spread = jnp.where(keep, spread, 0.0).reshape(rows, width)
         qexp_ref[g] = spread.astype(jnp.bfloat16)
-    h, m, l = parts_of(rw_ref[...], 3)
-    stack = jnp.concatenate([h, h, m, h, l, m], axis=0)
+    h, m, l = parts_of(0.5 * rw_ref[...], 3)
     hidden = rw_ref.shape[1]
+    row = lax.broadcasted_iota(jnp.int32, (16, hidden), 0)
+    tail = jnp.zeros((16, hidden), jnp.float32)
+    for k, part in enumerate(parts_of(0.5 * ro_ref[...], 3)):
+        tail = jnp.where(row == k, part.astype(jnp.float32), tail)
+    stack = jnp.concatenate([h, h, m, h, l, m, tail.astype(jnp.bfloat16)], axis=0)
     w1_ref[...] = mm(unit(hidden, hidden, jnp.bfloat16), stack, ((1,), (1,))).astype(jnp.bfloat16)
     h, l = parts_of(pw_ref[...], 2)
     w2_ref[...] = jnp.concatenate([h, h, l], axis=1)
-    off_ref[...] = jnp.broadcast_to(to_column(ro_ref[...]), off_ref.shape)
     str_ref[...] = jnp.broadcast_to(to_column(cs_ref[...]), str_ref.shape)
     pos = pack_ref[:, dim:].astype(jnp.float32)
     pos = pos + pltpu.roll(pos, 120, 1) + pltpu.roll(pos, 112, 1)
@@ -450,7 +452,6 @@
         own_ref,
         w1_ref,
         w2_ref,
-        off_ref,
         wout_ref,
         in_ref,
         _,
@@ -496,22 +497,17 @@
         gap = (at - own_ref[0, :, c : c + 1]) * cell_ref[c]
         square = gap * gap if square is None else square + gap * gap
     dist = jnp.sqrt(square + 0.25)
-    nrbf = w1_ref.shape[1] // 6
+    nrbf = (w1_ref.shape[1] - 16) // 6
     centers = lax.broadcasted_iota(jnp.int32, (nrbf, 1), 0).astype(jnp.float32) * rbf_step
-    offset = off_ref[:, :1]
-    step = 4
+    step = 16
+    ones = jnp.ones((16, step * listed), jnp.bfloat16)
     for i in range(0, atoms, step):
-        radial = jnp.concatenate(
-            [
-                jnp.exp(-((dist[j : j + 1] - centers) ** 2) * (0.5 / rbf_width**2))
-                for j in range(i, i + step)
-            ],
-            axis=1,
-        )
+        gap = jnp.concatenate([dist[j : j + 1] - centers for j in range(i, i + step)], axis=1)
+        radial = jnp.exp(gap * gap * (-0.5 / rbf_width**2))
         h, m, l = parts_of(radial, 3)
-        stack = jnp.concatenate([h, m, h, l, h, m], axis=0)
-        u = mm(w1_ref[...], stack, ((1,), (0,))) + offset
-        u = u / (1.0 + jnp.exp(-u))
+        stack = jnp.concatenate([h, m, h, l, h, m, ones], axis=0)
+        u = mm(w1_ref[...], stack, ((1,), (0,)))
+        u = u + u * jnp.tanh(u)
         h, l = parts_of(u, 2)
         pair = mm(w2_ref[...], jnp.concatenate([h, l, h], axis=0), ((1,), (0,)))
         for j in range(step):
@@ -629,9 +625,8 @@
         functools.partial(query_kernel, head_dim),
         [
             vm((groups, rows, width), bf16),
-            vm((hidden, 6 * nrbf), bf16),
+            vm((hidden, 6 * nrbf + 16), bf16),
             vm((heads, 3 * hidden), bf16),
-            vm((hidden, 128), f32),
             vm((heads, 128), f32),
             vm((3, atoms, 128), f32),
         ],
@@ -648,7 +643,7 @@
         hbm=5,
     )
     ups, ready = tied((ups, ready))
-    qexp, w1, w2, off, strength, own = ready
+    qexp, w1, w2, strength, own = ready
     count = 4 * atoms
     base = call(repack_kernel, vm((count + 8, dim), bf16), [], 0, (pack, *ups))
     east = swap(base, 1 | flip)
@@ -684,10 +679,12 @@
     state = step((0,), (base,), None)
     base_late, state = tied((base, state))
     base2 = swap(base_late, flip)
-    east, north, base2, state = tied((east, north, base2, state))
+    base2, state = tied((base2, state))
+    state = step((4,), (base2,), state)
+    east, north, state = tied((east, north, state))
     east2, north2 = swap(east, flip), swap(north, flip)
-    state = step((1, 2, 4), (east, north, base2), state)
-    diag, east2, north2, state = tied((diag, east2, north2, state))
+    state = step((1, 2), (east, north), state)
+    diag, state = tied((diag, state))
     diag2 = swap(diag, flip)
     state = step((3, 5, 6), (diag, east2, north2), state)
     diag2, state = tied((diag2, state))
@@ -716,12 +713,11 @@
             *common,
             w1,
             w2,
-            off,
             w_out,
             features,
             *state,
         ),
-        {4 + 8 + len(common) + 5: 1},
+        {4 + 8 + len(common) + 4: 1},
     )
     return updated
 

time: 28.3 us -> 28.9 us (1.021)
  waiting for transfers between devices: 7.69 us -> 8.42 us
    ppermute x10, waiting for transfers between devices: 7.69 us -> 8.42 us  [swap(): return lax.ppermute(array, axes, [(i, i ^ mask) for i in range(total)])]
    pallas_call x7 -> x8, Pallas kernels: 10.7 us -> 10.5 us  [call(): pl.pallas_call(kernel, out_shape=outs, in_specs=specs, out_specs=[vmem] *...]
  transfers between devices with their start and end apart: 10 -> 10, of which waited for: 3 -> 5; matrix products, arithmetic and copies ran while one was open for 0% -> 0% of each run, Pallas kernels for 18% -> 17%
where the time goes in v3:
time: 28.9 us; the launch traced here: 28.8 us
  Pallas kernels  10.5 us (36%)
  starting transfers between devices  9.7 us (34%)
  waiting for transfers between devices  8.42 us (29%)
    pallas_call x8, Pallas kernels, call(): pl.pallas_call(kernel, out_shape=outs, in_specs=specs, out_specs=[vmem] *...  10.5 us
    ppermute x10, starting transfers between devices, swap(): return lax.ppermute(array, axes, [(i, i ^ mask) for i in range(total)])  9.7 us
    ppermute x10, waiting for transfers between devices, swap(): return lax.ppermute(array, axes, [(i, i ^ mask) for i in range(total)])  8.42 us
  transfers between devices with their start and end apart: 10, of which 5 were waited for; matrix products, arithmetic and copies ran while one was open for 0% of the time, Pallas kernels for 17%

profile of v3, /device:TPU:0, one launch (start us, length us, event | category | flops | bytes accessed | tf_op | source)
XLA Modules:
  0.0 28.8 jit_solution(11427572229982615169)
XLA Ops:
  0.0 0.0 copy-start
  0.0 1.1 %shard_map.127.pack_ref.refs_0_ = bf16[32,640]{1,0:T(8,128)(2,1)S(1)} custom-call(bf16[32,512]{1,0:T(8,128)(2,1)} %refs_15_.1, f32[1,512]{1,0:T(1,128)} %bitcast.5, f32[3,32]{1,0:T(4,128)} %pos_hbm.1), custom_call_target="tpu_custom_call" | custom-call | tf_op jit(solution)/shard_map/pallas_call | solution.py:552
  1.1 2.6 %collective-permute-start = (bf16[32,640]{1,0:T(8,128)(2,1)S(1)}, bf16[32,640]{1,0:T(8,128)(2,1)S(1)}, u32[]{:S(2)}, u32[]{:S(2)}) collective-permute-start(bf16[32,640]{1,0:T(8,128)(2,1)S(1)} %shard_map.127.pack_ref.refs_0_), channel_id=1, source_target_pairs={{0,10},{1,11},{2,8},{3,9},{4,14},{5,15},{6,12},{7,13},{8,2},{9,3},... | collective-permute-start | bytes 122888 | tf_op jit(solution)/shard_map/ppermute | solution.py:599
  3.6 2.9 %collective-permute-start.1 = (bf16[32,640]{1,0:T(8,128)(2,1)S(1)}, bf16[32,640]{1,0:T(8,128)(2,1)S(1)}, u32[]{:S(2)}, u32[]{:S(2)}) collective-permute-start(bf16[32,640]{1,0:T(8,128)(2,1)S(1)} %shard_map.127.pack_ref.refs_0_), channel_id=1, source_target_pairs={{0,12},{1,13},{2,14},{3,15},{4,8},{5,9},{6,10},{7,11},{8,4},{9,5},... | collective-permute-start | bytes 122888 | tf_op jit(solution)/shard_map/ppermute | solution.py:599
  6.5 0.0 collective-permute-start.2
  6.5 1.4 %shard_map.128 = (bf16[2,256,256]{2,1,0:T(8,128)(2,1)S(1)}, bf16[64,112]{1,0:T(8,128)(2,1)S(1)}, bf16[16,192]{1,0:T(8,128)(2,1)S(1)}, f32[16,128]{1,0:T(8,128)S(1)}, f32[3,32,128]{2,1,0:T(8,128)S(1)}) custom-call(bf16[512,1536]{1,0:T(8,128)(2,1)} %refs_8_.1, f32[16,64]{1,0:T(8,128)} %rw_hbm.1, f32[1,64]{1,0:T(1,128)} %bitcast.6, f32[16,64]{1,0:T(8,128)} %bitcast.4, ...), custom_call_target="tpu_custom_call" | custom-call | tf_op jit(solution)/shard_map/pallas_call | solution.py:552
  7.9 0.0 collective-permute-done.refs_1_
  7.9 0.3 %collective-permute-done.1.refs_2_ = bf16[32,640]{1,0:T(8,128)(2,1)S(1)} collective-permute-done((bf16[32,640]{1,0:T(8,128)(2,1)S(1)}, bf16[32,640]{1,0:T(8,128)(2,1)S(1)}, u32[]{:S(2)}, u32[]{:S(2)}) %collective-permute-start.1) | collective-permute-done | bytes 40992 | tf_op jit(solution)/shard_map/ppermute | solution.py:599
  8.2 4.0 %collective-permute-done.2.refs_3_ = bf16[32,640]{1,0:T(8,128)(2,1)S(1)} collective-permute-done((bf16[32,640]{1,0:T(8,128)(2,1)S(1)}, bf16[32,640]{1,0:T(8,128)(2,1)S(1)}, u32[]{:S(2)}, u32[]{:S(2)}) %collective-permute-start.2) | collective-permute-done | bytes 40992 | tf_op jit(solution)/shard_map/ppermute | solution.py:599
  12.2 0.2 shard_map.129.refs_0_
  12.3 0.0 copy-done
  12.3 0.8 %shard_map.130 = (bf16[1024,1024]{1,0:T(8,128)(2,1)S(1)}, f32[2,32,8,256]{3,2,1,0:T(8,128)S(1)}, f32[2,32,8,128]{3,2,1,0:T(8,128)S(1)}, f32[2,32,8,128]{3,2,1,0:T(8,128)S(1)}) custom-call(bf16[136,512]{1,0:T(8,128)(2,1)S(1)} %shard_map.129.refs_0_, bf16[512,1536]{1,0:T(8,128)(2,1)S(1)} %copy-done, ...), custom_call_target="tpu_custom_call" | custom-call | tf_op jit(solution)/shard_map/pallas_call | solution.py:552
  13.1 0.2 collective-permute-start.5
  13.3 1.5 %collective-permute-start.3 = (bf16[136,512]{1,0:T(8,128)(2,1)S(1)}, bf16[136,512]{1,0:T(8,128)(2,1)S(1)}, u32[]{:S(2)}, u32[]{:S(2)}) collective-permute-start(bf16[136,512]{1,0:T(8,128)(2,1)S(1)} %shard_map.129.refs_0_), channel_id=1, source_target_pairs={{0,9},{1,8},{2,11},{3,10},{4,13},{5,12},{6,15},{7,14},{8,1},{9,0},... | collective-permute-start | bytes 417800 | tf_op jit(solution)/shard_map/ppermute | solution.py:599
  14.8 1.2 %collective-permute-start.4 = (bf16[136,512]{1,0:T(8,128)(2,1)S(1)}, bf16[136,512]{1,0:T(8,128)(2,1)S(1)}, u32[]{:S(2)}, u32[]{:S(2)}) collective-permute-start(bf16[136,512]{1,0:T(8,128)(2,1)S(1)} %shard_map.129.refs_0_), channel_id=1, source_target_pairs={{0,24},{1,25},{2,26},{3,27},{4,28},{5,29},{6,30},{7,31},{8,16},{9,... | collective-permute-start | bytes 417800 | tf_op jit(solution)/shard_map/ppermute | solution.py:599
  16.0 0.5 %collective-permute-start.6 = (bf16[136,512]{1,0:T(8,128)(2,1)S(1)}, bf16[136,512]{1,0:T(8,128)(2,1)S(1)}, u32[]{:S(2)}, u32[]{:S(2)}) collective-permute-start(bf16[136,512]{1,0:T(8,128)(2,1)S(1)} %shard_map.129.refs_0_), channel_id=1, source_target_pairs={{0,25},{1,24},{2,27},{3,26},{4,29},{5,28},{6,31},{7,30},{8,17},{9,... | collective-permute-start | bytes 417800 | tf_op jit(solution)/shard_map/ppermute | solution.py:599
  16.5 0.0 collective-permute-done.5.refs_0_.refs_4_
  16.5 0.9 %shard_map.131 = (bf16[1024,1024]{1,0:T(8,128)(2,1)S(1)}, f32[2,32,8,256]{3,2,1,0:T(8,128)S(1)}, f32[2,32,8,128]{3,2,1,0:T(8,128)S(1)}, f32[2,32,8,128]{3,2,1,0:T(8,128)S(1)}) custom-call(bf16[136,512]{1,0:T(8,128)(2,1)S(1)} %collective-permute-done.5.refs_0_.refs_4_, ...), custom_call_target="tpu_custom_call", output_to_operand_aliasing={{0}: (5, {}), {1}: (6, {}), {2}: (7, {}), {3}: (8, {})} | custom-call | tf_op jit(solution)/shard_map/pallas_call | solution.py:552
  17.4 1.2 %collective-permute-done.3.refs_0_.refs_1_ = bf16[136,512]{1,0:T(8,128)(2,1)S(1)} collective-permute-done((bf16[136,512]{1,0:T(8,128)(2,1)S(1)}, bf16[136,512]{1,0:T(8,128)(2,1)S(1)}, u32[]{:S(2)}, u32[]{:S(2)}) %collective-permute-start.3) | collective-permute-done | bytes 139296 | tf_op jit(solution)/shard_map/ppermute | solution.py:599
  18.7 1.8 %collective-permute-done.4.refs_1_.refs_2_ = bf16[136,512]{1,0:T(8,128)(2,1)S(1)} collective-permute-done((bf16[136,512]{1,0:T(8,128)(2,1)S(1)}, bf16[136,512]{1,0:T(8,128)(2,1)S(1)}, u32[]{:S(2)}, u32[]{:S(2)}) %collective-permute-start.4) | collective-permute-done | bytes 139296 | tf_op jit(solution)/shard_map/ppermute | solution.py:599
  20.5 0.7 %collective-permute-start.7 = (bf16[136,512]{1,0:T(8,128)(2,1)S(1)}, bf16[136,512]{1,0:T(8,128)(2,1)S(1)}, u32[]{:S(2)}, u32[]{:S(2)}) collective-permute-start(bf16[136,512]{1,0:T(8,128)(2,1)S(1)} %collective-permute-done.3.refs_0_.refs_1_), channel_id=1, source_target_pairs={{0,8},{1,9},{2,10},{3,11},{4,12},{5,13},{6,14},{7,15},{8,0},{9,1},... | collective-permute-start | bytes 417800 | tf_op jit(solution)/shard_map/ppermute | solution.py:599
  21.2 0.0 collective-permute-start.8
  21.2 1.1 %shard_map.132 = (bf16[1024,1024]{1,0:T(8,128)(2,1)S(1)}, f32[2,32,8,256]{3,2,1,0:T(8,128)S(1)}, f32[2,32,8,128]{3,2,1,0:T(8,128)S(1)}, f32[2,32,8,128]{3,2,1,0:T(8,128)S(1)}) custom-call(bf16[136,512]{1,0:T(8,128)(2,1)S(1)} %collective-permute-done.3.refs_0_.refs_1_, ...), custom_call_target="tpu_custom_call", output_to_operand_aliasing={{0}: (6, {}), {1}: (7, {}), {2}: (8, {}), {3}: (9, {})} | custom-call | tf_op jit(solution)/shard_map/pallas_call | solution.py:552
  22.3 1.1 %collective-permute-done.6.refs_0_.refs_3_ = bf16[136,512]{1,0:T(8,128)(2,1)S(1)} collective-permute-done((bf16[136,512]{1,0:T(8,128)(2,1)S(1)}, bf16[136,512]{1,0:T(8,128)(2,1)S(1)}, u32[]{:S(2)}, u32[]{:S(2)}) %collective-permute-start.6) | collective-permute-done | bytes 139296 | tf_op jit(solution)/shard_map/ppermute | solution.py:599
  23.4 0.0 copy-start.1
  23.4 0.0 copy-start.2
  23.4 0.0 copy-start.3
  23.4 0.0 copy-start.4
  23.4 0.0 copy-start.5
  23.4 0.0 copy-start.6
  23.4 0.2 collective-permute-start.9
  23.6 0.0 collective-permute-done.7.refs_1_.refs_5_
  23.6 0.0 collective-permute-done.8.refs_2_.refs_6_
  23.6 1.4 %shard_map.133 = (bf16[1024,1024]{1,0:T(8,128)(2,1)S(1)}, f32[2,32,8,256]{3,2,1,0:T(8,128)S(1)}, f32[2,32,8,128]{3,2,1,0:T(8,128)S(1)}, f32[2,32,8,128]{3,2,1,0:T(8,128)S(1)}) custom-call(bf16[136,512]{1,0:T(8,128)(2,1)S(1)} %collective-permute-done.6.refs_0_.refs_3_, ...), custom_call_target="tpu_custom_call", output_to_operand_aliasing={{0}: (7, {}), {1}: (8, {}), {2}: (9, {}), {3}: (10, {})} | custom-call | tf_op jit(solution)/shard_map/pallas_call | solution.py:552
  25.1 0.0 collective-permute-done.9.refs_7_
  25.1 0.0 copy-done.1
  25.1 0.0 copy-done.2
  25.1 0.0 copy-done.3
  25.1 0.0 copy-done.4
  25.1 0.0 copy-done.5
  25.1 0.0 copy-done.6
  25.1 3.7 %shard_map.134 = (bf16[32,512]{1,0:T(8,128)(2,1)}, bf16[1024,1024]{1,0:T(8,128)(2,1)S(1)}) custom-call(s32[1,8]{1,0:T(1,128)S(1)} %copy-done.4, s32[1,8]{1,0:T(1,128)S(1)} %copy-done.5, s32[3,1,8]{2,1,0:T(1,128)S(1)} %copy-done.3, f32[3]{0:T(128)S(1)} %copy-done.6, bf16[136,512]{1,0:T(8,128)(2,1)S(1)} %shard_map.129.refs_0_, ...), custom_call_target="tpu_custom_call", output_to_operand_aliasing={{1}: (20, {})} | custom-call | tf_op jit(solution)/shard_map/pallas_call | solution.py:552
Async XLA Ops:
  0.0 12.3 %copy-start = (bf16[512,1536]{1,0:T(8,128)(2,1)S(1)}, bf16[512,1536]{1,0:T(8,128)(2,1)}, u32[]{:S(2)}) copy-start(bf16[512,1536]{1,0:T(8,128)(2,1)} %refs_8_.1) | copy-start | bytes 4718596
  1.1 6.8 %collective-permute-start = (bf16[32,640]{1,0:T(8,128)(2,1)S(1)}, bf16[32,640]{1,0:T(8,128)(2,1)S(1)}, u32[]{:S(2)}, u32[]{:S(2)}) collective-permute-start(bf16[32,640]{1,0:T(8,128)(2,1)S(1)} %shard_map.127.pack_ref.refs_0_), channel_id=1, source_target_pairs={{0,10},{1,11},{2,8},{3,9},{4,14},{5,15},{6,12},{7,13},{8,2},{9,3},... | collective-permute-start | bytes 122888 | tf_op jit(solution)/shard_map/ppermute | solution.py:599
  3.6 4.6 %collective-permute-start.1 = (bf16[32,640]{1,0:T(8,128)(2,1)S(1)}, bf16[32,640]{1,0:T(8,128)(2,1)S(1)}, u32[]{:S(2)}, u32[]{:S(2)}) collective-permute-start(bf16[32,640]{1,0:T(8,128)(2,1)S(1)} %shard_map.127.pack_ref.refs_0_), channel_id=1, source_target_pairs={{0,12},{1,13},{2,14},{3,15},{4,8},{5,9},{6,10},{7,11},{8,4},{9,5},... | collective-permute-start | bytes 122888 | tf_op jit(solution)/shard_map/ppermute | solution.py:599
  6.5 5.6 %collective-permute-start.2 = (bf16[32,640]{1,0:T(8,128)(2,1)S(1)}, bf16[32,640]{1,0:T(8,128)(2,1)S(1)}, u32[]{:S(2)}, u32[]{:S(2)}) collective-permute-start(bf16[32,640]{1,0:T(8,128)(2,1)S(1)} %shard_map.127.pack_ref.refs_0_), channel_id=1, source_target_pairs={{0,14},{1,15},{2,12},{3,13},{4,10},{5,11},{6,8},{7,9},{8,6},{9,7},... | collective-permute-start | bytes 122888 | tf_op jit(solution)/shard_map/ppermute | solution.py:599
  13.1 3.4 %collective-permute-start.5 = (bf16[136,512]{1,0:T(8,128)(2,1)S(1)}, bf16[136,512]{1,0:T(8,128)(2,1)S(1)}, u32[]{:S(2)}, u32[]{:S(2)}) collective-permute-start(bf16[136,512]{1,0:T(8,128)(2,1)S(1)} %shard_map.129.refs_0_), channel_id=1, source_target_pairs={{0,8},{1,9},{2,10},{3,11},{4,12},{5,13},{6,14},{7,15},{8,0},{9,1},... | collective-permute-start | bytes 417800 | tf_op jit(solution)/shard_map/ppermute | solution.py:599
  13.3 5.4 %collective-permute-start.3 = (bf16[136,512]{1,0:T(8,128)(2,1)S(1)}, bf16[136,512]{1,0:T(8,128)(2,1)S(1)}, u32[]{:S(2)}, u32[]{:S(2)}) collective-permute-start(bf16[136,512]{1,0:T(8,128)(2,1)S(1)} %shard_map.129.refs_0_), channel_id=1, source_target_pairs={{0,9},{1,8},{2,11},{3,10},{4,13},{5,12},{6,15},{7,14},{8,1},{9,0},... | collective-permute-start | bytes 417800 | tf_op jit(solution)/shard_map/ppermute | solution.py:599
  14.8 5.7 %collective-permute-start.4 = (bf16[136,512]{1,0:T(8,128)(2,1)S(1)}, bf16[136,512]{1,0:T(8,128)(2,1)S(1)}, u32[]{:S(2)}, u32[]{:S(2)}) collective-permute-start(bf16[136,512]{1,0:T(8,128)(2,1)S(1)} %shard_map.129.refs_0_), channel_id=1, source_target_pairs={{0,24},{1,25},{2,26},{3,27},{4,28},{5,29},{6,30},{7,31},{8,16},{9,... | collective-permute-start | bytes 417800 | tf_op jit(solution)/shard_map/ppermute | solution.py:599
  16.0 7.4 %collective-permute-start.6 = (bf16[136,512]{1,0:T(8,128)(2,1)S(1)}, bf16[136,512]{1,0:T(8,128)(2,1)S(1)}, u32[]{:S(2)}, u32[]{:S(2)}) collective-permute-start(bf16[136,512]{1,0:T(8,128)(2,1)S(1)} %shard_map.129.refs_0_), channel_id=1, source_target_pairs={{0,25},{1,24},{2,27},{3,26},{4,29},{5,28},{6,31},{7,30},{8,17},{9,... | collective-permute-start | bytes 417800 | tf_op jit(solution)/shard_map/ppermute | solution.py:599
  20.5 3.1 %collective-permute-start.7 = (bf16[136,512]{1,0:T(8,128)(2,1)S(1)}, bf16[136,512]{1,0:T(8,128)(2,1)S(1)}, u32[]{:S(2)}, u32[]{:S(2)}) collective-permute-start(bf16[136,512]{1,0:T(8,128)(2,1)S(1)} %collective-permute-done.3.refs_0_.refs_1_), channel_id=1, source_target_pairs={{0,8},{1,9},{2,10},{3,11},{4,12},{5,13},{6,14},{7,15},{8,0},{9,1},... | collective-permute-start | bytes 417800 | tf_op jit(solution)/shard_map/ppermute | solution.py:599
  21.2 2.4 %collective-permute-start.8 = (bf16[136,512]{1,0:T(8,128)(2,1)S(1)}, bf16[136,512]{1,0:T(8,128)(2,1)S(1)}, u32[]{:S(2)}, u32[]{:S(2)}) collective-permute-start(bf16[136,512]{1,0:T(8,128)(2,1)S(1)} %collective-permute-done.4.refs_1_.refs_2_), channel_id=1, source_target_pairs={{0,8},{1,9},{2,10},{3,11},{4,12},{5,13},{6,14},{7,15},{8,0},{9,1},... | collective-permute-start | bytes 417800 | tf_op jit(solution)/shard_map/ppermute | solution.py:599
  23.4 1.7 %copy-start.1 = (bf16[512,512]{1,0:T(8,128)(2,1)S(1)}, bf16[512,512]{1,0:T(8,128)(2,1)}, u32[]{:S(2)}) copy-start(bf16[512,512]{1,0:T(8,128)(2,1)} %refs_14_.1) | copy-start | bytes 1572868
  23.4 1.7 %copy-start.2 = (bf16[32,512]{1,0:T(8,128)(2,1)S(1)}, bf16[32,512]{1,0:T(8,128)(2,1)}, u32[]{:S(2)}) copy-start(bf16[32,512]{1,0:T(8,128)(2,1)} %refs_15_.1) | copy-start | bytes 98308
  23.4 1.7 %copy-start.3 = (s32[3,1,8]{2,1,0:T(1,128)S(1)}, s32[3,1,8]{2,1,0:T(1,128)}, u32[]{:S(2)}) copy-start(s32[3,1,8]{2,1,0:T(1,128)} %shift_ref.1) | copy-start | bytes 292
  23.4 1.7 %copy-start.4 = (s32[1,8]{1,0:T(1,128)S(1)}, s32[1,8]{1,0:T(1,128)}, u32[]{:S(2)}) copy-start(s32[1,8]{1,0:T(1,128)} %list_ref.1) | copy-start | bytes 100
  23.4 1.7 %copy-start.5 = (s32[1,8]{1,0:T(1,128)S(1)}, s32[1,8]{1,0:T(1,128)}, u32[]{:S(2)}) copy-start(s32[1,8]{1,0:T(1,128)} %valid_ref.1) | copy-start | bytes 100
  23.4 1.7 %copy-start.6 = (f32[3]{0:T(128)S(1)}, f32[3]{0:T(128)}, u32[]{:S(2)}) copy-start(f32[3]{0:T(128)} %cell_ref.1) | copy-start | bytes 40
  23.4 1.6 %collective-permute-start.9 = (bf16[136,512]{1,0:T(8,128)(2,1)S(1)}, bf16[136,512]{1,0:T(8,128)(2,1)S(1)}, u32[]{:S(2)}, u32[]{:S(2)}) collective-permute-start(bf16[136,512]{1,0:T(8,128)(2,1)S(1)} %collective-permute-done.6.refs_0_.refs_3_), channel_id=1, source_target_pairs={{0,8},{1,9},{2,10},{3,11},{4,12},{5,13},{6,14},{7,15},{8,0},{9,1},... | collective-permute-start | bytes 417800 | tf_op jit(solution)/shard_map/ppermute | solution.py:599

commit v4 on v3

--- a/solution.py
+++ b/solution.py
@@ -247,12 +247,16 @@
     copies = [pltpu.make_async_copy(src, dst, sems.at[k]) for k, (src, dst) in enumerate(pairs)]
     for copy in copies:
         copy.start()
+    return copies
+
+
+def settle(copies):
     for copy in copies:
         copy.wait()
 
 
 def pack_kernel(feat_hbm, gain_hbm, pos_hbm, out_ref, feat_ref, gain_ref, pos_ref, tmp_ref, sems):
-    fetch(((feat_hbm, feat_ref), (gain_hbm, gain_ref), (pos_hbm, pos_ref)), sems)
+    settle(fetch(((feat_hbm, feat_ref), (gain_hbm, gain_ref), (pos_hbm, pos_ref)), sems))
     atoms, dim = feat_ref.shape
     floats = feat_ref[...].astype(jnp.float32)
     spread = jnp.mean(floats * floats, axis=-1, keepdims=True)
@@ -288,7 +292,7 @@
 ):
     atoms = pack_ref.shape[0]
     dim = wq_ref.shape[0]
-    fetch(
+    copies = fetch(
         (
             (wqkv_hbm.at[:, pl.ds(0, dim)], wq_ref),
             (rw_hbm, rw_ref),
@@ -300,16 +304,12 @@
     )
     groups, rows, width = qexp_ref.shape
     per = rows // atoms
-    q = mm(pack_ref[:, :dim], wq_ref[...], ((1,), (0,)))
-    q = q.astype(jnp.bfloat16).astype(jnp.float32)
-    lane = lax.broadcasted_iota(jnp.int32, (per, width), 1) // head_dim
-    sub = lax.broadcasted_iota(jnp.int32, (per, width), 0)
-    keep = (lane == sub)[None]
-    for g in range(groups):
-        part = q[:, g * width : (g + 1) * width]
-        spread = jnp.broadcast_to(part[:, None, :], (atoms, per, width))
-        spread = jnp.where(keep, spread, 0.0).reshape(rows, width)
-        qexp_ref[g] = spread.astype(jnp.bfloat16)
+    pos = pack_ref[:, dim:].astype(jnp.float32)
+    pos = pos + pltpu.roll(pos, 120, 1) + pltpu.roll(pos, 112, 1)
+    own_ref[0] = pos
+    own_ref[1] = jnp.cos(two_pi * pos)
+    own_ref[2] = jnp.sin(two_pi * pos)
+    settle(copies[1:])
     h, m, l = parts_of(0.5 * rw_ref[...], 3)
     hidden = rw_ref.shape[1]
     row = lax.broadcasted_iota(jnp.int32, (16, hidden), 0)
@@ -321,11 +321,17 @@
     h, l = parts_of(pw_ref[...], 2)
     w2_ref[...] = jnp.concatenate([h, h, l], axis=1)
     str_ref[...] = jnp.broadcast_to(to_column(cs_ref[...]), str_ref.shape)
-    pos = pack_ref[:, dim:].astype(jnp.float32)
-    pos = pos + pltpu.roll(pos, 120, 1) + pltpu.roll(pos, 112, 1)
-    own_ref[0] = pos
-    own_ref[1] = jnp.cos(two_pi * pos)
-    own_ref[2] = jnp.sin(two_pi * pos)
+    settle(copies[:1])
+    q = mm(pack_ref[:, :dim], wq_ref[...], ((1,), (0,)))
+    q = q.astype(jnp.bfloat16).astype(jnp.float32)
+    lane = lax.broadcasted_iota(jnp.int32, (per, width), 1) // head_dim
+    sub = lax.broadcasted_iota(jnp.int32, (per, width), 0)
+    keep = (lane == sub)[None]
+    for g in range(groups):
+        part = q[:, g * width : (g + 1) * width]
+        spread = jnp.broadcast_to(part[:, None, :], (atoms, per, width))
+        spread = jnp.where(keep, spread, 0.0).reshape(rows, width)
+        qexp_ref[g] = spread.astype(jnp.bfloat16)
 
 
 def repack_kernel(*refs):

time: 28.9 us -> 28.9 us (level)
  no operation moved by 1% of the time
where the time goes in v4:
time: 28.9 us; the launch traced here: 28.8 us
  Pallas kernels  10.5 us (36%)
  starting transfers between devices  9.7 us (34%)
  waiting for transfers between devices  8.43 us (29%)
    pallas_call x8, Pallas kernels, call(): pl.pallas_call(kernel, out_shape=outs, in_specs=specs, out_specs=[vmem] *...  10.5 us
    ppermute x10, starting transfers between devices, swap(): return lax.ppermute(array, axes, [(i, i ^ mask) for i in range(total)])  9.7 us
    ppermute x10, waiting for transfers between devices, swap(): return lax.ppermute(array, axes, [(i, i ^ mask) for i in range(total)])  8.43 us
  transfers between devices with their start and end apart: 10, of which 5 were waited for; matrix products, arithmetic and copies ran while one was open for 0% of the time, Pallas kernels for 17%

profile of v4, /device:TPU:0, one launch (start us, length us, event | category | flops | bytes accessed | tf_op | source)
XLA Modules:
  0.0 28.8 jit_solution(8966393228420488673)
XLA Ops:
  0.0 0.0 copy-start
  0.0 1.1 %shard_map.127.pack_ref.refs_0_ = bf16[32,640]{1,0:T(8,128)(2,1)S(1)} custom-call(bf16[32,512]{1,0:T(8,128)(2,1)} %refs_15_.1, f32[1,512]{1,0:T(1,128)} %bitcast.5, f32[3,32]{1,0:T(4,128)} %pos_hbm.1), custom_call_target="tpu_custom_call" | custom-call | tf_op jit(solution)/shard_map/pallas_call | solution.py:558
  1.1 2.6 %collective-permute-start = (bf16[32,640]{1,0:T(8,128)(2,1)S(1)}, bf16[32,640]{1,0:T(8,128)(2,1)S(1)}, u32[]{:S(2)}, u32[]{:S(2)}) collective-permute-start(bf16[32,640]{1,0:T(8,128)(2,1)S(1)} %shard_map.127.pack_ref.refs_0_), channel_id=1, source_target_pairs={{0,10},{1,11},{2,8},{3,9},{4,14},{5,15},{6,12},{7,13},{8,2},{9,3},... | collective-permute-start | bytes 122888 | tf_op jit(solution)/shard_map/ppermute | solution.py:605
  3.6 2.9 %collective-permute-start.1 = (bf16[32,640]{1,0:T(8,128)(2,1)S(1)}, bf16[32,640]{1,0:T(8,128)(2,1)S(1)}, u32[]{:S(2)}, u32[]{:S(2)}) collective-permute-start(bf16[32,640]{1,0:T(8,128)(2,1)S(1)} %shard_map.127.pack_ref.refs_0_), channel_id=1, source_target_pairs={{0,12},{1,13},{2,14},{3,15},{4,8},{5,9},{6,10},{7,11},{8,4},{9,5},... | collective-permute-start | bytes 122888 | tf_op jit(solution)/shard_map/ppermute | solution.py:605
  6.5 0.0 collective-permute-start.2
  6.5 1.4 %shard_map.128 = (bf16[2,256,256]{2,1,0:T(8,128)(2,1)S(1)}, bf16[64,112]{1,0:T(8,128)(2,1)S(1)}, bf16[16,192]{1,0:T(8,128)(2,1)S(1)}, f32[16,128]{1,0:T(8,128)S(1)}, f32[3,32,128]{2,1,0:T(8,128)S(1)}) custom-call(bf16[512,1536]{1,0:T(8,128)(2,1)} %refs_8_.1, f32[16,64]{1,0:T(8,128)} %rw_hbm.1, f32[1,64]{1,0:T(1,128)} %bitcast.6, f32[16,64]{1,0:T(8,128)} %bitcast.4, ...), custom_call_target="tpu_custom_call" | custom-call | tf_op jit(solution)/shard_map/pallas_call | solution.py:558
  7.9 0.0 collective-permute-done.refs_1_
  7.9 0.3 %collective-permute-done.1.refs_2_ = bf16[32,640]{1,0:T(8,128)(2,1)S(1)} collective-permute-done((bf16[32,640]{1,0:T(8,128)(2,1)S(1)}, bf16[32,640]{1,0:T(8,128)(2,1)S(1)}, u32[]{:S(2)}, u32[]{:S(2)}) %collective-permute-start.1) | collective-permute-done | bytes 40992 | tf_op jit(solution)/shard_map/ppermute | solution.py:605
  8.2 4.0 %collective-permute-done.2.refs_3_ = bf16[32,640]{1,0:T(8,128)(2,1)S(1)} collective-permute-done((bf16[32,640]{1,0:T(8,128)(2,1)S(1)}, bf16[32,640]{1,0:T(8,128)(2,1)S(1)}, u32[]{:S(2)}, u32[]{:S(2)}) %collective-permute-start.2) | collective-permute-done | bytes 40992 | tf_op jit(solution)/shard_map/ppermute | solution.py:605
  12.2 0.2 shard_map.129.refs_0_
  12.3 0.0 copy-done
  12.3 0.8 %shard_map.130 = (bf16[1024,1024]{1,0:T(8,128)(2,1)S(1)}, f32[2,32,8,256]{3,2,1,0:T(8,128)S(1)}, f32[2,32,8,128]{3,2,1,0:T(8,128)S(1)}, f32[2,32,8,128]{3,2,1,0:T(8,128)S(1)}) custom-call(bf16[136,512]{1,0:T(8,128)(2,1)S(1)} %shard_map.129.refs_0_, bf16[512,1536]{1,0:T(8,128)(2,1)S(1)} %copy-done, ...), custom_call_target="tpu_custom_call" | custom-call | tf_op jit(solution)/shard_map/pallas_call | solution.py:558
  13.1 0.2 collective-permute-start.5
  13.3 1.5 %collective-permute-start.3 = (bf16[136,512]{1,0:T(8,128)(2,1)S(1)}, bf16[136,512]{1,0:T(8,128)(2,1)S(1)}, u32[]{:S(2)}, u32[]{:S(2)}) collective-permute-start(bf16[136,512]{1,0:T(8,128)(2,1)S(1)} %shard_map.129.refs_0_), channel_id=1, source_target_pairs={{0,9},{1,8},{2,11},{3,10},{4,13},{5,12},{6,15},{7,14},{8,1},{9,0},... | collective-permute-start | bytes 417800 | tf_op jit(solution)/shard_map/ppermute | solution.py:605
  14.8 1.2 %collective-permute-start.4 = (bf16[136,512]{1,0:T(8,128)(2,1)S(1)}, bf16[136,512]{1,0:T(8,128)(2,1)S(1)}, u32[]{:S(2)}, u32[]{:S(2)}) collective-permute-start(bf16[136,512]{1,0:T(8,128)(2,1)S(1)} %shard_map.129.refs_0_), channel_id=1, source_target_pairs={{0,24},{1,25},{2,26},{3,27},{4,28},{5,29},{6,30},{7,31},{8,16},{9,... | collective-permute-start | bytes 417800 | tf_op jit(solution)/shard_map/ppermute | solution.py:605
  16.0 0.5 %collective-permute-start.6 = (bf16[136,512]{1,0:T(8,128)(2,1)S(1)}, bf16[136,512]{1,0:T(8,128)(2,1)S(1)}, u32[]{:S(2)}, u32[]{:S(2)}) collective-permute-start(bf16[136,512]{1,0:T(8,128)(2,1)S(1)} %shard_map.129.refs_0_), channel_id=1, source_target_pairs={{0,25},{1,24},{2,27},{3,26},{4,29},{5,28},{6,31},{7,30},{8,17},{9,... | collective-permute-start | bytes 417800 | tf_op jit(solution)/shard_map/ppermute | solution.py:605
  16.5 0.0 collective-permute-done.5.refs_0_.refs_4_
  16.5 0.9 %shard_map.131 = (bf16[1024,1024]{1,0:T(8,128)(2,1)S(1)}, f32[2,32,8,256]{3,2,1,0:T(8,128)S(1)}, f32[2,32,8,128]{3,2,1,0:T(8,128)S(1)}, f32[2,32,8,128]{3,2,1,0:T(8,128)S(1)}) custom-call(bf16[136,512]{1,0:T(8,128)(2,1)S(1)} %collective-permute-done.5.refs_0_.refs_4_, ...), custom_call_target="tpu_custom_call", output_to_operand_aliasing={{0}: (5, {}), {1}: (6, {}), {2}: (7, {}), {3}: (8, {})} | custom-call | tf_op jit(solution)/shard_map/pallas_call | solution.py:558
  17.4 1.2 %collective-permute-done.3.refs_0_.refs_1_ = bf16[136,512]{1,0:T(8,128)(2,1)S(1)} collective-permute-done((bf16[136,512]{1,0:T(8,128)(2,1)S(1)}, bf16[136,512]{1,0:T(8,128)(2,1)S(1)}, u32[]{:S(2)}, u32[]{:S(2)}) %collective-permute-start.3) | collective-permute-done | bytes 139296 | tf_op jit(solution)/shard_map/ppermute | solution.py:605
  18.7 1.8 %collective-permute-done.4.refs_1_.refs_2_ = bf16[136,512]{1,0:T(8,128)(2,1)S(1)} collective-permute-done((bf16[136,512]{1,0:T(8,128)(2,1)S(1)}, bf16[136,512]{1,0:T(8,128)(2,1)S(1)}, u32[]{:S(2)}, u32[]{:S(2)}) %collective-permute-start.4) | collective-permute-done | bytes 139296 | tf_op jit(solution)/shard_map/ppermute | solution.py:605
  20.5 0.7 %collective-permute-start.7 = (bf16[136,512]{1,0:T(8,128)(2,1)S(1)}, bf16[136,512]{1,0:T(8,128)(2,1)S(1)}, u32[]{:S(2)}, u32[]{:S(2)}) collective-permute-start(bf16[136,512]{1,0:T(8,128)(2,1)S(1)} %collective-permute-done.3.refs_0_.refs_1_), channel_id=1, source_target_pairs={{0,8},{1,9},{2,10},{3,11},{4,12},{5,13},{6,14},{7,15},{8,0},{9,1},... | collective-permute-start | bytes 417800 | tf_op jit(solution)/shard_map/ppermute | solution.py:605
  21.2 0.0 collective-permute-start.8
  21.2 1.1 %shard_map.132 = (bf16[1024,1024]{1,0:T(8,128)(2,1)S(1)}, f32[2,32,8,256]{3,2,1,0:T(8,128)S(1)}, f32[2,32,8,128]{3,2,1,0:T(8,128)S(1)}, f32[2,32,8,128]{3,2,1,0:T(8,128)S(1)}) custom-call(bf16[136,512]{1,0:T(8,128)(2,1)S(1)} %collective-permute-done.3.refs_0_.refs_1_, ...), custom_call_target="tpu_custom_call", output_to_operand_aliasing={{0}: (6, {}), {1}: (7, {}), {2}: (8, {}), {3}: (9, {})} | custom-call | tf_op jit(solution)/shard_map/pallas_call | solution.py:558
  22.3 1.1 %collective-permute-done.6.refs_0_.refs_3_ = bf16[136,512]{1,0:T(8,128)(2,1)S(1)} collective-permute-done((bf16[136,512]{1,0:T(8,128)(2,1)S(1)}, bf16[136,512]{1,0:T(8,128)(2,1)S(1)}, u32[]{:S(2)}, u32[]{:S(2)}) %collective-permute-start.6) | collective-permute-done | bytes 139296 | tf_op jit(solution)/shard_map/ppermute | solution.py:605
  23.4 0.0 copy-start.1
  23.4 0.0 copy-start.2
  23.4 0.0 copy-start.3
  23.4 0.0 copy-start.4
  23.4 0.0 copy-start.5
  23.4 0.0 copy-start.6
  23.4 0.2 collective-permute-start.9
  23.6 0.0 collective-permute-done.7.refs_1_.refs_5_
  23.6 0.0 collective-permute-done.8.refs_2_.refs_6_
  23.6 1.4 %shard_map.133 = (bf16[1024,1024]{1,0:T(8,128)(2,1)S(1)}, f32[2,32,8,256]{3,2,1,0:T(8,128)S(1)}, f32[2,32,8,128]{3,2,1,0:T(8,128)S(1)}, f32[2,32,8,128]{3,2,1,0:T(8,128)S(1)}) custom-call(bf16[136,512]{1,0:T(8,128)(2,1)S(1)} %collective-permute-done.6.refs_0_.refs_3_, ...), custom_call_target="tpu_custom_call", output_to_operand_aliasing={{0}: (7, {}), {1}: (8, {}), {2}: (9, {}), {3}: (10, {})} | custom-call | tf_op jit(solution)/shard_map/pallas_call | solution.py:558
  25.1 0.0 collective-permute-done.9.refs_7_
  25.1 0.0 copy-done.1
  25.1 0.0 copy-done.2
  25.1 0.0 copy-done.3
  25.1 0.0 copy-done.4
  25.1 0.0 copy-done.5
  25.1 0.0 copy-done.6
  25.1 3.7 %shard_map.134 = (bf16[32,512]{1,0:T(8,128)(2,1)}, bf16[1024,1024]{1,0:T(8,128)(2,1)S(1)}) custom-call(s32[1,8]{1,0:T(1,128)S(1)} %copy-done.4, s32[1,8]{1,0:T(1,128)S(1)} %copy-done.5, s32[3,1,8]{2,1,0:T(1,128)S(1)} %copy-done.3, f32[3]{0:T(128)S(1)} %copy-done.6, bf16[136,512]{1,0:T(8,128)(2,1)S(1)} %shard_map.129.refs_0_, ...), custom_call_target="tpu_custom_call", output_to_operand_aliasing={{1}: (20, {})} | custom-call | tf_op jit(solution)/shard_map/pallas_call | solution.py:558
Async XLA Ops:
  0.0 12.3 %copy-start = (bf16[512,1536]{1,0:T(8,128)(2,1)S(1)}, bf16[512,1536]{1,0:T(8,128)(2,1)}, u32[]{:S(2)}) copy-start(bf16[512,1536]{1,0:T(8,128)(2,1)} %refs_8_.1) | copy-start | bytes 4718596
  1.1 6.8 %collective-permute-start = (bf16[32,640]{1,0:T(8,128)(2,1)S(1)}, bf16[32,640]{1,0:T(8,128)(2,1)S(1)}, u32[]{:S(2)}, u32[]{:S(2)}) collective-permute-start(bf16[32,640]{1,0:T(8,128)(2,1)S(1)} %shard_map.127.pack_ref.refs_0_), channel_id=1, source_target_pairs={{0,10},{1,11},{2,8},{3,9},{4,14},{5,15},{6,12},{7,13},{8,2},{9,3},... | collective-permute-start | bytes 122888 | tf_op jit(solution)/shard_map/ppermute | solution.py:605
  3.6 4.6 %collective-permute-start.1 = (bf16[32,640]{1,0:T(8,128)(2,1)S(1)}, bf16[32,640]{1,0:T(8,128)(2,1)S(1)}, u32[]{:S(2)}, u32[]{:S(2)}) collective-permute-start(bf16[32,640]{1,0:T(8,128)(2,1)S(1)} %shard_map.127.pack_ref.refs_0_), channel_id=1, source_target_pairs={{0,12},{1,13},{2,14},{3,15},{4,8},{5,9},{6,10},{7,11},{8,4},{9,5},... | collective-permute-start | bytes 122888 | tf_op jit(solution)/shard_map/ppermute | solution.py:605
  6.5 5.6 %collective-permute-start.2 = (bf16[32,640]{1,0:T(8,128)(2,1)S(1)}, bf16[32,640]{1,0:T(8,128)(2,1)S(1)}, u32[]{:S(2)}, u32[]{:S(2)}) collective-permute-start(bf16[32,640]{1,0:T(8,128)(2,1)S(1)} %shard_map.127.pack_ref.refs_0_), channel_id=1, source_target_pairs={{0,14},{1,15},{2,12},{3,13},{4,10},{5,11},{6,8},{7,9},{8,6},{9,7},... | collective-permute-start | bytes 122888 | tf_op jit(solution)/shard_map/ppermute | solution.py:605
  13.1 3.4 %collective-permute-start.5 = (bf16[136,512]{1,0:T(8,128)(2,1)S(1)}, bf16[136,512]{1,0:T(8,128)(2,1)S(1)}, u32[]{:S(2)}, u32[]{:S(2)}) collective-permute-start(bf16[136,512]{1,0:T(8,128)(2,1)S(1)} %shard_map.129.refs_0_), channel_id=1, source_target_pairs={{0,8},{1,9},{2,10},{3,11},{4,12},{5,13},{6,14},{7,15},{8,0},{9,1},... | collective-permute-start | bytes 417800 | tf_op jit(solution)/shard_map/ppermute | solution.py:605
  13.3 5.4 %collective-permute-start.3 = (bf16[136,512]{1,0:T(8,128)(2,1)S(1)}, bf16[136,512]{1,0:T(8,128)(2,1)S(1)}, u32[]{:S(2)}, u32[]{:S(2)}) collective-permute-start(bf16[136,512]{1,0:T(8,128)(2,1)S(1)} %shard_map.129.refs_0_), channel_id=1, source_target_pairs={{0,9},{1,8},{2,11},{3,10},{4,13},{5,12},{6,15},{7,14},{8,1},{9,0},... | collective-permute-start | bytes 417800 | tf_op jit(solution)/shard_map/ppermute | solution.py:605
  14.8 5.7 %collective-permute-start.4 = (bf16[136,512]{1,0:T(8,128)(2,1)S(1)}, bf16[136,512]{1,0:T(8,128)(2,1)S(1)}, u32[]{:S(2)}, u32[]{:S(2)}) collective-permute-start(bf16[136,512]{1,0:T(8,128)(2,1)S(1)} %shard_map.129.refs_0_), channel_id=1, source_target_pairs={{0,24},{1,25},{2,26},{3,27},{4,28},{5,29},{6,30},{7,31},{8,16},{9,... | collective-permute-start | bytes 417800 | tf_op jit(solution)/shard_map/ppermute | solution.py:605
  16.0 7.4 %collective-permute-start.6 = (bf16[136,512]{1,0:T(8,128)(2,1)S(1)}, bf16[136,512]{1,0:T(8,128)(2,1)S(1)}, u32[]{:S(2)}, u32[]{:S(2)}) collective-permute-start(bf16[136,512]{1,0:T(8,128)(2,1)S(1)} %shard_map.129.refs_0_), channel_id=1, source_target_pairs={{0,25},{1,24},{2,27},{3,26},{4,29},{5,28},{6,31},{7,30},{8,17},{9,... | collective-permute-start | bytes 417800 | tf_op jit(solution)/shard_map/ppermute | solution.py:605
  20.5 3.1 %collective-permute-start.7 = (bf16[136,512]{1,0:T(8,128)(2,1)S(1)}, bf16[136,512]{1,0:T(8,128)(2,1)S(1)}, u32[]{:S(2)}, u32[]{:S(2)}) collective-permute-start(bf16[136,512]{1,0:T(8,128)(2,1)S(1)} %collective-permute-done.3.refs_0_.refs_1_), channel_id=1, source_target_pairs={{0,8},{1,9},{2,10},{3,11},{4,12},{5,13},{6,14},{7,15},{8,0},{9,1},... | collective-permute-start | bytes 417800 | tf_op jit(solution)/shard_map/ppermute | solution.py:605
  21.2 2.4 %collective-permute-start.8 = (bf16[136,512]{1,0:T(8,128)(2,1)S(1)}, bf16[136,512]{1,0:T(8,128)(2,1)S(1)}, u32[]{:S(2)}, u32[]{:S(2)}) collective-permute-start(bf16[136,512]{1,0:T(8,128)(2,1)S(1)} %collective-permute-done.4.refs_1_.refs_2_), channel_id=1, source_target_pairs={{0,8},{1,9},{2,10},{3,11},{4,12},{5,13},{6,14},{7,15},{8,0},{9,1},... | collective-permute-start | bytes 417800 | tf_op jit(solution)/shard_map/ppermute | solution.py:605
  23.4 1.7 %copy-start.1 = (bf16[512,512]{1,0:T(8,128)(2,1)S(1)}, bf16[512,512]{1,0:T(8,128)(2,1)}, u32[]{:S(2)}) copy-start(bf16[512,512]{1,0:T(8,128)(2,1)} %refs_14_.1) | copy-start | bytes 1572868
  23.4 1.7 %copy-start.2 = (bf16[32,512]{1,0:T(8,128)(2,1)S(1)}, bf16[32,512]{1,0:T(8,128)(2,1)}, u32[]{:S(2)}) copy-start(bf16[32,512]{1,0:T(8,128)(2,1)} %refs_15_.1) | copy-start | bytes 98308
  23.4 1.7 %copy-start.3 = (s32[3,1,8]{2,1,0:T(1,128)S(1)}, s32[3,1,8]{2,1,0:T(1,128)}, u32[]{:S(2)}) copy-start(s32[3,1,8]{2,1,0:T(1,128)} %shift_ref.1) | copy-start | bytes 292
  23.4 1.7 %copy-start.4 = (s32[1,8]{1,0:T(1,128)S(1)}, s32[1,8]{1,0:T(1,128)}, u32[]{:S(2)}) copy-start(s32[1,8]{1,0:T(1,128)} %list_ref.1) | copy-start | bytes 100
  23.4 1.7 %copy-start.5 = (s32[1,8]{1,0:T(1,128)S(1)}, s32[1,8]{1,0:T(1,128)}, u32[]{:S(2)}) copy-start(s32[1,8]{1,0:T(1,128)} %valid_ref.1) | copy-start | bytes 100
  23.4 1.7 %copy-start.6 = (f32[3]{0:T(128)S(1)}, f32[3]{0:T(128)}, u32[]{:S(2)}) copy-start(f32[3]{0:T(128)} %cell_ref.1) | copy-start | bytes 40
  23.4 1.6 %collective-permute-start.9 = (bf16[136,512]{1,0:T(8,128)(2,1)S(1)}, bf16[136,512]{1,0:T(8,128)(2,1)S(1)}, u32[]{:S(2)}, u32[]{:S(2)}) collective-permute-start(bf16[136,512]{1,0:T(8,128)(2,1)S(1)} %collective-permute-done.6.refs_0_.refs_3_), channel_id=1, source_target_pairs={{0,8},{1,9},{2,10},{3,11},{4,12},{5,13},{6,14},{7,15},{8,0},{9,1},... | collective-permute-start | bytes 417800 | tf_op jit(solution)/shard_map/ppermute | solution.py:605

commit v5 on v4

--- a/solution.py
+++ b/solution.py
@@ -334,27 +334,37 @@
         qexp_ref[g] = spread.astype(jnp.bfloat16)
 
 
+def position_tile(blocks, dim):
+    pos = jnp.concatenate([block[:, dim:] for block in blocks], axis=0)
+    r = lax.broadcasted_iota(jnp.int32, (8, 128), 0)
+    c = lax.broadcasted_iota(jnp.int32, (8, 128), 1)
+    out = []
+    for p in range(3):
+        pick = ((c == 8 * p + r) & (r < 3)).astype(jnp.bfloat16)
+        part = mm(pick, pos, ((1,), (1,)))
+        if part.shape[1] < 128:
+            part = jnp.concatenate([part, jnp.zeros((8, 128 - part.shape[1]), jnp.float32)], axis=1)
+        out.append(part)
+    out.append(jnp.zeros((8, dim - 3 * 128), jnp.float32))
+    return jnp.concatenate(out, axis=1).astype(jnp.bfloat16)
+
+
 def repack_kernel(*refs):
     blocks, out_ref = refs[:-1], refs[-1]
     atoms = blocks[0].shape[0]
     dim = out_ref.shape[1]
-    count = atoms * len(blocks)
     for k, block in enumerate(blocks):
         out_ref[k * atoms : (k + 1) * atoms, :] = block[:, :dim]
-    pos = jnp.concatenate([block[:, dim:] for block in blocks], axis=0)
-    r = lax.broadcasted_iota(jnp.int32, (8, 128), 0)
-    c = lax.broadcasted_iota(jnp.int32, (8, 128), 1)
-    tail = []
-    for p in range(3):
-        pick = ((c == 8 * p + r) & (r < 3)).astype(jnp.bfloat16)
-        tail.append(mm(pick, pos, ((1,), (1,))))
-    tail.append(jnp.zeros((8, dim - 3 * count), jnp.float32))
-    out_ref[count:, :] = jnp.concatenate(tail, axis=1).astype(jnp.bfloat16)
-
-
-def piece_positions(piece_ref, count):
-    tail = piece_ref[count:, :].astype(jnp.float32)
-    return tail[:, :count] + tail[:, count : 2 * count] + tail[:, 2 * count : 3 * count]
+    out_ref[len(blocks) * atoms :, :] = position_tile(blocks, dim)
+
+
+def piece_tiles(piece, counts):
+    total = sum(counts)
+    out = []
+    for k in range(len(counts)):
+        tail = piece[total + 8 * k : total + 8 * (k + 1), :].astype(jnp.float32)
+        out.append(tail[:, :128] + tail[:, 128:256] + tail[:, 256:384])
+    return out
 
 
 def attend(qexp, keys, vals, scale, bias3):
@@ -369,17 +379,22 @@
     return top, total, o.reshape(atoms, per, vals.shape[1])
 
 
-def absorb(head_dim, places, pieces, wqkv_ref, qexp_ref, str_ref, own_ref, kv_ref):
+def absorb(head_dim, plan, pieces, wqkv_ref, qexp_ref, str_ref, own_ref, kv_ref):
     dim = wqkv_ref.shape[0]
     atoms = own_ref.shape[1]
     groups, rows, width = qexp_ref.shape
     per = rows // atoms
-    count = pieces[0].shape[0] - 8
-    rows_in = jnp.concatenate([piece[:count, :] for piece in pieces], axis=0)
+    rows_in = jnp.concatenate(
+        [piece[: sum(counts), :] for piece, (_, counts) in zip(pieces, plan)], axis=0
+    )
     kv = mm(rows_in, wqkv_ref[:, dim:], ((1,), (0,))).astype(jnp.bfloat16)
-    for k, place in enumerate(places):
-        kv_ref[place * count : (place + 1) * count, :] = kv[k * count : (k + 1) * count]
-    pos8 = jnp.concatenate([piece_positions(piece, count) for piece in pieces], axis=1)
+    at = 0
+    tiles = []
+    for piece, (start, counts) in zip(pieces, plan):
+        kv_ref[start : start + sum(counts), :] = kv[at : at + sum(counts)]
+        at += sum(counts)
+        tiles += [t[:, :n] for t, n in zip(piece_tiles(piece, counts), counts)]
+    pos8 = jnp.concatenate(tiles, axis=1)
     cos_k, sin_k = jnp.cos(two_pi * pos8), jnp.sin(two_pi * pos8)
     waves = None
     for c in range(3):
@@ -409,11 +424,19 @@
     return jnp.concatenate([array] * (lanes // array.shape[-1]), axis=-1)
 
 
-def first_kernel(head_dim, places, *refs):
-    pieces = refs[: len(places)]
-    wqkv_ref, qexp_ref, str_ref, own_ref = refs[len(places) : -4]
-    kv_ref, acc_ref, top_ref, sum_ref = refs[-4:]
-    got = absorb(head_dim, places, pieces, wqkv_ref, qexp_ref, str_ref, own_ref, kv_ref)
+def first_kernel(head_dim, plan, own_ref0, *refs):
+    blocks = (own_ref0,) + refs[:3]
+    ring_ref, wqkv_ref, qexp_ref, str_ref, own_ref = refs[3:8]
+    core_ref, kv_ref, acc_ref, top_ref, sum_ref = refs[8:]
+    atoms = own_ref.shape[1]
+    dim = wqkv_ref.shape[0]
+    four, three = plan[0][1]
+    for k, block in enumerate(blocks):
+        core_ref[k * atoms : (k + 1) * atoms, :] = block[:, :dim]
+    core_ref[four : four + three, :] = ring_ref[:three, :]
+    core_ref[four + three : four + three + 8, :] = position_tile(blocks, dim)
+    core_ref[four + three + 8 :, :] = ring_ref[three:, :]
+    got = absorb(head_dim, plan, (core_ref,), wqkv_ref, qexp_ref, str_ref, own_ref, kv_ref)
     for g, (top, total, o) in enumerate(got):
         acc_ref[g] = o
         top_ref[g] = widen(top, 128)
@@ -430,11 +453,11 @@
     return best, summed, acc
 
 
-def next_kernel(head_dim, places, *refs):
-    pieces = refs[: len(places)]
-    wqkv_ref, qexp_ref, str_ref, own_ref = refs[len(places) : len(places) + 4]
-    _, acc_in, top_in, sum_in, kv_ref, acc_ref, top_ref, sum_ref = refs[len(places) + 4 :]
-    got = absorb(head_dim, places, pieces, wqkv_ref, qexp_ref, str_ref, own_ref, kv_ref)
+def next_kernel(head_dim, plan, *refs):
+    pieces = refs[: len(plan)]
+    wqkv_ref, qexp_ref, str_ref, own_ref = refs[len(plan) : len(plan) + 4]
+    _, acc_in, top_in, sum_in, kv_ref, acc_ref, top_ref, sum_ref = refs[len(plan) + 4 :]
+    got = absorb(head_dim, plan, pieces, wqkv_ref, qexp_ref, str_ref, own_ref, kv_ref)
     for g in range(len(got)):
         best, summed, acc = merge(got, g, acc_in, top_in, sum_in)
         acc_ref[g] = acc
@@ -449,7 +472,7 @@
     return out
 
 
-def last_kernel(head_dim, locate, col_count, list_ref, valid_ref, shift_ref, cell_ref, *refs):
+def last_kernel(head_dim, locate, plan, col_count, list_ref, valid_ref, shift_ref, cell_ref, *refs):
     piece_refs = refs[:8]
     (
         wqkv_ref,
@@ -474,24 +497,25 @@
     atoms = own_ref.shape[1]
     groups, rows, width = qexp_ref.shape
     per = rows // atoms
-    count = piece_refs[0].shape[0] - 8
-    got = absorb(head_dim, (7,), piece_refs[7:], wqkv_ref, qexp_ref, str_ref, own_ref, kv_ref)
-    for k in range(8):
-        pos_ref[k] = piece_positions(piece_refs[k], count)
+    got = absorb(head_dim, plan[7:], piece_refs[7:], wqkv_ref, qexp_ref, str_ref, own_ref, kv_ref)
+    at = 0
+    for piece, (_, counts) in zip(piece_refs, plan):
+        for tile in piece_tiles(piece, counts):
+            pos_ref[at] = tile
+            at += 1
     me = lax.axis_index("rows") * col_count + lax.axis_index("cols")
     entries = list_ref.shape[1]
     listed = entries * atoms
     lane = lax.broadcasted_iota(jnp.int32, (1, listed), 1) // atoms
-    in_tile = lax.broadcasted_iota(jnp.int32, (1, count), 1) // atoms
-    a_tile = count // atoms
+    a_tile = 128 // atoms
+    in_tile = lax.broadcasted_iota(jnp.int32, (1, 128), 1) // atoms
     tiles = []
     for e in range(entries):
-        up, across, turn = locate(list_ref[0, e] ^ me)
-        place = across + 4 * turn
-        start = pl.multiple_of((place * a_tile + up) * atoms, atoms)
+        slot, tile, spot = locate(list_ref[0, e] ^ me)
+        start = pl.multiple_of(slot * atoms, atoms)
         near_ref[e * atoms : (e + 1) * atoms, :] = kv_ref[pl.ds(start, atoms), :]
         into = e % a_tile
-        moved = pltpu.roll(pos_ref[place], (into - up + a_tile) % a_tile * atoms, 1)
+        moved = pltpu.roll(pos_ref[tile], (into - spot + a_tile) % a_tile * atoms, 1)
         if into == 0:
             tiles.append(moved)
         else:
@@ -609,7 +633,11 @@
         across = (rel & 1) + 2 * ((rel >> across_bits[1]) & 1)
         turn = (rel >> col_bits) & 1
         turn = turn ^ jnp.minimum(up, 1) ^ jnp.minimum(across, 1)
-        return up, across, turn
+        far = jnp.minimum(up, 1)
+        slot = turn * 16 + across + far * (3 + 2 * across + up)
+        tile = turn * 5 + far * (1 + across)
+        spot = across + far * (up - 1 - across)
+        return slot, tile, spot
 
     tied = lax.optimization_barrier
     pack = call(
@@ -626,7 +654,10 @@
         (features, norm_gain[None], positions),
         hbm=3,
     )
+    across_masks = {"e": 1 | flip, "n": (1 << across_bits[1]) | flip}
+    across_masks["d"] = 1 | across_masks["n"]
     ups = [swap(pack, (d << 1) | flip) for d in (1, 2, 3)]
+    owns = [swap(pack, mask) for mask in across_masks.values()]
     ready = call(
         functools.partial(query_kernel, head_dim),
         [
@@ -648,33 +679,33 @@
         (w_qkv, rbf_weight, rbf_offset[None], pair_weight.T, cosine_scale[None], pack),
         hbm=5,
     )
-    ups, ready = tied((ups, ready))
     qexp, w1, w2, strength, own = ready
-    count = 4 * atoms
-    base = call(repack_kernel, vm((count + 8, dim), bf16), [], 0, (pack, *ups))
-    east = swap(base, 1 | flip)
-    north = swap(base, (1 << across_bits[1]) | flip)
-    diag = swap(base, 1 | (1 << across_bits[1]) | flip)
+    four, three = 4 * atoms, 3 * atoms
+    ring = call(repack_kernel, vm((three + 8, dim), bf16), [], 0, tuple(ups))
+    east, north, diag = [swap(ring, mask) for mask in across_masks.values()]
     state_shapes = [
-        vm((8 * count, 2 * dim), bf16),
+        vm((total * atoms, 2 * dim), bf16),
         vm((groups, atoms, per, width), f32),
         vm((groups, atoms, per, 128), f32),
         vm((groups, atoms, per, 128), f32),
     ]
     common = (w_qkv, qexp, strength, own)
+    half = total // 2 * atoms
+    plan = [(0, (four, three))] + [(four + k * three, (three,)) for k in (1, 2, 3)]
+    plan += [(half + start, counts) for start, counts in plan]
+
+    core, *state = call(
+        functools.partial(first_kernel, head_dim, plan[:1]),
+        [vm((four + three + 16, dim), bf16)] + state_shapes,
+        [],
+        0,
+        (pack, *owns, ring, *common),
+    )
 
     def step(places, pieces, state):
-        if state is None:
-            return call(
-                functools.partial(first_kernel, head_dim, places),
-                state_shapes,
-                [],
-                0,
-                (*pieces, *common),
-            )
         at = len(pieces) + len(common)
         return call(
-            functools.partial(next_kernel, head_dim, places),
+            functools.partial(next_kernel, head_dim, [plan[k] for k in places]),
             state_shapes,
             [],
             0,
@@ -682,24 +713,20 @@
             {at + k: k for k in range(4)},
         )
 
-    state = step((0,), (base,), None)
-    base_late, state = tied((base, state))
-    base2 = swap(base_late, flip)
-    base2, state = tied((base2, state))
-    state = step((4,), (base2,), state)
+    core2 = swap(core, flip)
     east, north, state = tied((east, north, state))
     east2, north2 = swap(east, flip), swap(north, flip)
-    state = step((1, 2), (east, north), state)
+    state = step((1, 2, 4), (east, north, core2), state)
     diag, state = tied((diag, state))
     diag2 = swap(diag, flip)
     state = step((3, 5, 6), (diag, east2, north2), state)
     diag2, state = tied((diag2, state))
     updated, _ = call(
-        functools.partial(last_kernel, head_dim, locate, col_count),
+        functools.partial(last_kernel, head_dim, locate, plan, col_count),
         [jax.ShapeDtypeStruct((atoms, dim), bf16), state_shapes[0]],
         [
             vm((entries * atoms, 2 * dim), bf16),
-            vm((8, 8, count), f32),
+            vm((10, 8, 128), f32),
             vm((groups, atoms, per, entries * atoms), f32),
         ],
         4,
@@ -708,11 +735,11 @@
             block_valid,
             image_offsets,
             cell_lengths,
-            base,
+            core,
             east,
             north,
             diag,
-            base2,
+            core2,
             east2,
             north2,
             diag2,

time: 28.9 us -> 29.9 us (1.035)
  starting transfers between devices: 9.7 us -> 12.5 us
  waiting for transfers between devices: 8.43 us -> 7.29 us
  Pallas kernels: 10.5 us -> 9.82 us
    ppermute x10 -> x13, starting transfers between devices: 9.7 us -> 12.5 us  [swap(): return lax.ppermute(array, axes, [(i, i ^ mask) for i in range(total)])]
    ppermute x10 -> x13, waiting for transfers between devices: 8.43 us -> 7.29 us  [swap(): return lax.ppermute(array, axes, [(i, i ^ mask) for i in range(total)])]
    pallas_call x8 -> x7, Pallas kernels: 10.5 us -> 9.82 us  [call(): pl.pallas_call(kernel, out_shape=outs, in_specs=specs, out_specs=[vmem] *...]
  transfers between devices with their start and end apart: 10 -> 13, of which waited for: 5 -> 5; matrix products, arithmetic and copies ran while one was open for 0% -> 0% of each run, Pallas kernels for 17% -> 14%
where the time goes in v5:
time: 29.9 us; the launch traced here: 29.8 us
  starting transfers between devices  12.5 us (42%)
  Pallas kernels  9.82 us (33%)
  waiting for transfers between devices  7.29 us (24%)
    ppermute x13, starting transfers between devices, swap(): return lax.ppermute(array, axes, [(i, i ^ mask) for i in range(total)])  12.5 us
    pallas_call x7, Pallas kernels, call(): pl.pallas_call(kernel, out_shape=outs, in_specs=specs, out_specs=[vmem] *...  9.82 us
    ppermute x13, waiting for transfers between devices, swap(): return lax.ppermute(array, axes, [(i, i ^ mask) for i in range(total)])  7.29 us
  transfers between devices with their start and end apart: 13, of which 5 were waited for; matrix products, arithmetic and copies ran while one was open for 0% of the time, Pallas kernels for 14%

profile of v5, /device:TPU:0, one launch (start us, length us, event | category | flops | bytes accessed | tf_op | source)
XLA Modules:
  0.0 29.8 jit_solution(15107820194609202689)
XLA Ops:
  0.0 0.0 copy-start
  0.0 1.1 %shard_map.127.pack_ref.own_ref0 = bf16[32,640]{1,0:T(8,128)(2,1)S(1)} custom-call(bf16[32,512]{1,0:T(8,128)(2,1)} %refs_15_.1, f32[1,512]{1,0:T(1,128)} %bitcast.5, f32[3,32]{1,0:T(4,128)} %pos_hbm.1), custom_call_target="tpu_custom_call" | custom-call | tf_op jit(solution)/shard_map/pallas_call | solution.py:582
  1.1 4.6 %collective-permute-start.5 = (bf16[32,640]{1,0:T(8,128)(2,1)S(1)}, bf16[32,640]{1,0:T(8,128)(2,1)S(1)}, u32[]{:S(2)}, u32[]{:S(2)}) collective-permute-start(bf16[32,640]{1,0:T(8,128)(2,1)S(1)} %shard_map.127.pack_ref.own_ref0), channel_id=1, source_target_pairs={{0,14},{1,15},{2,12},{3,13},{4,10},{5,11},{6,8},{7,9},{8,6},{9,7},... | collective-permute-start | bytes 122888 | tf_op jit(solution)/shard_map/ppermute | solution.py:629
  5.7 0.0 collective-permute-start.4
  5.7 0.9 %collective-permute-start.3 = (bf16[32,640]{1,0:T(8,128)(2,1)S(1)}, bf16[32,640]{1,0:T(8,128)(2,1)S(1)}, u32[]{:S(2)}, u32[]{:S(2)}) collective-permute-start(bf16[32,640]{1,0:T(8,128)(2,1)S(1)} %shard_map.127.pack_ref.own_ref0), channel_id=1, source_target_pairs={{0,10},{1,11},{2,8},{3,9},{4,14},{5,15},{6,12},{7,13},{8,2},{9,3},... | collective-permute-start | bytes 122888 | tf_op jit(solution)/shard_map/ppermute | solution.py:629
  6.6 2.3 %collective-permute-start.2 = (bf16[32,640]{1,0:T(8,128)(2,1)S(1)}, bf16[32,640]{1,0:T(8,128)(2,1)S(1)}, u32[]{:S(2)}, u32[]{:S(2)}) collective-permute-start(bf16[32,640]{1,0:T(8,128)(2,1)S(1)} %shard_map.127.pack_ref.own_ref0), channel_id=1, source_target_pairs={{0,25},{1,24},{2,27},{3,26},{4,29},{5,28},{6,31},{7,30},{8,17},{9,... | collective-permute-start | bytes 122888 | tf_op jit(solution)/shard_map/ppermute | solution.py:629
  8.9 0.4 %collective-permute-start.1 = (bf16[32,640]{1,0:T(8,128)(2,1)S(1)}, bf16[32,640]{1,0:T(8,128)(2,1)S(1)}, u32[]{:S(2)}, u32[]{:S(2)}) collective-permute-start(bf16[32,640]{1,0:T(8,128)(2,1)S(1)} %shard_map.127.pack_ref.own_ref0), channel_id=1, source_target_pairs={{0,24},{1,25},{2,26},{3,27},{4,28},{5,29},{6,30},{7,31},{8,16},{9,... | collective-permute-start | bytes 122888 | tf_op jit(solution)/shard_map/ppermute | solution.py:629
  9.3 0.0 collective-permute-done.5.refs_2_
  9.3 0.0 collective-permute-start
  9.3 1.4 %shard_map.129 = (bf16[2,256,256]{2,1,0:T(8,128)(2,1)S(1)}, bf16[64,112]{1,0:T(8,128)(2,1)S(1)}, bf16[16,192]{1,0:T(8,128)(2,1)S(1)}, f32[16,128]{1,0:T(8,128)S(1)}, f32[3,32,128]{2,1,0:T(8,128)S(1)}) custom-call(bf16[512,1536]{1,0:T(8,128)(2,1)} %refs_8_.1, f32[16,64]{1,0:T(8,128)} %rw_hbm.1, f32[1,64]{1,0:T(1,128)} %bitcast.6, f32[16,64]{1,0:T(8,128)} %bitcast.4, ...), custom_call_target="tpu_custom_call" | custom-call | tf_op jit(solution)/shard_map/pallas_call | solution.py:582
  10.7 0.0 collective-permute-done.4.refs_1_
  10.7 0.0 collective-permute-done.3.refs_0_
  10.7 0.1 shard_map.128.refs_3_
  10.8 0.4 %collective-permute-done.2.refs_2_ = bf16[32,640]{1,0:T(8,128)(2,1)S(1)} collective-permute-done((bf16[32,640]{1,0:T(8,128)(2,1)S(1)}, bf16[32,640]{1,0:T(8,128)(2,1)S(1)}, u32[]{:S(2)}, u32[]{:S(2)}) %collective-permute-start.2) | collective-permute-done | bytes 40992 | tf_op jit(solution)/shard_map/ppermute | solution.py:629
  11.2 1.1 %collective-permute-done.1.refs_1_ = bf16[32,640]{1,0:T(8,128)(2,1)S(1)} collective-permute-done((bf16[32,640]{1,0:T(8,128)(2,1)S(1)}, bf16[32,640]{1,0:T(8,128)(2,1)S(1)}, u32[]{:S(2)}, u32[]{:S(2)}) %collective-permute-start.1) | collective-permute-done | bytes 40992 | tf_op jit(solution)/shard_map/ppermute | solution.py:629
  12.3 0.4 %collective-permute-done.refs_0_ = bf16[32,640]{1,0:T(8,128)(2,1)S(1)} collective-permute-done((bf16[32,640]{1,0:T(8,128)(2,1)S(1)}, bf16[32,640]{1,0:T(8,128)(2,1)S(1)}, u32[]{:S(2)}, u32[]{:S(2)}) %collective-permute-start) | collective-permute-done | bytes 40992 | tf_op jit(solution)/shard_map/ppermute | solution.py:629
  12.7 0.0 copy-done
  12.7 0.8 %shard_map.130 = (bf16[240,512]{1,0:T(8,128)(2,1)S(1)}, bf16[1024,1024]{1,0:T(8,128)(2,1)S(1)}, f32[2,32,8,256]{3,2,1,0:T(8,128)S(1)}, f32[2,32,8,128]{3,2,1,0:T(8,128)S(1)}, f32[2,32,8,128]{3,2,1,0:T(8,128)S(1)}) custom-call(bf16[32,640]{1,0:T(8,128)(2,1)S(1)} %shard_map.127.pack_ref.own_ref0, bf16[32,640]{1,0:T(8,128)(2,1)S(1)} %collective-permute-done.refs_0_, ...), custom_call_target="tpu_custom_call" | custom-call | tf_op jit(solution)/shard_map/pallas_call | solution.py:582
  13.6 0.3 %collective-permute-start.9 = (bf16[240,512]{1,0:T(8,128)(2,1)S(1)}, bf16[240,512]{1,0:T(8,128)(2,1)S(1)}, u32[]{:S(2)}, u32[]{:S(2)}) collective-permute-start(bf16[240,512]{1,0:T(8,128)(2,1)S(1)} %get-tuple-element.43.refs_0_), channel_id=1, source_target_pairs={{0,8},{1,9},{2,10},{3,11},{4,12},{5,13},{6,14},{7,15},{8,0},{9,1},... | collective-permute-start | bytes 737288 | tf_op jit(solution)/shard_map/ppermute | solution.py:629
  13.9 1.3 %collective-permute-start.7 = (bf16[104,512]{1,0:T(8,128)(2,1)S(1)}, bf16[104,512]{1,0:T(8,128)(2,1)S(1)}, u32[]{:S(2)}, u32[]{:S(2)}) collective-permute-start(bf16[104,512]{1,0:T(8,128)(2,1)S(1)} %shard_map.128.refs_3_), channel_id=1, source_target_pairs={{0,24},{1,25},{2,26},{3,27},{4,28},{5,29},{6,30},{7,31},{8,16},{9,... | collective-permute-start | bytes 319496 | tf_op jit(solution)/shard_map/ppermute | solution.py:629
  15.2 0.7 %collective-permute-start.6 = (bf16[104,512]{1,0:T(8,128)(2,1)S(1)}, bf16[104,512]{1,0:T(8,128)(2,1)S(1)}, u32[]{:S(2)}, u32[]{:S(2)}) collective-permute-start(bf16[104,512]{1,0:T(8,128)(2,1)S(1)} %shard_map.128.refs_3_), channel_id=1, source_target_pairs={{0,9},{1,8},{2,11},{3,10},{4,13},{5,12},{6,15},{7,14},{8,1},{9,0},... | collective-permute-start | bytes 319496 | tf_op jit(solution)/shard_map/ppermute | solution.py:629
  15.9 1.0 %collective-permute-start.8 = (bf16[104,512]{1,0:T(8,128)(2,1)S(1)}, bf16[104,512]{1,0:T(8,128)(2,1)S(1)}, u32[]{:S(2)}, u32[]{:S(2)}) collective-permute-start(bf16[104,512]{1,0:T(8,128)(2,1)S(1)} %shard_map.128.refs_3_), channel_id=1, source_target_pairs={{0,25},{1,24},{2,27},{3,26},{4,29},{5,28},{6,31},{7,30},{8,17},{9,... | collective-permute-start | bytes 319496 | tf_op jit(solution)/shard_map/ppermute | solution.py:629
  16.9 1.8 %collective-permute-done.7.refs_1_.refs_2_ = bf16[104,512]{1,0:T(8,128)(2,1)S(1)} collective-permute-done((bf16[104,512]{1,0:T(8,128)(2,1)S(1)}, bf16[104,512]{1,0:T(8,128)(2,1)S(1)}, u32[]{:S(2)}, u32[]{:S(2)}) %collective-permute-start.7) | collective-permute-done | bytes 106528 | tf_op jit(solution)/shard_map/ppermute | solution.py:629
  18.7 3.6 %collective-permute-done.6.refs_0_.refs_1_ = bf16[104,512]{1,0:T(8,128)(2,1)S(1)} collective-permute-done((bf16[104,512]{1,0:T(8,128)(2,1)S(1)}, bf16[104,512]{1,0:T(8,128)(2,1)S(1)}, u32[]{:S(2)}, u32[]{:S(2)}) %collective-permute-start.6) | collective-permute-done | bytes 106528 | tf_op jit(solution)/shard_map/ppermute | solution.py:629
  22.3 0.3 collective-permute-start.10
  22.6 0.2 collective-permute-start.11
  22.8 0.0 collective-permute-done.9.refs_2_.refs_4_
  22.8 1.5 %shard_map.131 = (bf16[1024,1024]{1,0:T(8,128)(2,1)S(1)}, f32[2,32,8,256]{3,2,1,0:T(8,128)S(1)}, f32[2,32,8,128]{3,2,1,0:T(8,128)S(1)}, f32[2,32,8,128]{3,2,1,0:T(8,128)S(1)}) custom-call(bf16[104,512]{1,0:T(8,128)(2,1)S(1)} %collective-permute-done.6.refs_0_.refs_1_, ...), custom_call_target="tpu_custom_call", output_to_operand_aliasing={{0}: (7, {}), {1}: (8, {}), {2}: (9, {}), {3}: (10, {})} | custom-call | tf_op jit(solution)/shard_map/pallas_call | solution.py:582
  24.4 0.0 collective-permute-done.8.refs_0_.refs_3_
  24.4 0.0 copy-start.1
  24.4 0.0 copy-start.2
  24.4 0.0 copy-start.3
  24.4 0.0 copy-start.4
  24.4 0.0 copy-start.5
  24.4 0.0 copy-start.6
  24.5 0.3 %collective-permute-start.12 = (bf16[104,512]{1,0:T(8,128)(2,1)S(1)}, bf16[104,512]{1,0:T(8,128)(2,1)S(1)}, u32[]{:S(2)}, u32[]{:S(2)}) collective-permute-start(bf16[104,512]{1,0:T(8,128)(2,1)S(1)} %collective-permute-done.8.refs_0_.refs_3_), channel_id=1, source_target_pairs={{0,8},{1,9},{2,10},{3,11},{4,12},{5,13},{6,14},{7,15},{8,0},{9,1},... | collective-permute-start | bytes 319496 | tf_op jit(solution)/shard_map/ppermute | solution.py:629
  24.8 0.0 collective-permute-done.10.refs_1_.refs_5_
  24.8 0.0 collective-permute-done.11.refs_2_.refs_6_
  24.8 1.3 %shard_map.132 = (bf16[1024,1024]{1,0:T(8,128)(2,1)S(1)}, f32[2,32,8,256]{3,2,1,0:T(8,128)S(1)}, f32[2,32,8,128]{3,2,1,0:T(8,128)S(1)}, f32[2,32,8,128]{3,2,1,0:T(8,128)S(1)}) custom-call(bf16[104,512]{1,0:T(8,128)(2,1)S(1)} %collective-permute-done.8.refs_0_.refs_3_, ...), custom_call_target="tpu_custom_call", output_to_operand_aliasing={{0}: (7, {}), {1}: (8, {}), {2}: (9, {}), {3}: (10, {})} | custom-call | tf_op jit(solution)/shard_map/pallas_call | solution.py:582
  26.1 0.0 collective-permute-done.12.refs_7_
  26.1 0.0 copy-done.1
  26.1 0.0 copy-done.2
  26.1 0.0 copy-done.3
  26.1 0.0 copy-done.4
  26.1 0.0 copy-done.5
  26.2 0.0 copy-done.6
  26.2 3.6 %shard_map.133 = (bf16[32,512]{1,0:T(8,128)(2,1)}, bf16[1024,1024]{1,0:T(8,128)(2,1)S(1)}) custom-call(s32[1,8]{1,0:T(1,128)S(1)} %copy-done.4, s32[1,8]{1,0:T(1,128)S(1)} %copy-done.5, s32[3,1,8]{2,1,0:T(1,128)S(1)} %copy-done.3, f32[3]{0:T(128)S(1)} %copy-done.6, bf16[240,512]{1,0:T(8,128)(2,1)S(1)} %get-tuple-element.43.refs_0_, ...), custom_call_target="tpu_custom_call", output_to_operand_aliasing={{1}: (20, {})} | custom-call | tf_op jit(solution)/shard_map/pallas_call | solution.py:582
Async XLA Ops:
  0.0 12.7 %copy-start = (bf16[512,1536]{1,0:T(8,128)(2,1)S(1)}, bf16[512,1536]{1,0:T(8,128)(2,1)}, u32[]{:S(2)}) copy-start(bf16[512,1536]{1,0:T(8,128)(2,1)} %refs_8_.1) | copy-start | bytes 4718596
  1.1 8.2 %collective-permute-start.5 = (bf16[32,640]{1,0:T(8,128)(2,1)S(1)}, bf16[32,640]{1,0:T(8,128)(2,1)S(1)}, u32[]{:S(2)}, u32[]{:S(2)}) collective-permute-start(bf16[32,640]{1,0:T(8,128)(2,1)S(1)} %shard_map.127.pack_ref.own_ref0), channel_id=1, source_target_pairs={{0,14},{1,15},{2,12},{3,13},{4,10},{5,11},{6,8},{7,9},{8,6},{9,7},... | collective-permute-start | bytes 122888 | tf_op jit(solution)/shard_map/ppermute | solution.py:629
  5.7 5.0 %collective-permute-start.4 = (bf16[32,640]{1,0:T(8,128)(2,1)S(1)}, bf16[32,640]{1,0:T(8,128)(2,1)S(1)}, u32[]{:S(2)}, u32[]{:S(2)}) collective-permute-start(bf16[32,640]{1,0:T(8,128)(2,1)S(1)} %shard_map.127.pack_ref.own_ref0), channel_id=1, source_target_pairs={{0,12},{1,13},{2,14},{3,15},{4,8},{5,9},{6,10},{7,11},{8,4},{9,5},... | collective-permute-start | bytes 122888 | tf_op jit(solution)/shard_map/ppermute | solution.py:629
  5.7 5.0 %collective-permute-start.3 = (bf16[32,640]{1,0:T(8,128)(2,1)S(1)}, bf16[32,640]{1,0:T(8,128)(2,1)S(1)}, u32[]{:S(2)}, u32[]{:S(2)}) collective-permute-start(bf16[32,640]{1,0:T(8,128)(2,1)S(1)} %shard_map.127.pack_ref.own_ref0), channel_id=1, source_target_pairs={{0,10},{1,11},{2,8},{3,9},{4,14},{5,15},{6,12},{7,13},{8,2},{9,3},... | collective-permute-start | bytes 122888 | tf_op jit(solution)/shard_map/ppermute | solution.py:629
  6.6 4.7 %collective-permute-start.2 = (bf16[32,640]{1,0:T(8,128)(2,1)S(1)}, bf16[32,640]{1,0:T(8,128)(2,1)S(1)}, u32[]{:S(2)}, u32[]{:S(2)}) collective-permute-start(bf16[32,640]{1,0:T(8,128)(2,1)S(1)} %shard_map.127.pack_ref.own_ref0), channel_id=1, source_target_pairs={{0,25},{1,24},{2,27},{3,26},{4,29},{5,28},{6,31},{7,30},{8,17},{9,... | collective-permute-start | bytes 122888 | tf_op jit(solution)/shard_map/ppermute | solution.py:629
  8.9 3.4 %collective-permute-start.1 = (bf16[32,640]{1,0:T(8,128)(2,1)S(1)}, bf16[32,640]{1,0:T(8,128)(2,1)S(1)}, u32[]{:S(2)}, u32[]{:S(2)}) collective-permute-start(bf16[32,640]{1,0:T(8,128)(2,1)S(1)} %shard_map.127.pack_ref.own_ref0), channel_id=1, source_target_pairs={{0,24},{1,25},{2,26},{3,27},{4,28},{5,29},{6,30},{7,31},{8,16},{9,... | collective-permute-start | bytes 122888 | tf_op jit(solution)/shard_map/ppermute | solution.py:629
  9.3 3.4 %collective-permute-start = (bf16[32,640]{1,0:T(8,128)(2,1)S(1)}, bf16[32,640]{1,0:T(8,128)(2,1)S(1)}, u32[]{:S(2)}, u32[]{:S(2)}) collective-permute-start(bf16[32,640]{1,0:T(8,128)(2,1)S(1)} %shard_map.127.pack_ref.own_ref0), channel_id=1, source_target_pairs={{0,9},{1,8},{2,11},{3,10},{4,13},{5,12},{6,15},{7,14},{8,1},{9,0},... | collective-permute-start | bytes 122888 | tf_op jit(solution)/shard_map/ppermute | solution.py:629
  13.6 9.3 %collective-permute-start.9 = (bf16[240,512]{1,0:T(8,128)(2,1)S(1)}, bf16[240,512]{1,0:T(8,128)(2,1)S(1)}, u32[]{:S(2)}, u32[]{:S(2)}) collective-permute-start(bf16[240,512]{1,0:T(8,128)(2,1)S(1)} %get-tuple-element.43.refs_0_), channel_id=1, source_target_pairs={{0,8},{1,9},{2,10},{3,11},{4,12},{5,13},{6,14},{7,15},{8,0},{9,1},... | collective-permute-start | bytes 737288 | tf_op jit(solution)/shard_map/ppermute | solution.py:629
  13.9 4.8 %collective-permute-start.7 = (bf16[104,512]{1,0:T(8,128)(2,1)S(1)}, bf16[104,512]{1,0:T(8,128)(2,1)S(1)}, u32[]{:S(2)}, u32[]{:S(2)}) collective-permute-start(bf16[104,512]{1,0:T(8,128)(2,1)S(1)} %shard_map.128.refs_3_), channel_id=1, source_target_pairs={{0,24},{1,25},{2,26},{3,27},{4,28},{5,29},{6,30},{7,31},{8,16},{9,... | collective-permute-start | bytes 319496 | tf_op jit(solution)/shard_map/ppermute | solution.py:629
  15.2 7.1 %collective-permute-start.6 = (bf16[104,512]{1,0:T(8,128)(2,1)S(1)}, bf16[104,512]{1,0:T(8,128)(2,1)S(1)}, u32[]{:S(2)}, u32[]{:S(2)}) collective-permute-start(bf16[104,512]{1,0:T(8,128)(2,1)S(1)} %shard_map.128.refs_3_), channel_id=1, source_target_pairs={{0,9},{1,8},{2,11},{3,10},{4,13},{5,12},{6,15},{7,14},{8,1},{9,0},... | collective-permute-start | bytes 319496 | tf_op jit(solution)/shard_map/ppermute | solution.py:629
  15.9 8.4 %collective-permute-start.8 = (bf16[104,512]{1,0:T(8,128)(2,1)S(1)}, bf16[104,512]{1,0:T(8,128)(2,1)S(1)}, u32[]{:S(2)}, u32[]{:S(2)}) collective-permute-start(bf16[104,512]{1,0:T(8,128)(2,1)S(1)} %shard_map.128.refs_3_), channel_id=1, source_target_pairs={{0,25},{1,24},{2,27},{3,26},{4,29},{5,28},{6,31},{7,30},{8,17},{9,... | collective-permute-start | bytes 319496 | tf_op jit(solution)/shard_map/ppermute | solution.py:629
  22.3 2.5 %collective-permute-start.10 = (bf16[104,512]{1,0:T(8,128)(2,1)S(1)}, bf16[104,512]{1,0:T(8,128)(2,1)S(1)}, u32[]{:S(2)}, u32[]{:S(2)}) collective-permute-start(bf16[104,512]{1,0:T(8,128)(2,1)S(1)} %collective-permute-done.6.refs_0_.refs_1_), channel_id=1, source_target_pairs={{0,8},{1,9},{2,10},{3,11},{4,12},{5,13},{6,14},{7,15},{8,0},{9,1},... | collective-permute-start | bytes 319496 | tf_op jit(solution)/shard_map/ppermute | solution.py:629
  22.6 2.2 %collective-permute-start.11 = (bf16[104,512]{1,0:T(8,128)(2,1)S(1)}, bf16[104,512]{1,0:T(8,128)(2,1)S(1)}, u32[]{:S(2)}, u32[]{:S(2)}) collective-permute-start(bf16[104,512]{1,0:T(8,128)(2,1)S(1)} %collective-permute-done.7.refs_1_.refs_2_), channel_id=1, source_target_pairs={{0,8},{1,9},{2,10},{3,11},{4,12},{5,13},{6,14},{7,15},{8,0},{9,1},... | collective-permute-start | bytes 319496 | tf_op jit(solution)/shard_map/ppermute | solution.py:629
  24.4 1.7 %copy-start.1 = (bf16[512,512]{1,0:T(8,128)(2,1)S(1)}, bf16[512,512]{1,0:T(8,128)(2,1)}, u32[]{:S(2)}) copy-start(bf16[512,512]{1,0:T(8,128)(2,1)} %refs_14_.1) | copy-start | bytes 1572868
  24.4 1.7 %copy-start.2 = (bf16[32,512]{1,0:T(8,128)(2,1)S(1)}, bf16[32,512]{1,0:T(8,128)(2,1)}, u32[]{:S(2)}) copy-start(bf16[32,512]{1,0:T(8,128)(2,1)} %refs_15_.1) | copy-start | bytes 98308
  24.4 1.7 %copy-start.3 = (s32[3,1,8]{2,1,0:T(1,128)S(1)}, s32[3,1,8]{2,1,0:T(1,128)}, u32[]{:S(2)}) copy-start(s32[3,1,8]{2,1,0:T(1,128)} %shift_ref.1) | copy-start | bytes 292
  24.4 1.7 %copy-start.4 = (s32[1,8]{1,0:T(1,128)S(1)}, s32[1,8]{1,0:T(1,128)}, u32[]{:S(2)}) copy-start(s32[1,8]{1,0:T(1,128)} %list_ref.1) | copy-start | bytes 100
  24.4 1.7 %copy-start.5 = (s32[1,8]{1,0:T(1,128)S(1)}, s32[1,8]{1,0:T(1,128)}, u32[]{:S(2)}) copy-start(s32[1,8]{1,0:T(1,128)} %valid_ref.1) | copy-start | bytes 100
  24.4 1.7 %copy-start.6 = (f32[3]{0:T(128)S(1)}, f32[3]{0:T(128)}, u32[]{:S(2)}) copy-start(f32[3]{0:T(128)} %cell_ref.1) | copy-start | bytes 40
  24.5 1.6 %collective-permute-start.12 = (bf16[104,512]{1,0:T(8,128)(2,1)S(1)}, bf16[104,512]{1,0:T(8,128)(2,1)S(1)}, u32[]{:S(2)}, u32[]{:S(2)}) collective-permute-start(bf16[104,512]{1,0:T(8,128)(2,1)S(1)} %collective-permute-done.8.refs_0_.refs_3_), channel_id=1, source_target_pairs={{0,8},{1,9},{2,10},{3,11},{4,12},{5,13},{6,14},{7,15},{8,0},{9,1},... | collective-permute-start | bytes 319496 | tf_op jit(solution)/shard_map/ppermute | solution.py:629

commit v6 on v5

--- a/solution.py
+++ b/solution.py
@@ -255,8 +255,11 @@
         copy.wait()
 
 
-def pack_kernel(feat_hbm, gain_hbm, pos_hbm, out_ref, feat_ref, gain_ref, pos_ref, tmp_ref, sems):
-    settle(fetch(((feat_hbm, feat_ref), (gain_hbm, gain_ref), (pos_hbm, pos_ref)), sems))
+def pack_kernel(*refs):
+    sources, out_ref, tables = refs[:7], refs[7], refs[8:12]
+    feat_ref, gain_ref, pos_ref, tmp_ref, sems = refs[12:]
+    copies = fetch(list(zip(sources, (feat_ref, gain_ref, pos_ref, *tables))), sems)
+    settle(copies[:3])
     atoms, dim = feat_ref.shape
     floats = feat_ref[...].astype(jnp.float32)
     spread = jnp.mean(floats * floats, axis=-1, keepdims=True)
@@ -268,40 +271,25 @@
     eye = unit(atoms, atoms, jnp.bfloat16)
     turned = mm(eye, tmp_ref[...].astype(jnp.bfloat16), ((1,), (1,)))
     out_ref[:, dim:] = turned.astype(jnp.bfloat16)
-
-
-def query_kernel(
+    settle(copies[3:])
+
+
+def prepare(
     head_dim,
-    wqkv_hbm,
-    rw_hbm,
-    ro_hbm,
-    pw_hbm,
-    cs_hbm,
+    wqkv_ref,
+    rw_ref,
+    ro_ref,
+    pw_ref,
+    cs_ref,
     pack_ref,
     qexp_ref,
     w1_ref,
     w2_ref,
     str_ref,
     own_ref,
-    wq_ref,
-    rw_ref,
-    ro_ref,
-    pw_ref,
-    cs_ref,
-    sems,
 ):
     atoms = pack_ref.shape[0]
-    dim = wq_ref.shape[0]
-    copies = fetch(
-        (
-            (wqkv_hbm.at[:, pl.ds(0, dim)], wq_ref),
-            (rw_hbm, rw_ref),
-            (ro_hbm, ro_ref),
-            (pw_hbm, pw_ref),
-            (cs_hbm, cs_ref),
-        ),
-        sems,
-    )
+    dim = wqkv_ref.shape[0]
     groups, rows, width = qexp_ref.shape
     per = rows // atoms
     pos = pack_ref[:, dim:].astype(jnp.float32)
@@ -309,7 +297,6 @@
     own_ref[0] = pos
     own_ref[1] = jnp.cos(two_pi * pos)
     own_ref[2] = jnp.sin(two_pi * pos)
-    settle(copies[1:])
     h, m, l = parts_of(0.5 * rw_ref[...], 3)
     hidden = rw_ref.shape[1]
     row = lax.broadcasted_iota(jnp.int32, (16, hidden), 0)
@@ -321,8 +308,7 @@
     h, l = parts_of(pw_ref[...], 2)
     w2_ref[...] = jnp.concatenate([h, h, l], axis=1)
     str_ref[...] = jnp.broadcast_to(to_column(cs_ref[...]), str_ref.shape)
-    settle(copies[:1])
-    q = mm(pack_ref[:, :dim], wq_ref[...], ((1,), (0,)))
+    q = mm(pack_ref[:, :dim], wqkv_ref[:, :dim], ((1,), (0,)))
     q = q.astype(jnp.bfloat16).astype(jnp.float32)
     lane = lax.broadcasted_iota(jnp.int32, (per, width), 1) // head_dim
     sub = lax.broadcasted_iota(jnp.int32, (per, width), 0)
@@ -349,7 +335,7 @@
     return jnp.concatenate(out, axis=1).astype(jnp.bfloat16)
 
 
-def repack_kernel(*refs):
+def repack_kernel(_, *refs):
     blocks, out_ref = refs[:-1], refs[-1]
     atoms = blocks[0].shape[0]
     dim = out_ref.shape[1]
@@ -424,10 +410,12 @@
     return jnp.concatenate([array] * (lanes // array.shape[-1]), axis=-1)
 
 
-def first_kernel(head_dim, plan, own_ref0, *refs):
-    blocks = (own_ref0,) + refs[:3]
-    ring_ref, wqkv_ref, qexp_ref, str_ref, own_ref = refs[3:8]
-    core_ref, kv_ref, acc_ref, top_ref, sum_ref = refs[8:]
+def first_kernel(head_dim, plan, *refs):
+    blocks, ring_ref, wqkv_ref, tables = refs[:4], refs[4], refs[5], refs[6:10]
+    core_ref, kv_ref, acc_ref, top_ref, sum_ref, qexp_ref, w1_ref, w2_ref, str_ref, own_ref = refs[10:]
+    prepare(
+        head_dim, wqkv_ref, *tables, blocks[0], qexp_ref, w1_ref, w2_ref, str_ref, own_ref
+    )
     atoms = own_ref.shape[1]
     dim = wqkv_ref.shape[0]
     four, three = plan[0][1]
@@ -465,10 +453,10 @@
         sum_ref[g] = summed
 
 
-def chosen(scalars, lane):
-    out = jnp.full(lane.shape, scalars[0])
-    for e in range(1, len(scalars)):
-        out = jnp.where(lane == e, scalars[e], out)
+def chosen(row, lane):
+    out = jnp.broadcast_to(row[:, :1], lane.shape)
+    for e in range(1, row.shape[1]):
+        out = jnp.where(lane == e, row[:, e : e + 1], out)
     return out
 
 
@@ -511,7 +499,7 @@
     in_tile = lax.broadcasted_iota(jnp.int32, (1, 128), 1) // atoms
     tiles = []
     for e in range(entries):
-        slot, tile, spot = locate(list_ref[0, e] ^ me)
+        slot, tile, spot = locate(jnp.sum(list_ref[:, e : e + 1]) ^ me)
         start = pl.multiple_of(slot * atoms, atoms)
         near_ref[e * atoms : (e + 1) * atoms, :] = kv_ref[pl.ds(start, atoms), :]
         into = e % a_tile
@@ -523,8 +511,8 @@
     near = jnp.concatenate(tiles, axis=1)
     square = None
     for c in range(3):
-        at = near[c : c + 1] + chosen([shift_ref[c, 0, e] for e in range(entries)], lane).astype(jnp.float32)
-        gap = (at - own_ref[0, :, c : c + 1]) * cell_ref[c]
+        at = near[c : c + 1] + chosen(shift_ref[c].astype(jnp.float32), lane)
+        gap = (at - own_ref[0, :, c : c + 1]) * cell_ref[:, c : c + 1]
         square = gap * gap if square is None else square + gap * gap
     dist = jnp.sqrt(square + 0.25)
     nrbf = (w1_ref.shape[1] - 16) // 6
@@ -543,8 +531,7 @@
         for j in range(step):
             for g in range(groups):
                 bias_ref[g, i + j] = pair[g * per : (g + 1) * per, j * listed : (j + 1) * listed]
-    lane3 = lax.broadcasted_iota(jnp.int32, (1, 1, listed), 2) // atoms
-    live = chosen([valid_ref[0, e] for e in range(entries)], lane3) > 0
+    live = (chosen(valid_ref[...], lane) > 0)[None]
     block = lax.broadcasted_iota(jnp.int32, (1, per, width), 2) // head_dim
     keep = block == lax.broadcasted_iota(jnp.int32, (1, per, width), 1)
     pieces = []
@@ -640,48 +627,27 @@
         return slot, tile, spot
 
     tied = lax.optimization_barrier
-    pack = call(
+    tables = (rbf_weight, rbf_offset[None], pair_weight.T, cosine_scale[None])
+    pack, *tables = call(
         pack_kernel,
-        vm((atoms, dim + 128), bf16),
+        [vm((atoms, dim + 128), bf16)] + [vm(table.shape, f32) for table in tables],
         [
             vm((atoms, dim), bf16),
             vm((1, dim), f32),
             vm(positions.shape, f32),
             vm((128, atoms), f32),
-            pltpu.SemaphoreType.DMA((3,)),
+            pltpu.SemaphoreType.DMA((7,)),
         ],
         0,
-        (features, norm_gain[None], positions),
-        hbm=3,
+        (features, norm_gain[None], positions, *tables),
+        hbm=7,
     )
     across_masks = {"e": 1 | flip, "n": (1 << across_bits[1]) | flip}
     across_masks["d"] = 1 | across_masks["n"]
     ups = [swap(pack, (d << 1) | flip) for d in (1, 2, 3)]
     owns = [swap(pack, mask) for mask in across_masks.values()]
-    ready = call(
-        functools.partial(query_kernel, head_dim),
-        [
-            vm((groups, rows, width), bf16),
-            vm((hidden, 6 * nrbf + 16), bf16),
-            vm((heads, 3 * hidden), bf16),
-            vm((heads, 128), f32),
-            vm((3, atoms, 128), f32),
-        ],
-        [
-            vm((dim, dim), bf16),
-            vm((nrbf, hidden), f32),
-            vm((1, hidden), f32),
-            vm((heads, hidden), f32),
-            vm((1, heads), f32),
-            pltpu.SemaphoreType.DMA((5,)),
-        ],
-        0,
-        (w_qkv, rbf_weight, rbf_offset[None], pair_weight.T, cosine_scale[None], pack),
-        hbm=5,
-    )
-    qexp, w1, w2, strength, own = ready
     four, three = 4 * atoms, 3 * atoms
-    ring = call(repack_kernel, vm((three + 8, dim), bf16), [], 0, tuple(ups))
+    ring = call(repack_kernel, vm((three + 8, dim), bf16), [], 0, (w_qkv, *ups), hbm=1)
     east, north, diag = [swap(ring, mask) for mask in across_masks.values()]
     state_shapes = [
         vm((total * atoms, 2 * dim), bf16),
@@ -689,18 +655,27 @@
         vm((groups, atoms, per, 128), f32),
         vm((groups, atoms, per, 128), f32),
     ]
-    common = (w_qkv, qexp, strength, own)
     half = total // 2 * atoms
     plan = [(0, (four, three))] + [(four + k * three, (three,)) for k in (1, 2, 3)]
     plan += [(half + start, counts) for start, counts in plan]
 
-    core, *state = call(
+    core, kv, acc, top, summed, qexp, w1, w2, strength, own = call(
         functools.partial(first_kernel, head_dim, plan[:1]),
-        [vm((four + three + 16, dim), bf16)] + state_shapes,
+        [vm((four + three + 16, dim), bf16)]
+        + state_shapes
+        + [
+            vm((groups, rows, width), bf16),
+            vm((hidden, 6 * nrbf + 16), bf16),
+            vm((heads, 3 * hidden), bf16),
+            vm((heads, 128), f32),
+            vm((3, atoms, 128), f32),
+        ],
         [],
         0,
-        (pack, *owns, ring, *common),
-    )
+        (pack, *owns, ring, w_qkv, *tables),
+    )
+    state = (kv, acc, top, summed)
+    common = (w_qkv, qexp, strength, own)
 
     def step(places, pieces, state):
         at = len(pieces) + len(common)
@@ -729,12 +704,12 @@
             vm((10, 8, 128), f32),
             vm((groups, atoms, per, entries * atoms), f32),
         ],
-        4,
+        0,
         (
             block_lists,
             block_valid,
             image_offsets,
-            cell_lengths,
+            cell_lengths[None],
             core,
             east,
             north,

time: 29.9 us -> 29.6 us (0.990)
  Pallas kernels: 9.82 us -> 8.17 us
  waiting for transfers between devices: 7.29 us -> 8.66 us
    pallas_call x7 -> x6, Pallas kernels: 9.82 us -> 8.17 us  [call(): pl.pallas_call(kernel, out_shape=outs, in_specs=specs, out_specs=[vmem] *...]
    ppermute x13, waiting for transfers between devices: 7.29 us -> 8.66 us  [swap(): return lax.ppermute(array, axes, [(i, i ^ mask) for i in range(total)])]
  transfers between devices with their start and end apart: 13 -> 13, of which waited for: 5 -> 6; matrix products, arithmetic and copies ran while one was open for 0% -> 0% of each run, Pallas kernels for 14% -> 10%
where the time goes in v6:
time: 29.6 us; the launch traced here: 29.5 us
  starting transfers between devices  12.5 us (42%)
  waiting for transfers between devices  8.66 us (29%)
  Pallas kernels  8.17 us (28%)
    ppermute x13, starting transfers between devices, swap(): return lax.ppermute(array, axes, [(i, i ^ mask) for i in range(total)])  12.5 us
    ppermute x13, waiting for transfers between devices, swap(): return lax.ppermute(array, axes, [(i, i ^ mask) for i in range(total)])  8.66 us
    pallas_call x6, Pallas kernels, call(): pl.pallas_call(kernel, out_shape=outs, in_specs=specs, out_specs=[vmem] *...  8.17 us
  transfers between devices with their start and end apart: 13, of which 6 were waited for; matrix products, arithmetic and copies ran while one was open for 0% of the time, Pallas kernels for 10%

profile of v6, /device:TPU:0, one launch (start us, length us, event | category | flops | bytes accessed | tf_op | source)
XLA Modules:
  0.0 29.5 jit_solution(6775150723231841995)
XLA Ops:
  0.0 0.0 copy-start
  0.0 1.1 %shard_map.127 = (bf16[32,640]{1,0:T(8,128)(2,1)S(1)}, f32[16,64]{1,0:T(8,128)S(1)}, f32[1,64]{1,0:T(1,128)S(1)}, f32[16,64]{1,0:T(8,128)S(1)}, f32[1,16]{1,0:T(1,128)S(1)}) custom-call(bf16[32,512]{1,0:T(8,128)(2,1)} %refs_15_.1, f32[1,512]{1,0:T(1,128)} %bitcast.7, f32[3,32]{1,0:T(4,128)} %refs_2_.1, f32[16,64]{1,0:T(8,128)} %refs_3_.3, f32[1,64]{1,0:T(1,128)} %bitcast.8, ...), custom_call_target="tpu_custom_call" | custom-call | tf_op jit(solution)/shard_map/pallas_call | solution.py:569
  1.1 4.6 %collective-permute-start.5 = (bf16[32,640]{1,0:T(8,128)(2,1)S(1)}, bf16[32,640]{1,0:T(8,128)(2,1)S(1)}, u32[]{:S(2)}, u32[]{:S(2)}) collective-permute-start(bf16[32,640]{1,0:T(8,128)(2,1)S(1)} %get-tuple-element.45.refs_0_), channel_id=1, source_target_pairs={{0,14},{1,15},{2,12},{3,13},{4,10},{5,11},{6,8},{7,9},{8,6},{9,7},... | collective-permute-start | bytes 122888 | tf_op jit(solution)/shard_map/ppermute | solution.py:616
  5.7 0.0 collective-permute-start.4
  5.7 0.9 %collective-permute-start.3 = (bf16[32,640]{1,0:T(8,128)(2,1)S(1)}, bf16[32,640]{1,0:T(8,128)(2,1)S(1)}, u32[]{:S(2)}, u32[]{:S(2)}) collective-permute-start(bf16[32,640]{1,0:T(8,128)(2,1)S(1)} %get-tuple-element.45.refs_0_), channel_id=1, source_target_pairs={{0,10},{1,11},{2,8},{3,9},{4,14},{5,15},{6,12},{7,13},{8,2},{9,3},... | collective-permute-start | bytes 122888 | tf_op jit(solution)/shard_map/ppermute | solution.py:616
  6.6 2.3 %collective-permute-start.2 = (bf16[32,640]{1,0:T(8,128)(2,1)S(1)}, bf16[32,640]{1,0:T(8,128)(2,1)S(1)}, u32[]{:S(2)}, u32[]{:S(2)}) collective-permute-start(bf16[32,640]{1,0:T(8,128)(2,1)S(1)} %get-tuple-element.45.refs_0_), channel_id=1, source_target_pairs={{0,25},{1,24},{2,27},{3,26},{4,29},{5,28},{6,31},{7,30},{8,17},{9,... | collective-permute-start | bytes 122888 | tf_op jit(solution)/shard_map/ppermute | solution.py:616
  8.9 0.4 %collective-permute-start.1 = (bf16[32,640]{1,0:T(8,128)(2,1)S(1)}, bf16[32,640]{1,0:T(8,128)(2,1)S(1)}, u32[]{:S(2)}, u32[]{:S(2)}) collective-permute-start(bf16[32,640]{1,0:T(8,128)(2,1)S(1)} %get-tuple-element.45.refs_0_), channel_id=1, source_target_pairs={{0,24},{1,25},{2,26},{3,27},{4,28},{5,29},{6,30},{7,31},{8,16},{9,... | collective-permute-start | bytes 122888 | tf_op jit(solution)/shard_map/ppermute | solution.py:616
  9.3 0.0 collective-permute-done.5.refs_2_
  9.3 0.0 collective-permute-start
  9.4 1.0 %collective-permute-done.4.refs_1_ = bf16[32,640]{1,0:T(8,128)(2,1)S(1)} collective-permute-done((bf16[32,640]{1,0:T(8,128)(2,1)S(1)}, bf16[32,640]{1,0:T(8,128)(2,1)S(1)}, u32[]{:S(2)}, u32[]{:S(2)}) %collective-permute-start.4) | collective-permute-done | bytes 40992 | tf_op jit(solution)/shard_map/ppermute | solution.py:616
  10.4 0.0 collective-permute-done.3.refs_0_
  10.4 0.1 shard_map.128.refs_4_
  10.6 0.7 %collective-permute-done.2.refs_3_ = bf16[32,640]{1,0:T(8,128)(2,1)S(1)} collective-permute-done((bf16[32,640]{1,0:T(8,128)(2,1)S(1)}, bf16[32,640]{1,0:T(8,128)(2,1)S(1)}, u32[]{:S(2)}, u32[]{:S(2)}) %collective-permute-start.2) | collective-permute-done | bytes 40992 | tf_op jit(solution)/shard_map/ppermute | solution.py:616
  11.3 1.1 %collective-permute-done.1.refs_2_ = bf16[32,640]{1,0:T(8,128)(2,1)S(1)} collective-permute-done((bf16[32,640]{1,0:T(8,128)(2,1)S(1)}, bf16[32,640]{1,0:T(8,128)(2,1)S(1)}, u32[]{:S(2)}, u32[]{:S(2)}) %collective-permute-start.1) | collective-permute-done | bytes 40992 | tf_op jit(solution)/shard_map/ppermute | solution.py:616
  12.4 0.4 %collective-permute-done.refs_1_ = bf16[32,640]{1,0:T(8,128)(2,1)S(1)} collective-permute-done((bf16[32,640]{1,0:T(8,128)(2,1)S(1)}, bf16[32,640]{1,0:T(8,128)(2,1)S(1)}, u32[]{:S(2)}, u32[]{:S(2)}) %collective-permute-start) | collective-permute-done | bytes 40992 | tf_op jit(solution)/shard_map/ppermute | solution.py:616
  12.8 0.0 copy-done
  12.8 1.0 %shard_map.129 = (bf16[240,512]{1,0:T(8,128)(2,1)S(1)}, bf16[1024,1024]{1,0:T(8,128)(2,1)S(1)}, f32[2,32,8,256]{3,2,1,0:T(8,128)S(1)}, f32[2,32,8,128]{3,2,1,0:T...) custom-call(bf16[32,640]{1,0:T(8,128)(2,1)S(1)} %get-tuple-element.4, ...), custom_call_target="tpu_custom_call" | custom-call | tf_op jit(solution)/shard_map/pallas_call | solution.py:569
  13.8 0.3 %collective-permute-start.9 = (bf16[240,512]{1,0:T(8,128)(2,1)S(1)}, bf16[240,512]{1,0:T(8,128)(2,1)S(1)}, u32[]{:S(2)}, u32[]{:S(2)}) collective-permute-start(bf16[240,512]{1,0:T(8,128)(2,1)S(1)} %get-tuple-element.50.refs_0_), channel_id=1, source_target_pairs={{0,8},{1,9},{2,10},{3,11},{4,12},{5,13},{6,14},{7,15},{8,0},{9,1},... | collective-permute-start | bytes 737288 | tf_op jit(solution)/shard_map/ppermute | solution.py:616
  14.1 1.3 %collective-permute-start.7 = (bf16[104,512]{1,0:T(8,128)(2,1)S(1)}, bf16[104,512]{1,0:T(8,128)(2,1)S(1)}, u32[]{:S(2)}, u32[]{:S(2)}) collective-permute-start(bf16[104,512]{1,0:T(8,128)(2,1)S(1)} %shard_map.128.refs_4_), channel_id=1, source_target_pairs={{0,24},{1,25},{2,26},{3,27},{4,28},{5,29},{6,30},{7,31},{8,16},{9,... | collective-permute-start | bytes 319496 | tf_op jit(solution)/shard_map/ppermute | solution.py:616
  15.4 0.7 %collective-permute-start.6 = (bf16[104,512]{1,0:T(8,128)(2,1)S(1)}, bf16[104,512]{1,0:T(8,128)(2,1)S(1)}, u32[]{:S(2)}, u32[]{:S(2)}) collective-permute-start(bf16[104,512]{1,0:T(8,128)(2,1)S(1)} %shard_map.128.refs_4_), channel_id=1, source_target_pairs={{0,9},{1,8},{2,11},{3,10},{4,13},{5,12},{6,15},{7,14},{8,1},{9,0},... | collective-permute-start | bytes 319496 | tf_op jit(solution)/shard_map/ppermute | solution.py:616
  16.1 1.0 %collective-permute-start.8 = (bf16[104,512]{1,0:T(8,128)(2,1)S(1)}, bf16[104,512]{1,0:T(8,128)(2,1)S(1)}, u32[]{:S(2)}, u32[]{:S(2)}) collective-permute-start(bf16[104,512]{1,0:T(8,128)(2,1)S(1)} %shard_map.128.refs_4_), channel_id=1, source_target_pairs={{0,25},{1,24},{2,27},{3,26},{4,29},{5,28},{6,31},{7,30},{8,17},{9,... | collective-permute-start | bytes 319496 | tf_op jit(solution)/shard_map/ppermute | solution.py:616
  17.2 1.8 %collective-permute-done.7.refs_1_.refs_2_ = bf16[104,512]{1,0:T(8,128)(2,1)S(1)} collective-permute-done((bf16[104,512]{1,0:T(8,128)(2,1)S(1)}, bf16[104,512]{1,0:T(8,128)(2,1)S(1)}, u32[]{:S(2)}, u32[]{:S(2)}) %collective-permute-start.7) | collective-permute-done | bytes 106528 | tf_op jit(solution)/shard_map/ppermute | solution.py:616
  18.9 3.6 %collective-permute-done.6.refs_0_.refs_1_ = bf16[104,512]{1,0:T(8,128)(2,1)S(1)} collective-permute-done((bf16[104,512]{1,0:T(8,128)(2,1)S(1)}, bf16[104,512]{1,0:T(8,128)(2,1)S(1)}, u32[]{:S(2)}, u32[]{:S(2)}) %collective-permute-start.6) | collective-permute-done | bytes 106528 | tf_op jit(solution)/shard_map/ppermute | solution.py:616
  22.6 0.3 collective-permute-start.10
  22.8 0.3 collective-permute-start.11
  23.1 0.0 collective-permute-done.9.refs_2_.refs_4_
  23.1 1.5 %shard_map.130 = (bf16[1024,1024]{1,0:T(8,128)(2,1)S(1)}, f32[2,32,8,256]{3,2,1,0:T(8,128)S(1)}, f32[2,32,8,128]{3,2,1,0:T(8,128)S(1)}, f32[2,32,8,128]{3,2,1,0:T(8,128)S(1)}) custom-call(bf16[104,512]{1,0:T(8,128)(2,1)S(1)} %collective-permute-done.6.refs_0_.refs_1_, ...), custom_call_target="tpu_custom_call", output_to_operand_aliasing={{0}: (7, {}), {1}: (8, {}), {2}: (9, {}), {3}: (10, {})} | custom-call | tf_op jit(solution)/shard_map/pallas_call | solution.py:569
  24.6 0.0 collective-permute-done.8.refs_0_.refs_3_
  24.6 0.0 copy-start.1
  24.6 0.0 copy-start.2
  24.6 0.0 copy-start.3
  24.6 0.0 copy-start.4
  24.6 0.0 copy-start.5
  24.7 0.0 copy-start.6
  24.7 0.3 %collective-permute-start.12 = (bf16[104,512]{1,0:T(8,128)(2,1)S(1)}, bf16[104,512]{1,0:T(8,128)(2,1)S(1)}, u32[]{:S(2)}, u32[]{:S(2)}) collective-permute-start(bf16[104,512]{1,0:T(8,128)(2,1)S(1)} %collective-permute-done.8.refs_0_.refs_3_), channel_id=1, source_target_pairs={{0,8},{1,9},{2,10},{3,11},{4,12},{5,13},{6,14},{7,15},{8,0},{9,1},... | collective-permute-start | bytes 319496 | tf_op jit(solution)/shard_map/ppermute | solution.py:616
  25.0 0.0 collective-permute-done.10.refs_1_.refs_5_
  25.0 0.0 collective-permute-done.11.refs_2_.refs_6_
  25.0 1.3 %shard_map.131 = (bf16[1024,1024]{1,0:T(8,128)(2,1)S(1)}, f32[2,32,8,256]{3,2,1,0:T(8,128)S(1)}, f32[2,32,8,128]{3,2,1,0:T(8,128)S(1)}, f32[2,32,8,128]{3,2,1,0:T(8,128)S(1)}) custom-call(bf16[104,512]{1,0:T(8,128)(2,1)S(1)} %collective-permute-done.8.refs_0_.refs_3_, ...), custom_call_target="tpu_custom_call", output_to_operand_aliasing={{0}: (7, {}), {1}: (8, {}), {2}: (9, {}), {3}: (10, {})} | custom-call | tf_op jit(solution)/shard_map/pallas_call | solution.py:569
  26.3 0.0 collective-permute-done.12.refs_7_
  26.3 0.0 copy-done.1
  26.3 0.0 copy-done.2
  26.3 0.0 copy-done.3
  26.3 0.0 copy-done.4
  26.4 0.0 copy-done.5
  26.4 0.0 copy-done.6
  26.4 3.1 %shard_map.132 = (bf16[32,512]{1,0:T(8,128)(2,1)}, bf16[1024,1024]{1,0:T(8,128)(2,1)S(1)}) custom-call(s32[1,8]{1,0:T(1,128)S(1)} %copy-done.4, s32[1,8]{1,0:T(1,128)S(1)} %copy-done.5, s32[3,1,8]{2,1,0:T(1,128)S(1)} %copy-done.3, f32[1,3]{1,0:T(1,128)S(1)} %bitcast.5, ...), custom_call_target="tpu_custom_call", output_to_operand_aliasing={{1}: (20, {})} | custom-call | tf_op jit(solution)/shard_map/pallas_call | solution.py:569
Async XLA Ops:
  0.0 12.8 %copy-start = (bf16[512,1536]{1,0:T(8,128)(2,1)S(1)}, bf16[512,1536]{1,0:T(8,128)(2,1)}, u32[]{:S(2)}) copy-start(bf16[512,1536]{1,0:T(8,128)(2,1)} %refs_8_.1) | copy-start | bytes 4718596
  1.1 8.2 %collective-permute-start.5 = (bf16[32,640]{1,0:T(8,128)(2,1)S(1)}, bf16[32,640]{1,0:T(8,128)(2,1)S(1)}, u32[]{:S(2)}, u32[]{:S(2)}) collective-permute-start(bf16[32,640]{1,0:T(8,128)(2,1)S(1)} %get-tuple-element.45.refs_0_), channel_id=1, source_target_pairs={{0,14},{1,15},{2,12},{3,13},{4,10},{5,11},{6,8},{7,9},{8,6},{9,7},... | collective-permute-start | bytes 122888 | tf_op jit(solution)/shard_map/ppermute | solution.py:616
  5.7 4.7 %collective-permute-start.4 = (bf16[32,640]{1,0:T(8,128)(2,1)S(1)}, bf16[32,640]{1,0:T(8,128)(2,1)S(1)}, u32[]{:S(2)}, u32[]{:S(2)}) collective-permute-start(bf16[32,640]{1,0:T(8,128)(2,1)S(1)} %get-tuple-element.45.refs_0_), channel_id=1, source_target_pairs={{0,12},{1,13},{2,14},{3,15},{4,8},{5,9},{6,10},{7,11},{8,4},{9,5},... | collective-permute-start | bytes 122888 | tf_op jit(solution)/shard_map/ppermute | solution.py:616
  5.7 4.7 %collective-permute-start.3 = (bf16[32,640]{1,0:T(8,128)(2,1)S(1)}, bf16[32,640]{1,0:T(8,128)(2,1)S(1)}, u32[]{:S(2)}, u32[]{:S(2)}) collective-permute-start(bf16[32,640]{1,0:T(8,128)(2,1)S(1)} %get-tuple-element.45.refs_0_), channel_id=1, source_target_pairs={{0,10},{1,11},{2,8},{3,9},{4,14},{5,15},{6,12},{7,13},{8,2},{9,3},... | collective-permute-start | bytes 122888 | tf_op jit(solution)/shard_map/ppermute | solution.py:616
  6.6 4.7 %collective-permute-start.2 = (bf16[32,640]{1,0:T(8,128)(2,1)S(1)}, bf16[32,640]{1,0:T(8,128)(2,1)S(1)}, u32[]{:S(2)}, u32[]{:S(2)}) collective-permute-start(bf16[32,640]{1,0:T(8,128)(2,1)S(1)} %get-tuple-element.45.refs_0_), channel_id=1, source_target_pairs={{0,25},{1,24},{2,27},{3,26},{4,29},{5,28},{6,31},{7,30},{8,17},{9,... | collective-permute-start | bytes 122888 | tf_op jit(solution)/shard_map/ppermute | solution.py:616
  8.9 3.4 %collective-permute-start.1 = (bf16[32,640]{1,0:T(8,128)(2,1)S(1)}, bf16[32,640]{1,0:T(8,128)(2,1)S(1)}, u32[]{:S(2)}, u32[]{:S(2)}) collective-permute-start(bf16[32,640]{1,0:T(8,128)(2,1)S(1)} %get-tuple-element.45.refs_0_), channel_id=1, source_target_pairs={{0,24},{1,25},{2,26},{3,27},{4,28},{5,29},{6,30},{7,31},{8,16},{9,... | collective-permute-start | bytes 122888 | tf_op jit(solution)/shard_map/ppermute | solution.py:616
  9.3 3.4 %collective-permute-start = (bf16[32,640]{1,0:T(8,128)(2,1)S(1)}, bf16[32,640]{1,0:T(8,128)(2,1)S(1)}, u32[]{:S(2)}, u32[]{:S(2)}) collective-permute-start(bf16[32,640]{1,0:T(8,128)(2,1)S(1)} %get-tuple-element.45.refs_0_), channel_id=1, source_target_pairs={{0,9},{1,8},{2,11},{3,10},{4,13},{5,12},{6,15},{7,14},{8,1},{9,0},... | collective-permute-start | bytes 122888 | tf_op jit(solution)/shard_map/ppermute | solution.py:616
  13.8 9.3 %collective-permute-start.9 = (bf16[240,512]{1,0:T(8,128)(2,1)S(1)}, bf16[240,512]{1,0:T(8,128)(2,1)S(1)}, u32[]{:S(2)}, u32[]{:S(2)}) collective-permute-start(bf16[240,512]{1,0:T(8,128)(2,1)S(1)} %get-tuple-element.50.refs_0_), channel_id=1, source_target_pairs={{0,8},{1,9},{2,10},{3,11},{4,12},{5,13},{6,14},{7,15},{8,0},{9,1},... | collective-permute-start | bytes 737288 | tf_op jit(solution)/shard_map/ppermute | solution.py:616
  14.1 4.8 %collective-permute-start.7 = (bf16[104,512]{1,0:T(8,128)(2,1)S(1)}, bf16[104,512]{1,0:T(8,128)(2,1)S(1)}, u32[]{:S(2)}, u32[]{:S(2)}) collective-permute-start(bf16[104,512]{1,0:T(8,128)(2,1)S(1)} %shard_map.128.refs_4_), channel_id=1, source_target_pairs={{0,24},{1,25},{2,26},{3,27},{4,28},{5,29},{6,30},{7,31},{8,16},{9,... | collective-permute-start | bytes 319496 | tf_op jit(solution)/shard_map/ppermute | solution.py:616
  15.4 7.1 %collective-permute-start.6 = (bf16[104,512]{1,0:T(8,128)(2,1)S(1)}, bf16[104,512]{1,0:T(8,128)(2,1)S(1)}, u32[]{:S(2)}, u32[]{:S(2)}) collective-permute-start(bf16[104,512]{1,0:T(8,128)(2,1)S(1)} %shard_map.128.refs_4_), channel_id=1, source_target_pairs={{0,9},{1,8},{2,11},{3,10},{4,13},{5,12},{6,15},{7,14},{8,1},{9,0},... | collective-permute-start | bytes 319496 | tf_op jit(solution)/shard_map/ppermute | solution.py:616
  16.1 8.4 %collective-permute-start.8 = (bf16[104,512]{1,0:T(8,128)(2,1)S(1)}, bf16[104,512]{1,0:T(8,128)(2,1)S(1)}, u32[]{:S(2)}, u32[]{:S(2)}) collective-permute-start(bf16[104,512]{1,0:T(8,128)(2,1)S(1)} %shard_map.128.refs_4_), channel_id=1, source_target_pairs={{0,25},{1,24},{2,27},{3,26},{4,29},{5,28},{6,31},{7,30},{8,17},{9,... | collective-permute-start | bytes 319496 | tf_op jit(solution)/shard_map/ppermute | solution.py:616
  22.6 2.4 %collective-permute-start.10 = (bf16[104,512]{1,0:T(8,128)(2,1)S(1)}, bf16[104,512]{1,0:T(8,128)(2,1)S(1)}, u32[]{:S(2)}, u32[]{:S(2)}) collective-permute-start(bf16[104,512]{1,0:T(8,128)(2,1)S(1)} %collective-permute-done.6.refs_0_.refs_1_), channel_id=1, source_target_pairs={{0,8},{1,9},{2,10},{3,11},{4,12},{5,13},{6,14},{7,15},{8,0},{9,1},... | collective-permute-start | bytes 319496 | tf_op jit(solution)/shard_map/ppermute | solution.py:616
  22.8 2.2 %collective-permute-start.11 = (bf16[104,512]{1,0:T(8,128)(2,1)S(1)}, bf16[104,512]{1,0:T(8,128)(2,1)S(1)}, u32[]{:S(2)}, u32[]{:S(2)}) collective-permute-start(bf16[104,512]{1,0:T(8,128)(2,1)S(1)} %collective-permute-done.7.refs_1_.refs_2_), channel_id=1, source_target_pairs={{0,8},{1,9},{2,10},{3,11},{4,12},{5,13},{6,14},{7,15},{8,0},{9,1},... | collective-permute-start | bytes 319496 | tf_op jit(solution)/shard_map/ppermute | solution.py:616
  24.6 1.7 %copy-start.1 = (bf16[512,512]{1,0:T(8,128)(2,1)S(1)}, bf16[512,512]{1,0:T(8,128)(2,1)}, u32[]{:S(2)}) copy-start(bf16[512,512]{1,0:T(8,128)(2,1)} %refs_14_.1) | copy-start | bytes 1572868
  24.6 1.7 %copy-start.2 = (bf16[32,512]{1,0:T(8,128)(2,1)S(1)}, bf16[32,512]{1,0:T(8,128)(2,1)}, u32[]{:S(2)}) copy-start(bf16[32,512]{1,0:T(8,128)(2,1)} %refs_15_.1) | copy-start | bytes 98308
  24.6 1.7 %copy-start.3 = (s32[3,1,8]{2,1,0:T(1,128)S(1)}, s32[3,1,8]{2,1,0:T(1,128)}, u32[]{:S(2)}) copy-start(s32[3,1,8]{2,1,0:T(1,128)} %shift_ref.1) | copy-start | bytes 292
  24.6 1.7 %copy-start.4 = (s32[1,8]{1,0:T(1,128)S(1)}, s32[1,8]{1,0:T(1,128)}, u32[]{:S(2)}) copy-start(s32[1,8]{1,0:T(1,128)} %list_ref.1) | copy-start | bytes 100
  24.6 1.7 %copy-start.5 = (s32[1,8]{1,0:T(1,128)S(1)}, s32[1,8]{1,0:T(1,128)}, u32[]{:S(2)}) copy-start(s32[1,8]{1,0:T(1,128)} %valid_ref.1) | copy-start | bytes 100
  24.7 1.7 %copy-start.6 = (f32[3]{0:T(128)S(1)}, f32[3]{0:T(128)}, u32[]{:S(2)}) copy-start(f32[3]{0:T(128)} %param.15) | copy-start | bytes 40
  24.7 1.6 %collective-permute-start.12 = (bf16[104,512]{1,0:T(8,128)(2,1)S(1)}, bf16[104,512]{1,0:T(8,128)(2,1)S(1)}, u32[]{:S(2)}, u32[]{:S(2)}) collective-permute-start(bf16[104,512]{1,0:T(8,128)(2,1)S(1)} %collective-permute-done.8.refs_0_.refs_3_), channel_id=1, source_target_pairs={{0,8},{1,9},{2,10},{3,11},{4,12},{5,13},{6,14},{7,15},{8,0},{9,1},... | collective-permute-start | bytes 319496 | tf_op jit(solution)/shard_map/ppermute | solution.py:616

commit v7 on v6

--- a/solution.py
+++ b/solution.py
@@ -410,20 +410,22 @@
     return jnp.concatenate([array] * (lanes // array.shape[-1]), axis=-1)
 
 
-def first_kernel(head_dim, plan, *refs):
-    blocks, ring_ref, wqkv_ref, tables = refs[:4], refs[4], refs[5], refs[6:10]
-    core_ref, kv_ref, acc_ref, top_ref, sum_ref, qexp_ref, w1_ref, w2_ref, str_ref, own_ref = refs[10:]
-    prepare(
-        head_dim, wqkv_ref, *tables, blocks[0], qexp_ref, w1_ref, w2_ref, str_ref, own_ref
-    )
-    atoms = own_ref.shape[1]
-    dim = wqkv_ref.shape[0]
-    four, three = plan[0][1]
+def core_kernel(*refs):
+    blocks, ring_ref, core_ref = refs[:4], refs[4], refs[5]
+    atoms = blocks[0].shape[0]
+    dim = core_ref.shape[1]
+    four, three = 4 * atoms, 3 * atoms
     for k, block in enumerate(blocks):
         core_ref[k * atoms : (k + 1) * atoms, :] = block[:, :dim]
     core_ref[four : four + three, :] = ring_ref[:three, :]
     core_ref[four + three : four + three + 8, :] = position_tile(blocks, dim)
     core_ref[four + three + 8 :, :] = ring_ref[three:, :]
+
+
+def first_kernel(head_dim, plan, *refs):
+    pack_ref, core_ref, wqkv_ref, tables = refs[0], refs[1], refs[2], refs[3:7]
+    kv_ref, acc_ref, top_ref, sum_ref, qexp_ref, w1_ref, w2_ref, str_ref, own_ref = refs[7:]
+    prepare(head_dim, wqkv_ref, *tables, pack_ref, qexp_ref, w1_ref, w2_ref, str_ref, own_ref)
     got = absorb(head_dim, plan, (core_ref,), wqkv_ref, qexp_ref, str_ref, own_ref, kv_ref)
     for g, (top, total, o) in enumerate(got):
         acc_ref[g] = o
@@ -659,10 +661,11 @@
     plan = [(0, (four, three))] + [(four + k * three, (three,)) for k in (1, 2, 3)]
     plan += [(half + start, counts) for start, counts in plan]
 
-    core, kv, acc, top, summed, qexp, w1, w2, strength, own = call(
+    core = call(core_kernel, vm((four + three + 16, dim), bf16), [], 0, (pack, *owns, ring))
+    core2 = swap(core, flip)
+    kv, acc, top, summed, qexp, w1, w2, strength, own = call(
         functools.partial(first_kernel, head_dim, plan[:1]),
-        [vm((four + three + 16, dim), bf16)]
-        + state_shapes
+        state_shapes
         + [
             vm((groups, rows, width), bf16),
             vm((hidden, 6 * nrbf + 16), bf16),
@@ -672,7 +675,7 @@
         ],
         [],
         0,
-        (pack, *owns, ring, w_qkv, *tables),
+        (pack, core, w_qkv, *tables),
     )
     state = (kv, acc, top, summed)
     common = (w_qkv, qexp, strength, own)
@@ -688,10 +691,11 @@
             {at + k: k for k in range(4)},
         )
 
-    core2 = swap(core, flip)
+    core2, state = tied((core2, state))
+    state = step((4,), (core2,), state)
     east, north, state = tied((east, north, state))
     east2, north2 = swap(east, flip), swap(north, flip)
-    state = step((1, 2, 4), (east, north, core2), state)
+    state = step((1, 2), (east, north), state)
     diag, state = tied((diag, state))
     diag2 = swap(diag, flip)
     state = step((3, 5, 6), (diag, east2, north2), state)

time: 29.6 us -> 27.5 us (0.929)
  waiting for transfers between devices: 8.66 us -> 5.41 us
  starting transfers between devices: 12.5 us -> 13.1 us
  Pallas kernels: 8.17 us -> 8.63 us
    ppermute x13, waiting for transfers between devices: 8.66 us -> 5.41 us  [swap(): return lax.ppermute(array, axes, [(i, i ^ mask) for i in range(total)])]
    ppermute x13, starting transfers between devices: 12.5 us -> 13.1 us  [swap(): return lax.ppermute(array, axes, [(i, i ^ mask) for i in range(total)])]
    pallas_call x6 -> x8, Pallas kernels: 8.17 us -> 8.63 us  [call(): pl.pallas_call(kernel, out_shape=outs, in_specs=specs, out_specs=[vmem] *...]
  transfers between devices with their start and end apart: 13 -> 13, of which waited for: 6 -> 4; matrix products, arithmetic and copies ran while one was open for 0% -> 0% of each run, Pallas kernels for 10% -> 16%
where the time goes in v7:
time: 27.5 us; the launch traced here: 27.4 us
  starting transfers between devices  13.1 us (48%)
  Pallas kernels  8.63 us (31%)
  waiting for transfers between devices  5.41 us (20%)
    ppermute x13, starting transfers between devices, swap(): return lax.ppermute(array, axes, [(i, i ^ mask) for i in range(total)])  13.1 us
    pallas_call x8, Pallas kernels, call(): pl.pallas_call(kernel, out_shape=outs, in_specs=specs, out_specs=[vmem] *...  8.63 us
    ppermute x13, waiting for transfers between devices, swap(): return lax.ppermute(array, axes, [(i, i ^ mask) for i in range(total)])  5.41 us
  transfers between devices with their start and end apart: 13, of which 4 were waited for; matrix products, arithmetic and copies ran while one was open for 0% of the time, Pallas kernels for 16%

profile of v7, /device:TPU:0, one launch (start us, length us, event | category | flops | bytes accessed | tf_op | source)
XLA Modules:
  0.0 27.4 jit_solution(6927490660677317015)
XLA Ops:
  0.0 0.0 copy-start
  0.0 1.1 %shard_map.127 = (bf16[32,640]{1,0:T(8,128)(2,1)S(1)}, f32[16,64]{1,0:T(8,128)S(1)}, f32[1,64]{1,0:T(1,128)S(1)}, f32[16,64]{1,0:T(8,128)S(1)}, f32[1,16]{1,0:T(1,128)S(1)}) custom-call(bf16[32,512]{1,0:T(8,128)(2,1)} %refs_15_.1, f32[1,512]{1,0:T(1,128)} %bitcast.7, f32[3,32]{1,0:T(4,128)} %refs_2_.3, f32[16,64]{1,0:T(8,128)} %refs_3_.2, f32[1,64]{1,0:T(1,128)} %bitcast.8, ...), custom_call_target="tpu_custom_call" | custom-call | tf_op jit(solution)/shard_map/pallas_call | solution.py:571
  1.1 2.6 %collective-permute-start.3 = (bf16[32,640]{1,0:T(8,128)(2,1)S(1)}, bf16[32,640]{1,0:T(8,128)(2,1)S(1)}, u32[]{:S(2)}, u32[]{:S(2)}) collective-permute-start(bf16[32,640]{1,0:T(8,128)(2,1)S(1)} %get-tuple-element.53.refs_0_), channel_id=1, source_target_pairs={{0,10},{1,11},{2,8},{3,9},{4,14},{5,15},{6,12},{7,13},{8,2},{9,3},... | collective-permute-start | bytes 122888 | tf_op jit(solution)/shard_map/ppermute | solution.py:618
  3.7 2.9 %collective-permute-start.4 = (bf16[32,640]{1,0:T(8,128)(2,1)S(1)}, bf16[32,640]{1,0:T(8,128)(2,1)S(1)}, u32[]{:S(2)}, u32[]{:S(2)}) collective-permute-start(bf16[32,640]{1,0:T(8,128)(2,1)S(1)} %get-tuple-element.53.refs_0_), channel_id=1, source_target_pairs={{0,12},{1,13},{2,14},{3,15},{4,8},{5,9},{6,10},{7,11},{8,4},{9,5},... | collective-permute-start | bytes 122888 | tf_op jit(solution)/shard_map/ppermute | solution.py:618
  6.5 0.0 collective-permute-start.5
  6.6 1.5 %collective-permute-start = (bf16[32,640]{1,0:T(8,128)(2,1)S(1)}, bf16[32,640]{1,0:T(8,128)(2,1)S(1)}, u32[]{:S(2)}, u32[]{:S(2)}) collective-permute-start(bf16[32,640]{1,0:T(8,128)(2,1)S(1)} %get-tuple-element.53.refs_0_), channel_id=1, source_target_pairs={{0,9},{1,8},{2,11},{3,10},{4,13},{5,12},{6,15},{7,14},{8,1},{9,0},... | collective-permute-start | bytes 122888 | tf_op jit(solution)/shard_map/ppermute | solution.py:618
  8.0 1.3 %collective-permute-start.1 = (bf16[32,640]{1,0:T(8,128)(2,1)S(1)}, bf16[32,640]{1,0:T(8,128)(2,1)S(1)}, u32[]{:S(2)}, u32[]{:S(2)}) collective-permute-start(bf16[32,640]{1,0:T(8,128)(2,1)S(1)} %get-tuple-element.53.refs_0_), channel_id=1, source_target_pairs={{0,24},{1,25},{2,26},{3,27},{4,28},{5,29},{6,30},{7,31},{8,16},{9,... | collective-permute-start | bytes 122888 | tf_op jit(solution)/shard_map/ppermute | solution.py:618
  9.3 0.0 collective-permute-done.3.refs_0_
  9.3 0.1 collective-permute-start.2
  9.4 0.0 collective-permute-done.4.refs_1_
  9.4 2.8 %collective-permute-done.5.refs_2_ = bf16[32,640]{1,0:T(8,128)(2,1)S(1)} collective-permute-done((bf16[32,640]{1,0:T(8,128)(2,1)S(1)}, bf16[32,640]{1,0:T(8,128)(2,1)S(1)}, u32[]{:S(2)}, u32[]{:S(2)}) %collective-permute-start.5) | collective-permute-done | bytes 40992 | tf_op jit(solution)/shard_map/ppermute | solution.py:618
  12.2 0.1 shard_map.128.refs_4_
  12.3 0.0 collective-permute-done.refs_1_
  12.3 0.0 collective-permute-done.1.refs_2_
  12.4 1.2 %collective-permute-done.2.refs_3_ = bf16[32,640]{1,0:T(8,128)(2,1)S(1)} collective-permute-done((bf16[32,640]{1,0:T(8,128)(2,1)S(1)}, bf16[32,640]{1,0:T(8,128)(2,1)S(1)}, u32[]{:S(2)}, u32[]{:S(2)}) %collective-permute-start.2) | collective-permute-done | bytes 40992 | tf_op jit(solution)/shard_map/ppermute | solution.py:618
  13.6 0.2 shard_map.129.refs_1_.refs_0_
  13.8 0.4 %collective-permute-start.8 = (bf16[240,512]{1,0:T(8,128)(2,1)S(1)}, bf16[240,512]{1,0:T(8,128)(2,1)S(1)}, u32[]{:S(2)}, u32[]{:S(2)}) collective-permute-start(bf16[240,512]{1,0:T(8,128)(2,1)S(1)} %shard_map.129.refs_1_.refs_0_), channel_id=1, source_target_pairs={{0,8},{1,9},{2,10},{3,11},{4,12},{5,13},{6,14},{7,15},{8,0},{9,1},... | collective-permute-start | bytes 737288 | tf_op jit(solution)/shard_map/ppermute | solution.py:618
  14.1 0.3 %collective-permute-start.6 = (bf16[104,512]{1,0:T(8,128)(2,1)S(1)}, bf16[104,512]{1,0:T(8,128)(2,1)S(1)}, u32[]{:S(2)}, u32[]{:S(2)}) collective-permute-start(bf16[104,512]{1,0:T(8,128)(2,1)S(1)} %shard_map.128.refs_4_), channel_id=1, source_target_pairs={{0,9},{1,8},{2,11},{3,10},{4,13},{5,12},{6,15},{7,14},{8,1},{9,0},... | collective-permute-start | bytes 319496 | tf_op jit(solution)/shard_map/ppermute | solution.py:618
  14.4 1.0 %collective-permute-start.7 = (bf16[104,512]{1,0:T(8,128)(2,1)S(1)}, bf16[104,512]{1,0:T(8,128)(2,1)S(1)}, u32[]{:S(2)}, u32[]{:S(2)}) collective-permute-start(bf16[104,512]{1,0:T(8,128)(2,1)S(1)} %shard_map.128.refs_4_), channel_id=1, source_target_pairs={{0,24},{1,25},{2,26},{3,27},{4,28},{5,29},{6,30},{7,31},{8,16},{9,... | collective-permute-start | bytes 319496 | tf_op jit(solution)/shard_map/ppermute | solution.py:618
  15.4 1.7 %collective-permute-start.9 = (bf16[104,512]{1,0:T(8,128)(2,1)S(1)}, bf16[104,512]{1,0:T(8,128)(2,1)S(1)}, u32[]{:S(2)}, u32[]{:S(2)}) collective-permute-start(bf16[104,512]{1,0:T(8,128)(2,1)S(1)} %shard_map.128.refs_4_), channel_id=1, source_target_pairs={{0,25},{1,24},{2,27},{3,26},{4,29},{5,28},{6,31},{7,30},{8,17},{9,... | collective-permute-start | bytes 319496 | tf_op jit(solution)/shard_map/ppermute | solution.py:618
  17.1 0.0 copy-done
  17.1 0.9 %shard_map.130 = (bf16[1024,1024]{1,0:T(8,128)(2,1)S(1)}, f32[2,32,8,256]{3,2,1,0:T(8,128)S(1)}, f32[2,32,8,128]{3,2,1,0:T(8,128)S(1)}, f32[2,32,8,128]{3,2,1,0:...) custom-call(bf16[32,640]{1,0:T(8,128)(2,1)S(1)} %get-tuple-element.5, ...), custom_call_target="tpu_custom_call" | custom-call | tf_op jit(solution)/shard_map/pallas_call | solution.py:571
  18.0 0.0 collective-permute-done.8.refs_0_.refs_4_
  18.1 1.0 %shard_map.131 = (bf16[1024,1024]{1,0:T(8,128)(2,1)S(1)}, f32[2,32,8,256]{3,2,1,0:T(8,128)S(1)}, f32[2,32,8,128]{3,2,1,0:T(8,128)S(1)}, f32[2,32,8,128]{3,2,1,0:T(8,128)S(1)}) custom-call(bf16[240,512]{1,0:T(8,128)(2,1)S(1)} %collective-permute-done.8.refs_0_.refs_4_, ...), custom_call_target="tpu_custom_call", output_to_operand_aliasing={{0}: (5, {}), {1}: (6, {}), {2}: (7, {}), {3}: (8, {})} | custom-call | tf_op jit(solution)/shard_map/pallas_call | solution.py:571
  19.0 0.0 collective-permute-done.6.refs_0_.refs_1_
  19.1 0.1 collective-permute-done.7.refs_1_.refs_2_
  19.2 1.1 %collective-permute-start.10 = (bf16[104,512]{1,0:T(8,128)(2,1)S(1)}, bf16[104,512]{1,0:T(8,128)(2,1)S(1)}, u32[]{:S(2)}, u32[]{:S(2)}) collective-permute-start(bf16[104,512]{1,0:T(8,128)(2,1)S(1)} %collective-permute-done.6.refs_0_.refs_1_), channel_id=1, source_target_pairs={{0,8},{1,9},{2,10},{3,11},{4,12},{5,13},{6,14},{7,15},{8,0},{9,1},... | collective-permute-start | bytes 319496 | tf_op jit(solution)/shard_map/ppermute | solution.py:618
  20.3 0.0 collective-permute-start.11
  20.3 0.9 %shard_map.132 = (bf16[1024,1024]{1,0:T(8,128)(2,1)S(1)}, f32[2,32,8,256]{3,2,1,0:T(8,128)S(1)}, f32[2,32,8,128]{3,2,1,0:T(8,128)S(1)}, f32[2,32,8,128]{3,2,1,0:T(8,128)S(1)}) custom-call(bf16[104,512]{1,0:T(8,128)(2,1)S(1)} %collective-permute-done.6.refs_0_.refs_1_, ...), custom_call_target="tpu_custom_call", output_to_operand_aliasing={{0}: (6, {}), {1}: (7, {}), {2}: (8, {}), {3}: (9, {})} | custom-call | tf_op jit(solution)/shard_map/pallas_call | solution.py:571
  21.3 1.1 %collective-permute-done.9.refs_0_.refs_3_ = bf16[104,512]{1,0:T(8,128)(2,1)S(1)} collective-permute-done((bf16[104,512]{1,0:T(8,128)(2,1)S(1)}, bf16[104,512]{1,0:T(8,128)(2,1)S(1)}, u32[]{:S(2)}, u32[]{:S(2)}) %collective-permute-start.9) | collective-permute-done | bytes 106528 | tf_op jit(solution)/shard_map/ppermute | solution.py:618
  22.4 0.0 copy-start.1
  22.4 0.0 copy-start.2
  22.4 0.0 copy-start.3
  22.4 0.0 copy-start.4
  22.4 0.0 copy-start.5
  22.4 0.0 copy-start.6
  22.5 0.4 %collective-permute-start.12 = (bf16[104,512]{1,0:T(8,128)(2,1)S(1)}, bf16[104,512]{1,0:T(8,128)(2,1)S(1)}, u32[]{:S(2)}, u32[]{:S(2)}) collective-permute-start(bf16[104,512]{1,0:T(8,128)(2,1)S(1)} %collective-permute-done.9.refs_0_.refs_3_), channel_id=1, source_target_pairs={{0,8},{1,9},{2,10},{3,11},{4,12},{5,13},{6,14},{7,15},{8,0},{9,1},... | collective-permute-start | bytes 319496 | tf_op jit(solution)/shard_map/ppermute | solution.py:618
  22.9 0.0 collective-permute-done.10.refs_1_.refs_5_
  22.9 0.0 collective-permute-done.11.refs_2_.refs_6_
  22.9 1.3 %shard_map.133 = (bf16[1024,1024]{1,0:T(8,128)(2,1)S(1)}, f32[2,32,8,256]{3,2,1,0:T(8,128)S(1)}, f32[2,32,8,128]{3,2,1,0:T(8,128)S(1)}, f32[2,32,8,128]{3,2,1,0:T(8,128)S(1)}) custom-call(bf16[104,512]{1,0:T(8,128)(2,1)S(1)} %collective-permute-done.9.refs_0_.refs_3_, ...), custom_call_target="tpu_custom_call", output_to_operand_aliasing={{0}: (7, {}), {1}: (8, {}), {2}: (9, {}), {3}: (10, {})} | custom-call | tf_op jit(solution)/shard_map/pallas_call | solution.py:571
  24.2 0.0 collective-permute-done.12.refs_7_
  24.2 0.0 copy-done.1
  24.2 0.0 copy-done.2
  24.2 0.0 copy-done.3
  24.2 0.0 copy-done.4
  24.2 0.0 copy-done.5
  24.2 0.0 copy-done.6
  24.2 3.1 %shard_map.134 = (bf16[32,512]{1,0:T(8,128)(2,1)}, bf16[1024,1024]{1,0:T(8,128)(2,1)S(1)}) custom-call(s32[1,8]{1,0:T(1,128)S(1)} %copy-done.4, s32[1,8]{1,0:T(1,128)S(1)} %copy-done.5, s32[3,1,8]{2,1,0:T(1,128)S(1)} %copy-done.3, f32[1,3]{1,0:T(1,128)S(1)} %bitcast.5, ...), custom_call_target="tpu_custom_call", output_to_operand_aliasing={{1}: (20, {})} | custom-call | tf_op jit(solution)/shard_map/pallas_call | solution.py:571
Async XLA Ops:
  0.0 17.1 %copy-start = (bf16[512,1536]{1,0:T(8,128)(2,1)S(1)}, bf16[512,1536]{1,0:T(8,128)(2,1)}, u32[]{:S(2)}) copy-start(bf16[512,1536]{1,0:T(8,128)(2,1)} %refs_8_.1) | copy-start | bytes 4718596
  1.1 8.2 %collective-permute-start.3 = (bf16[32,640]{1,0:T(8,128)(2,1)S(1)}, bf16[32,640]{1,0:T(8,128)(2,1)S(1)}, u32[]{:S(2)}, u32[]{:S(2)}) collective-permute-start(bf16[32,640]{1,0:T(8,128)(2,1)S(1)} %get-tuple-element.53.refs_0_), channel_id=1, source_target_pairs={{0,10},{1,11},{2,8},{3,9},{4,14},{5,15},{6,12},{7,13},{8,2},{9,3},... | collective-permute-start | bytes 122888 | tf_op jit(solution)/shard_map/ppermute | solution.py:618
  3.7 5.7 %collective-permute-start.4 = (bf16[32,640]{1,0:T(8,128)(2,1)S(1)}, bf16[32,640]{1,0:T(8,128)(2,1)S(1)}, u32[]{:S(2)}, u32[]{:S(2)}) collective-permute-start(bf16[32,640]{1,0:T(8,128)(2,1)S(1)} %get-tuple-element.53.refs_0_), channel_id=1, source_target_pairs={{0,12},{1,13},{2,14},{3,15},{4,8},{5,9},{6,10},{7,11},{8,4},{9,5},... | collective-permute-start | bytes 122888 | tf_op jit(solution)/shard_map/ppermute | solution.py:618
  6.5 5.6 %collective-permute-start.5 = (bf16[32,640]{1,0:T(8,128)(2,1)S(1)}, bf16[32,640]{1,0:T(8,128)(2,1)S(1)}, u32[]{:S(2)}, u32[]{:S(2)}) collective-permute-start(bf16[32,640]{1,0:T(8,128)(2,1)S(1)} %get-tuple-element.53.refs_0_), channel_id=1, source_target_pairs={{0,14},{1,15},{2,12},{3,13},{4,10},{5,11},{6,8},{7,9},{8,6},{9,7},... | collective-permute-start | bytes 122888 | tf_op jit(solution)/shard_map/ppermute | solution.py:618
  6.6 5.8 %collective-permute-start = (bf16[32,640]{1,0:T(8,128)(2,1)S(1)}, bf16[32,640]{1,0:T(8,128)(2,1)S(1)}, u32[]{:S(2)}, u32[]{:S(2)}) collective-permute-start(bf16[32,640]{1,0:T(8,128)(2,1)S(1)} %get-tuple-element.53.refs_0_), channel_id=1, source_target_pairs={{0,9},{1,8},{2,11},{3,10},{4,13},{5,12},{6,15},{7,14},{8,1},{9,0},... | collective-permute-start | bytes 122888 | tf_op jit(solution)/shard_map/ppermute | solution.py:618
  8.0 4.3 %collective-permute-start.1 = (bf16[32,640]{1,0:T(8,128)(2,1)S(1)}, bf16[32,640]{1,0:T(8,128)(2,1)S(1)}, u32[]{:S(2)}, u32[]{:S(2)}) collective-permute-start(bf16[32,640]{1,0:T(8,128)(2,1)S(1)} %get-tuple-element.53.refs_0_), channel_id=1, source_target_pairs={{0,24},{1,25},{2,26},{3,27},{4,28},{5,29},{6,30},{7,31},{8,16},{9,... | collective-permute-start | bytes 122888 | tf_op jit(solution)/shard_map/ppermute | solution.py:618
  9.3 4.3 %collective-permute-start.2 = (bf16[32,640]{1,0:T(8,128)(2,1)S(1)}, bf16[32,640]{1,0:T(8,128)(2,1)S(1)}, u32[]{:S(2)}, u32[]{:S(2)}) collective-permute-start(bf16[32,640]{1,0:T(8,128)(2,1)S(1)} %get-tuple-element.53.refs_0_), channel_id=1, source_target_pairs={{0,25},{1,24},{2,27},{3,26},{4,29},{5,28},{6,31},{7,30},{8,17},{9,... | collective-permute-start | bytes 122888 | tf_op jit(solution)/shard_map/ppermute | solution.py:618
  13.8 4.3 %collective-permute-start.8 = (bf16[240,512]{1,0:T(8,128)(2,1)S(1)}, bf16[240,512]{1,0:T(8,128)(2,1)S(1)}, u32[]{:S(2)}, u32[]{:S(2)}) collective-permute-start(bf16[240,512]{1,0:T(8,128)(2,1)S(1)} %shard_map.129.refs_1_.refs_0_), channel_id=1, source_target_pairs={{0,8},{1,9},{2,10},{3,11},{4,12},{5,13},{6,14},{7,15},{8,0},{9,1},... | collective-permute-start | bytes 737288 | tf_op jit(solution)/shard_map/ppermute | solution.py:618
  14.1 4.9 %collective-permute-start.6 = (bf16[104,512]{1,0:T(8,128)(2,1)S(1)}, bf16[104,512]{1,0:T(8,128)(2,1)S(1)}, u32[]{:S(2)}, u32[]{:S(2)}) collective-permute-start(bf16[104,512]{1,0:T(8,128)(2,1)S(1)} %shard_map.128.refs_4_), channel_id=1, source_target_pairs={{0,9},{1,8},{2,11},{3,10},{4,13},{5,12},{6,15},{7,14},{8,1},{9,0},... | collective-permute-start | bytes 319496 | tf_op jit(solution)/shard_map/ppermute | solution.py:618
  14.4 4.8 %collective-permute-start.7 = (bf16[104,512]{1,0:T(8,128)(2,1)S(1)}, bf16[104,512]{1,0:T(8,128)(2,1)S(1)}, u32[]{:S(2)}, u32[]{:S(2)}) collective-permute-start(bf16[104,512]{1,0:T(8,128)(2,1)S(1)} %shard_map.128.refs_4_), channel_id=1, source_target_pairs={{0,24},{1,25},{2,26},{3,27},{4,28},{5,29},{6,30},{7,31},{8,16},{9,... | collective-permute-start | bytes 319496 | tf_op jit(solution)/shard_map/ppermute | solution.py:618
  15.4 7.0 %collective-permute-start.9 = (bf16[104,512]{1,0:T(8,128)(2,1)S(1)}, bf16[104,512]{1,0:T(8,128)(2,1)S(1)}, u32[]{:S(2)}, u32[]{:S(2)}) collective-permute-start(bf16[104,512]{1,0:T(8,128)(2,1)S(1)} %shard_map.128.refs_4_), channel_id=1, source_target_pairs={{0,25},{1,24},{2,27},{3,26},{4,29},{5,28},{6,31},{7,30},{8,17},{9,... | collective-permute-start | bytes 319496 | tf_op jit(solution)/shard_map/ppermute | solution.py:618
  19.2 3.7 %collective-permute-start.10 = (bf16[104,512]{1,0:T(8,128)(2,1)S(1)}, bf16[104,512]{1,0:T(8,128)(2,1)S(1)}, u32[]{:S(2)}, u32[]{:S(2)}) collective-permute-start(bf16[104,512]{1,0:T(8,128)(2,1)S(1)} %collective-permute-done.6.refs_0_.refs_1_), channel_id=1, source_target_pairs={{0,8},{1,9},{2,10},{3,11},{4,12},{5,13},{6,14},{7,15},{8,0},{9,1},... | collective-permute-start | bytes 319496 | tf_op jit(solution)/shard_map/ppermute | solution.py:618
  20.3 2.5 %collective-permute-start.11 = (bf16[104,512]{1,0:T(8,128)(2,1)S(1)}, bf16[104,512]{1,0:T(8,128)(2,1)S(1)}, u32[]{:S(2)}, u32[]{:S(2)}) collective-permute-start(bf16[104,512]{1,0:T(8,128)(2,1)S(1)} %collective-permute-done.7.refs_1_.refs_2_), channel_id=1, source_target_pairs={{0,8},{1,9},{2,10},{3,11},{4,12},{5,13},{6,14},{7,15},{8,0},{9,1},... | collective-permute-start | bytes 319496 | tf_op jit(solution)/shard_map/ppermute | solution.py:618
  22.4 1.8 %copy-start.1 = (bf16[512,512]{1,0:T(8,128)(2,1)S(1)}, bf16[512,512]{1,0:T(8,128)(2,1)}, u32[]{:S(2)}) copy-start(bf16[512,512]{1,0:T(8,128)(2,1)} %refs_14_.1) | copy-start | bytes 1572868
  22.4 1.8 %copy-start.2 = (bf16[32,512]{1,0:T(8,128)(2,1)S(1)}, bf16[32,512]{1,0:T(8,128)(2,1)}, u32[]{:S(2)}) copy-start(bf16[32,512]{1,0:T(8,128)(2,1)} %refs_15_.1) | copy-start | bytes 98308
  22.4 1.8 %copy-start.3 = (s32[3,1,8]{2,1,0:T(1,128)S(1)}, s32[3,1,8]{2,1,0:T(1,128)}, u32[]{:S(2)}) copy-start(s32[3,1,8]{2,1,0:T(1,128)} %shift_ref.1) | copy-start | bytes 292
  22.4 1.8 %copy-start.4 = (s32[1,8]{1,0:T(1,128)S(1)}, s32[1,8]{1,0:T(1,128)}, u32[]{:S(2)}) copy-start(s32[1,8]{1,0:T(1,128)} %list_ref.1) | copy-start | bytes 100
  22.4 1.8 %copy-start.5 = (s32[1,8]{1,0:T(1,128)S(1)}, s32[1,8]{1,0:T(1,128)}, u32[]{:S(2)}) copy-start(s32[1,8]{1,0:T(1,128)} %valid_ref.1) | copy-start | bytes 100
  22.4 1.8 %copy-start.6 = (f32[3]{0:T(128)S(1)}, f32[3]{0:T(128)}, u32[]{:S(2)}) copy-start(f32[3]{0:T(128)} %param.15) | copy-start | bytes 40
  22.5 1.7 %collective-permute-start.12 = (bf16[104,512]{1,0:T(8,128)(2,1)S(1)}, bf16[104,512]{1,0:T(8,128)(2,1)S(1)}, u32[]{:S(2)}, u32[]{:S(2)}) collective-permute-start(bf16[104,512]{1,0:T(8,128)(2,1)S(1)} %collective-permute-done.9.refs_0_.refs_3_), channel_id=1, source_target_pairs={{0,8},{1,9},{2,10},{3,11},{4,12},{5,13},{6,14},{7,15},{8,0},{9,1},... | collective-permute-start | bytes 319496 | tf_op jit(solution)/shard_map/ppermute | solution.py:618

commit v8 on v7

--- a/solution.py
+++ b/solution.py
@@ -12,6 +12,7 @@
 rbf_step = 2.0
 rbf_width = 2.0
 two_pi = 2.0 * math.pi
+log2_e = 1.0 / math.log(2.0)
 highest = lax.Precision.HIGHEST
 
 
@@ -260,17 +261,15 @@
     feat_ref, gain_ref, pos_ref, tmp_ref, sems = refs[12:]
     copies = fetch(list(zip(sources, (feat_ref, gain_ref, pos_ref, *tables))), sems)
     settle(copies[:3])
-    atoms, dim = feat_ref.shape
+    atoms, _ = feat_ref.shape
     floats = feat_ref[...].astype(jnp.float32)
     spread = jnp.mean(floats * floats, axis=-1, keepdims=True)
     normed = floats * lax.rsqrt(spread + 1e-06) * gain_ref[...]
-    out_ref[:, :dim] = normed.astype(jnp.bfloat16)
+    out_ref[:atoms, :] = normed.astype(jnp.bfloat16)
     tmp_ref[...] = jnp.zeros(tmp_ref.shape, jnp.float32)
     for p, part in enumerate(parts_of(pos_ref[...], 3)):
-        tmp_ref[8 * p : 8 * p + 3, :] = part.astype(jnp.float32)
-    eye = unit(atoms, atoms, jnp.bfloat16)
-    turned = mm(eye, tmp_ref[...].astype(jnp.bfloat16), ((1,), (1,)))
-    out_ref[:, dim:] = turned.astype(jnp.bfloat16)
+        tmp_ref[:3, p * 128 : p * 128 + atoms] = part.astype(jnp.float32)
+    out_ref[atoms:, :] = tmp_ref[...].astype(jnp.bfloat16)
     settle(copies[3:])
 
 
@@ -288,11 +287,14 @@
     str_ref,
     own_ref,
 ):
-    atoms = pack_ref.shape[0]
+    atoms = own_ref.shape[1]
     dim = wqkv_ref.shape[0]
     groups, rows, width = qexp_ref.shape
     per = rows // atoms
-    pos = pack_ref[:, dim:].astype(jnp.float32)
+    tile = pack_ref[atoms:, :].astype(jnp.float32)
+    tile = jnp.concatenate([tile[:, p * 128 : p * 128 + atoms] for p in range(3)], axis=0)
+    pos = mm(unit(atoms, atoms, jnp.bfloat16), tile.astype(jnp.bfloat16), ((1,), (1,)))
+    pos = jnp.concatenate([pos, jnp.zeros((atoms, 128 - 24), jnp.float32)], axis=1)
     pos = pos + pltpu.roll(pos, 120, 1) + pltpu.roll(pos, 112, 1)
     own_ref[0] = pos
     own_ref[1] = jnp.cos(two_pi * pos)
@@ -305,10 +307,10 @@
         tail = jnp.where(row == k, part.astype(jnp.float32), tail)
     stack = jnp.concatenate([h, h, m, h, l, m, tail.astype(jnp.bfloat16)], axis=0)
     w1_ref[...] = mm(unit(hidden, hidden, jnp.bfloat16), stack, ((1,), (1,))).astype(jnp.bfloat16)
-    h, l = parts_of(pw_ref[...], 2)
+    h, l = parts_of(log2_e * pw_ref[...], 2)
     w2_ref[...] = jnp.concatenate([h, h, l], axis=1)
-    str_ref[...] = jnp.broadcast_to(to_column(cs_ref[...]), str_ref.shape)
-    q = mm(pack_ref[:, :dim], wqkv_ref[:, :dim], ((1,), (0,)))
+    str_ref[...] = jnp.broadcast_to(to_column(log2_e * cs_ref[...]), str_ref.shape)
+    q = mm(pack_ref[:atoms, :], wqkv_ref[:, :dim], ((1,), (0,)))
     q = q.astype(jnp.bfloat16).astype(jnp.float32)
     lane = lax.broadcasted_iota(jnp.int32, (per, width), 1) // head_dim
     sub = lax.broadcasted_iota(jnp.int32, (per, width), 0)
@@ -320,28 +322,26 @@
         qexp_ref[g] = spread.astype(jnp.bfloat16)
 
 
-def position_tile(blocks, dim):
-    pos = jnp.concatenate([block[:, dim:] for block in blocks], axis=0)
-    r = lax.broadcasted_iota(jnp.int32, (8, 128), 0)
-    c = lax.broadcasted_iota(jnp.int32, (8, 128), 1)
+def position_tile(blocks, atoms, dim):
+    tiles = [block[atoms:, :].astype(jnp.float32) for block in blocks]
+    pad = 128 - atoms * len(blocks)
     out = []
     for p in range(3):
-        pick = ((c == 8 * p + r) & (r < 3)).astype(jnp.bfloat16)
-        part = mm(pick, pos, ((1,), (1,)))
-        if part.shape[1] < 128:
-            part = jnp.concatenate([part, jnp.zeros((8, 128 - part.shape[1]), jnp.float32)], axis=1)
-        out.append(part)
+        part = [tile[:, p * 128 : p * 128 + atoms] for tile in tiles]
+        if pad:
+            part.append(jnp.zeros((8, pad), jnp.float32))
+        out += part
     out.append(jnp.zeros((8, dim - 3 * 128), jnp.float32))
     return jnp.concatenate(out, axis=1).astype(jnp.bfloat16)
 
 
 def repack_kernel(_, *refs):
     blocks, out_ref = refs[:-1], refs[-1]
-    atoms = blocks[0].shape[0]
+    atoms = blocks[0].shape[0] - 8
     dim = out_ref.shape[1]
     for k, block in enumerate(blocks):
-        out_ref[k * atoms : (k + 1) * atoms, :] = block[:, :dim]
-    out_ref[len(blocks) * atoms :, :] = position_tile(blocks, dim)
+        out_ref[k * atoms : (k + 1) * atoms, :] = block[:atoms, :]
+    out_ref[len(blocks) * atoms :, :] = position_tile(blocks, atoms, dim)
 
 
 def piece_tiles(piece, counts):
@@ -359,7 +359,7 @@
     atoms, per, _ = bias3.shape
     s = mm(qexp, keys, ((1,), (1,))).reshape(atoms, per, count) * scale + bias3
     top = jnp.max(s, axis=-1, keepdims=True)
-    p = jnp.exp(s - top)
+    p = jnp.exp2(s - top)
     total = jnp.sum(p, axis=-1, keepdims=True)
     o = mm(p.astype(jnp.bfloat16).reshape(rows, count), vals, ((1,), (0,)))
     return top, total, o.reshape(atoms, per, vals.shape[1])
@@ -395,7 +395,7 @@
                 qexp_ref[g],
                 kv[:, low:high],
                 kv[:, dim + low : dim + high],
-                head_dim ** (-0.5),
+                log2_e * head_dim ** (-0.5),
                 bias3,
             )
         )
@@ -412,13 +412,13 @@
 
 def core_kernel(*refs):
     blocks, ring_ref, core_ref = refs[:4], refs[4], refs[5]
-    atoms = blocks[0].shape[0]
+    atoms = blocks[0].shape[0] - 8
     dim = core_ref.shape[1]
     four, three = 4 * atoms, 3 * atoms
     for k, block in enumerate(blocks):
-        core_ref[k * atoms : (k + 1) * atoms, :] = block[:, :dim]
+        core_ref[k * atoms : (k + 1) * atoms, :] = block[:atoms, :]
     core_ref[four : four + three, :] = ring_ref[:three, :]
-    core_ref[four + three : four + three + 8, :] = position_tile(blocks, dim)
+    core_ref[four + three : four + three + 8, :] = position_tile(blocks, atoms, dim)
     core_ref[four + three + 8 :, :] = ring_ref[three:, :]
 
 
@@ -437,7 +437,7 @@
     top, total, o = got[g]
     width = o.shape[-1]
     best = jnp.maximum(widen(top, 128), top_ref[g])
-    a, b = jnp.exp(top_ref[g] - best), jnp.exp(widen(top, 128) - best)
+    a, b = jnp.exp2(top_ref[g] - best), jnp.exp2(widen(top, 128) - best)
     summed = a * sum_ref[g] + b * widen(total, 128)
     acc = repeat_lanes(a, width) * acc_ref[g] + repeat_lanes(b, width) * o
     return best, summed, acc
@@ -540,19 +540,19 @@
     for g in range(groups):
         low, high = g * width, (g + 1) * width
         _, summed, far = merge(got, g, acc_in, top_in, sum_in)
-        far = far / repeat_lanes(summed, width)
+        far = far * repeat_lanes(1.0 / summed, width)
         far = jnp.sum(jnp.where(keep, far, 0.0), axis=1).astype(jnp.bfloat16)
         s = mm(qexp_ref[g], near_ref[:, low:high], ((1,), (1,)))
-        s = s.reshape(atoms, per, listed) * head_dim ** (-0.5) + bias_ref[g]
+        s = s.reshape(atoms, per, listed) * (log2_e * head_dim ** (-0.5)) + bias_ref[g]
         s = jnp.where(live, s, -1e30)
-        p = jnp.exp(s - jnp.max(s, axis=-1, keepdims=True))
+        p = jnp.exp2(s - jnp.max(s, axis=-1, keepdims=True))
         summed = jnp.sum(p, axis=-1, keepdims=True)
         o = mm(
             p.astype(jnp.bfloat16).reshape(rows, listed),
             near_ref[:, dim + low : dim + high],
             ((1,), (0,)),
         )
-        o = o.reshape(atoms, per, width) / summed
+        o = o.reshape(atoms, per, width) * (1.0 / summed)
         close = jnp.sum(jnp.where(keep, o, 0.0), axis=1).astype(jnp.bfloat16)
         pieces.append((close.astype(jnp.float32) + far.astype(jnp.float32)).astype(jnp.bfloat16))
     combined = jnp.concatenate(pieces, axis=1)
@@ -632,12 +632,12 @@
     tables = (rbf_weight, rbf_offset[None], pair_weight.T, cosine_scale[None])
     pack, *tables = call(
         pack_kernel,
-        [vm((atoms, dim + 128), bf16)] + [vm(table.shape, f32) for table in tables],
+        [vm((atoms + 8, dim), bf16)] + [vm(table.shape, f32) for table in tables],
         [
             vm((atoms, dim), bf16),
             vm((1, dim), f32),
             vm(positions.shape, f32),
-            vm((128, atoms), f32),
+            vm((8, dim), f32),
             pltpu.SemaphoreType.DMA((7,)),
         ],
         0,

time: 27.5 us -> 27.3 us (level)
  no operation moved by 1% of the time
where the time goes in v8:
time: 27.3 us; the launch traced here: 27.2 us
  starting transfers between devices  13.1 us (48%)
  Pallas kernels  8.49 us (31%)
  waiting for transfers between devices  5.42 us (20%)
    ppermute x13, starting transfers between devices, swap(): return lax.ppermute(array, axes, [(i, i ^ mask) for i in range(total)])  13.1 us
    pallas_call x8, Pallas kernels, call(): pl.pallas_call(kernel, out_shape=outs, in_specs=specs, out_specs=[vmem] *...  8.49 us
    ppermute x13, waiting for transfers between devices, swap(): return lax.ppermute(array, axes, [(i, i ^ mask) for i in range(total)])  5.42 us
  transfers between devices with their start and end apart: 13, of which 4 were waited for; matrix products, arithmetic and copies ran while one was open for 0% of the time, Pallas kernels for 16%

profile of v8, /device:TPU:0, one launch (start us, length us, event | category | flops | bytes accessed | tf_op | source)
XLA Modules:
  0.0 27.2 jit_solution(16168228749497404535)
XLA Ops:
  0.0 0.0 copy-start
  0.0 1.0 %shard_map.127 = (bf16[40,512]{1,0:T(8,128)(2,1)S(1)}, f32[16,64]{1,0:T(8,128)S(1)}, f32[1,64]{1,0:T(1,128)S(1)}, f32[16,64]{1,0:T(8,128)S(1)}, f32[1,16]{1,0:T(1,128)S(1)}) custom-call(bf16[32,512]{1,0:T(8,128)(2,1)} %refs_15_.1, f32[1,512]{1,0:T(1,128)} %bitcast.7, f32[3,32]{1,0:T(4,128)} %refs_2_.3, f32[16,64]{1,0:T(8,128)} %refs_3_.2, f32[1,64]{1,0:T(1,128)} %bitcast.8, ...), custom_call_target="tpu_custom_call" | custom-call | tf_op jit(solution)/shard_map/pallas_call | solution.py:571
  1.1 2.6 %collective-permute-start.3 = (bf16[40,512]{1,0:T(8,128)(2,1)S(1)}, bf16[40,512]{1,0:T(8,128)(2,1)S(1)}, u32[]{:S(2)}, u32[]{:S(2)}) collective-permute-start(bf16[40,512]{1,0:T(8,128)(2,1)S(1)} %get-tuple-element.53.refs_0_), channel_id=1, source_target_pairs={{0,10},{1,11},{2,8},{3,9},{4,14},{5,15},{6,12},{7,13},{8,2},{9,3},... | collective-permute-start | bytes 122888 | tf_op jit(solution)/shard_map/ppermute | solution.py:618
  3.6 2.9 %collective-permute-start.4 = (bf16[40,512]{1,0:T(8,128)(2,1)S(1)}, bf16[40,512]{1,0:T(8,128)(2,1)S(1)}, u32[]{:S(2)}, u32[]{:S(2)}) collective-permute-start(bf16[40,512]{1,0:T(8,128)(2,1)S(1)} %get-tuple-element.53.refs_0_), channel_id=1, source_target_pairs={{0,12},{1,13},{2,14},{3,15},{4,8},{5,9},{6,10},{7,11},{8,4},{9,5},... | collective-permute-start | bytes 122888 | tf_op jit(solution)/shard_map/ppermute | solution.py:618
  6.5 0.0 collective-permute-start.5
  6.5 1.5 %collective-permute-start = (bf16[40,512]{1,0:T(8,128)(2,1)S(1)}, bf16[40,512]{1,0:T(8,128)(2,1)S(1)}, u32[]{:S(2)}, u32[]{:S(2)}) collective-permute-start(bf16[40,512]{1,0:T(8,128)(2,1)S(1)} %get-tuple-element.53.refs_0_), channel_id=1, source_target_pairs={{0,9},{1,8},{2,11},{3,10},{4,13},{5,12},{6,15},{7,14},{8,1},{9,0},... | collective-permute-start | bytes 122888 | tf_op jit(solution)/shard_map/ppermute | solution.py:618
  7.9 1.3 %collective-permute-start.1 = (bf16[40,512]{1,0:T(8,128)(2,1)S(1)}, bf16[40,512]{1,0:T(8,128)(2,1)S(1)}, u32[]{:S(2)}, u32[]{:S(2)}) collective-permute-start(bf16[40,512]{1,0:T(8,128)(2,1)S(1)} %get-tuple-element.53.refs_0_), channel_id=1, source_target_pairs={{0,24},{1,25},{2,26},{3,27},{4,28},{5,29},{6,30},{7,31},{8,16},{9,... | collective-permute-start | bytes 122888 | tf_op jit(solution)/shard_map/ppermute | solution.py:618
  9.2 0.0 collective-permute-done.3.refs_0_
  9.2 0.1 collective-permute-start.2
  9.3 0.0 collective-permute-done.4.refs_1_
  9.3 2.8 %collective-permute-done.5.refs_2_ = bf16[40,512]{1,0:T(8,128)(2,1)S(1)} collective-permute-done((bf16[40,512]{1,0:T(8,128)(2,1)S(1)}, bf16[40,512]{1,0:T(8,128)(2,1)S(1)}, u32[]{:S(2)}, u32[]{:S(2)}) %collective-permute-start.5) | collective-permute-done | bytes 40992 | tf_op jit(solution)/shard_map/ppermute | solution.py:618
  12.1 0.1 shard_map.128.refs_4_
  12.2 0.0 collective-permute-done.refs_1_
  12.2 0.0 collective-permute-done.1.refs_2_
  12.2 1.3 %collective-permute-done.2.refs_3_ = bf16[40,512]{1,0:T(8,128)(2,1)S(1)} collective-permute-done((bf16[40,512]{1,0:T(8,128)(2,1)S(1)}, bf16[40,512]{1,0:T(8,128)(2,1)S(1)}, u32[]{:S(2)}, u32[]{:S(2)}) %collective-permute-start.2) | collective-permute-done | bytes 40992 | tf_op jit(solution)/shard_map/ppermute | solution.py:618
  13.5 0.1 shard_map.129.refs_1_.refs_0_
  13.6 0.4 %collective-permute-start.8 = (bf16[240,512]{1,0:T(8,128)(2,1)S(1)}, bf16[240,512]{1,0:T(8,128)(2,1)S(1)}, u32[]{:S(2)}, u32[]{:S(2)}) collective-permute-start(bf16[240,512]{1,0:T(8,128)(2,1)S(1)} %shard_map.129.refs_1_.refs_0_), channel_id=1, source_target_pairs={{0,8},{1,9},{2,10},{3,11},{4,12},{5,13},{6,14},{7,15},{8,0},{9,1},... | collective-permute-start | bytes 737288 | tf_op jit(solution)/shard_map/ppermute | solution.py:618
  14.0 0.3 %collective-permute-start.6 = (bf16[104,512]{1,0:T(8,128)(2,1)S(1)}, bf16[104,512]{1,0:T(8,128)(2,1)S(1)}, u32[]{:S(2)}, u32[]{:S(2)}) collective-permute-start(bf16[104,512]{1,0:T(8,128)(2,1)S(1)} %shard_map.128.refs_4_), channel_id=1, source_target_pairs={{0,9},{1,8},{2,11},{3,10},{4,13},{5,12},{6,15},{7,14},{8,1},{9,0},... | collective-permute-start | bytes 319496 | tf_op jit(solution)/shard_map/ppermute | solution.py:618
  14.3 1.0 %collective-permute-start.7 = (bf16[104,512]{1,0:T(8,128)(2,1)S(1)}, bf16[104,512]{1,0:T(8,128)(2,1)S(1)}, u32[]{:S(2)}, u32[]{:S(2)}) collective-permute-start(bf16[104,512]{1,0:T(8,128)(2,1)S(1)} %shard_map.128.refs_4_), channel_id=1, source_target_pairs={{0,24},{1,25},{2,26},{3,27},{4,28},{5,29},{6,30},{7,31},{8,16},{9,... | collective-permute-start | bytes 319496 | tf_op jit(solution)/shard_map/ppermute | solution.py:618
  15.3 1.7 %collective-permute-start.9 = (bf16[104,512]{1,0:T(8,128)(2,1)S(1)}, bf16[104,512]{1,0:T(8,128)(2,1)S(1)}, u32[]{:S(2)}, u32[]{:S(2)}) collective-permute-start(bf16[104,512]{1,0:T(8,128)(2,1)S(1)} %shard_map.128.refs_4_), channel_id=1, source_target_pairs={{0,25},{1,24},{2,27},{3,26},{4,29},{5,28},{6,31},{7,30},{8,17},{9,... | collective-permute-start | bytes 319496 | tf_op jit(solution)/shard_map/ppermute | solution.py:618
  17.0 0.0 copy-done
  17.0 0.9 %shard_map.130 = (bf16[1024,1024]{1,0:T(8,128)(2,1)S(1)}, f32[2,32,8,256]{3,2,1,0:T(8,128)S(1)}, f32[2,32,8,128]{3,2,1,0:T(8,128)S(1)}, f32[2,32,8,128]{3,2,1,0:...) custom-call(bf16[40,512]{1,0:T(8,128)(2,1)S(1)} %get-tuple-element.5, ...), custom_call_target="tpu_custom_call" | custom-call | tf_op jit(solution)/shard_map/pallas_call | solution.py:571
  17.9 0.0 collective-permute-done.8.refs_0_.refs_4_
  17.9 1.0 %shard_map.131 = (bf16[1024,1024]{1,0:T(8,128)(2,1)S(1)}, f32[2,32,8,256]{3,2,1,0:T(8,128)S(1)}, f32[2,32,8,128]{3,2,1,0:T(8,128)S(1)}, f32[2,32,8,128]{3,2,1,0:T(8,128)S(1)}) custom-call(bf16[240,512]{1,0:T(8,128)(2,1)S(1)} %collective-permute-done.8.refs_0_.refs_4_, ...), custom_call_target="tpu_custom_call", output_to_operand_aliasing={{0}: (5, {}), {1}: (6, {}), {2}: (7, {}), {3}: (8, {})} | custom-call | tf_op jit(solution)/shard_map/pallas_call | solution.py:571
  18.9 0.0 collective-permute-done.6.refs_0_.refs_1_
  18.9 0.1 collective-permute-done.7.refs_1_.refs_2_
  19.0 1.1 %collective-permute-start.10 = (bf16[104,512]{1,0:T(8,128)(2,1)S(1)}, bf16[104,512]{1,0:T(8,128)(2,1)S(1)}, u32[]{:S(2)}, u32[]{:S(2)}) collective-permute-start(bf16[104,512]{1,0:T(8,128)(2,1)S(1)} %collective-permute-done.6.refs_0_.refs_1_), channel_id=1, source_target_pairs={{0,8},{1,9},{2,10},{3,11},{4,12},{5,13},{6,14},{7,15},{8,0},{9,1},... | collective-permute-start | bytes 319496 | tf_op jit(solution)/shard_map/ppermute | solution.py:618
  20.2 0.0 collective-permute-start.11
  20.2 1.0 %shard_map.132 = (bf16[1024,1024]{1,0:T(8,128)(2,1)S(1)}, f32[2,32,8,256]{3,2,1,0:T(8,128)S(1)}, f32[2,32,8,128]{3,2,1,0:T(8,128)S(1)}, f32[2,32,8,128]{3,2,1,0:T(8,128)S(1)}) custom-call(bf16[104,512]{1,0:T(8,128)(2,1)S(1)} %collective-permute-done.6.refs_0_.refs_1_, ...), custom_call_target="tpu_custom_call", output_to_operand_aliasing={{0}: (6, {}), {1}: (7, {}), {2}: (8, {}), {3}: (9, {})} | custom-call | tf_op jit(solution)/shard_map/pallas_call | solution.py:571
  21.2 1.1 %collective-permute-done.9.refs_0_.refs_3_ = bf16[104,512]{1,0:T(8,128)(2,1)S(1)} collective-permute-done((bf16[104,512]{1,0:T(8,128)(2,1)S(1)}, bf16[104,512]{1,0:T(8,128)(2,1)S(1)}, u32[]{:S(2)}, u32[]{:S(2)}) %collective-permute-start.9) | collective-permute-done | bytes 106528 | tf_op jit(solution)/shard_map/ppermute | solution.py:618
  22.3 0.0 copy-start.1
  22.3 0.0 copy-start.2
  22.3 0.0 copy-start.3
  22.3 0.0 copy-start.4
  22.3 0.0 copy-start.5
  22.3 0.0 copy-start.6
  22.3 0.4 %collective-permute-start.12 = (bf16[104,512]{1,0:T(8,128)(2,1)S(1)}, bf16[104,512]{1,0:T(8,128)(2,1)S(1)}, u32[]{:S(2)}, u32[]{:S(2)}) collective-permute-start(bf16[104,512]{1,0:T(8,128)(2,1)S(1)} %collective-permute-done.9.refs_0_.refs_3_), channel_id=1, source_target_pairs={{0,8},{1,9},{2,10},{3,11},{4,12},{5,13},{6,14},{7,15},{8,0},{9,1},... | collective-permute-start | bytes 319496 | tf_op jit(solution)/shard_map/ppermute | solution.py:618
  22.7 0.0 collective-permute-done.10.refs_1_.refs_5_
  22.7 0.0 collective-permute-done.11.refs_2_.refs_6_
  22.7 1.3 %shard_map.133 = (bf16[1024,1024]{1,0:T(8,128)(2,1)S(1)}, f32[2,32,8,256]{3,2,1,0:T(8,128)S(1)}, f32[2,32,8,128]{3,2,1,0:T(8,128)S(1)}, f32[2,32,8,128]{3,2,1,0:T(8,128)S(1)}) custom-call(bf16[104,512]{1,0:T(8,128)(2,1)S(1)} %collective-permute-done.9.refs_0_.refs_3_, ...), custom_call_target="tpu_custom_call", output_to_operand_aliasing={{0}: (7, {}), {1}: (8, {}), {2}: (9, {}), {3}: (10, {})} | custom-call | tf_op jit(solution)/shard_map/pallas_call | solution.py:571
  24.0 0.0 collective-permute-done.12.refs_7_
  24.1 0.0 copy-done.1
  24.1 0.0 copy-done.2
  24.1 0.0 copy-done.3
  24.1 0.0 copy-done.4
  24.1 0.0 copy-done.5
  24.1 0.0 copy-done.6
  24.1 3.1 %shard_map.134 = (bf16[32,512]{1,0:T(8,128)(2,1)}, bf16[1024,1024]{1,0:T(8,128)(2,1)S(1)}) custom-call(s32[1,8]{1,0:T(1,128)S(1)} %copy-done.4, s32[1,8]{1,0:T(1,128)S(1)} %copy-done.5, s32[3,1,8]{2,1,0:T(1,128)S(1)} %copy-done.3, f32[1,3]{1,0:T(1,128)S(1)} %bitcast.5, ...), custom_call_target="tpu_custom_call", output_to_operand_aliasing={{1}: (20, {})} | custom-call | tf_op jit(solution)/shard_map/pallas_call | solution.py:571
Async XLA Ops:
  0.0 17.0 %copy-start = (bf16[512,1536]{1,0:T(8,128)(2,1)S(1)}, bf16[512,1536]{1,0:T(8,128)(2,1)}, u32[]{:S(2)}) copy-start(bf16[512,1536]{1,0:T(8,128)(2,1)} %refs_8_.1) | copy-start | bytes 4718596
  1.1 8.2 %collective-permute-start.3 = (bf16[40,512]{1,0:T(8,128)(2,1)S(1)}, bf16[40,512]{1,0:T(8,128)(2,1)S(1)}, u32[]{:S(2)}, u32[]{:S(2)}) collective-permute-start(bf16[40,512]{1,0:T(8,128)(2,1)S(1)} %get-tuple-element.53.refs_0_), channel_id=1, source_target_pairs={{0,10},{1,11},{2,8},{3,9},{4,14},{5,15},{6,12},{7,13},{8,2},{9,3},... | collective-permute-start | bytes 122888 | tf_op jit(solution)/shard_map/ppermute | solution.py:618
  3.6 5.7 %collective-permute-start.4 = (bf16[40,512]{1,0:T(8,128)(2,1)S(1)}, bf16[40,512]{1,0:T(8,128)(2,1)S(1)}, u32[]{:S(2)}, u32[]{:S(2)}) collective-permute-start(bf16[40,512]{1,0:T(8,128)(2,1)S(1)} %get-tuple-element.53.refs_0_), channel_id=1, source_target_pairs={{0,12},{1,13},{2,14},{3,15},{4,8},{5,9},{6,10},{7,11},{8,4},{9,5},... | collective-permute-start | bytes 122888 | tf_op jit(solution)/shard_map/ppermute | solution.py:618
  6.5 5.6 %collective-permute-start.5 = (bf16[40,512]{1,0:T(8,128)(2,1)S(1)}, bf16[40,512]{1,0:T(8,128)(2,1)S(1)}, u32[]{:S(2)}, u32[]{:S(2)}) collective-permute-start(bf16[40,512]{1,0:T(8,128)(2,1)S(1)} %get-tuple-element.53.refs_0_), channel_id=1, source_target_pairs={{0,14},{1,15},{2,12},{3,13},{4,10},{5,11},{6,8},{7,9},{8,6},{9,7},... | collective-permute-start | bytes 122888 | tf_op jit(solution)/shard_map/ppermute | solution.py:618
  6.5 5.7 %collective-permute-start = (bf16[40,512]{1,0:T(8,128)(2,1)S(1)}, bf16[40,512]{1,0:T(8,128)(2,1)S(1)}, u32[]{:S(2)}, u32[]{:S(2)}) collective-permute-start(bf16[40,512]{1,0:T(8,128)(2,1)S(1)} %get-tuple-element.53.refs_0_), channel_id=1, source_target_pairs={{0,9},{1,8},{2,11},{3,10},{4,13},{5,12},{6,15},{7,14},{8,1},{9,0},... | collective-permute-start | bytes 122888 | tf_op jit(solution)/shard_map/ppermute | solution.py:618
  7.9 4.3 %collective-permute-start.1 = (bf16[40,512]{1,0:T(8,128)(2,1)S(1)}, bf16[40,512]{1,0:T(8,128)(2,1)S(1)}, u32[]{:S(2)}, u32[]{:S(2)}) collective-permute-start(bf16[40,512]{1,0:T(8,128)(2,1)S(1)} %get-tuple-element.53.refs_0_), channel_id=1, source_target_pairs={{0,24},{1,25},{2,26},{3,27},{4,28},{5,29},{6,30},{7,31},{8,16},{9,... | collective-permute-start | bytes 122888 | tf_op jit(solution)/shard_map/ppermute | solution.py:618
  9.2 4.3 %collective-permute-start.2 = (bf16[40,512]{1,0:T(8,128)(2,1)S(1)}, bf16[40,512]{1,0:T(8,128)(2,1)S(1)}, u32[]{:S(2)}, u32[]{:S(2)}) collective-permute-start(bf16[40,512]{1,0:T(8,128)(2,1)S(1)} %get-tuple-element.53.refs_0_), channel_id=1, source_target_pairs={{0,25},{1,24},{2,27},{3,26},{4,29},{5,28},{6,31},{7,30},{8,17},{9,... | collective-permute-start | bytes 122888 | tf_op jit(solution)/shard_map/ppermute | solution.py:618
  13.6 4.3 %collective-permute-start.8 = (bf16[240,512]{1,0:T(8,128)(2,1)S(1)}, bf16[240,512]{1,0:T(8,128)(2,1)S(1)}, u32[]{:S(2)}, u32[]{:S(2)}) collective-permute-start(bf16[240,512]{1,0:T(8,128)(2,1)S(1)} %shard_map.129.refs_1_.refs_0_), channel_id=1, source_target_pairs={{0,8},{1,9},{2,10},{3,11},{4,12},{5,13},{6,14},{7,15},{8,0},{9,1},... | collective-permute-start | bytes 737288 | tf_op jit(solution)/shard_map/ppermute | solution.py:618
  14.0 4.9 %collective-permute-start.6 = (bf16[104,512]{1,0:T(8,128)(2,1)S(1)}, bf16[104,512]{1,0:T(8,128)(2,1)S(1)}, u32[]{:S(2)}, u32[]{:S(2)}) collective-permute-start(bf16[104,512]{1,0:T(8,128)(2,1)S(1)} %shard_map.128.refs_4_), channel_id=1, source_target_pairs={{0,9},{1,8},{2,11},{3,10},{4,13},{5,12},{6,15},{7,14},{8,1},{9,0},... | collective-permute-start | bytes 319496 | tf_op jit(solution)/shard_map/ppermute | solution.py:618
  14.3 4.8 %collective-permute-start.7 = (bf16[104,512]{1,0:T(8,128)(2,1)S(1)}, bf16[104,512]{1,0:T(8,128)(2,1)S(1)}, u32[]{:S(2)}, u32[]{:S(2)}) collective-permute-start(bf16[104,512]{1,0:T(8,128)(2,1)S(1)} %shard_map.128.refs_4_), channel_id=1, source_target_pairs={{0,24},{1,25},{2,26},{3,27},{4,28},{5,29},{6,30},{7,31},{8,16},{9,... | collective-permute-start | bytes 319496 | tf_op jit(solution)/shard_map/ppermute | solution.py:618
  15.3 7.0 %collective-permute-start.9 = (bf16[104,512]{1,0:T(8,128)(2,1)S(1)}, bf16[104,512]{1,0:T(8,128)(2,1)S(1)}, u32[]{:S(2)}, u32[]{:S(2)}) collective-permute-start(bf16[104,512]{1,0:T(8,128)(2,1)S(1)} %shard_map.128.refs_4_), channel_id=1, source_target_pairs={{0,25},{1,24},{2,27},{3,26},{4,29},{5,28},{6,31},{7,30},{8,17},{9,... | collective-permute-start | bytes 319496 | tf_op jit(solution)/shard_map/ppermute | solution.py:618
  19.0 3.7 %collective-permute-start.10 = (bf16[104,512]{1,0:T(8,128)(2,1)S(1)}, bf16[104,512]{1,0:T(8,128)(2,1)S(1)}, u32[]{:S(2)}, u32[]{:S(2)}) collective-permute-start(bf16[104,512]{1,0:T(8,128)(2,1)S(1)} %collective-permute-done.6.refs_0_.refs_1_), channel_id=1, source_target_pairs={{0,8},{1,9},{2,10},{3,11},{4,12},{5,13},{6,14},{7,15},{8,0},{9,1},... | collective-permute-start | bytes 319496 | tf_op jit(solution)/shard_map/ppermute | solution.py:618
  20.2 2.5 %collective-permute-start.11 = (bf16[104,512]{1,0:T(8,128)(2,1)S(1)}, bf16[104,512]{1,0:T(8,128)(2,1)S(1)}, u32[]{:S(2)}, u32[]{:S(2)}) collective-permute-start(bf16[104,512]{1,0:T(8,128)(2,1)S(1)} %collective-permute-done.7.refs_1_.refs_2_), channel_id=1, source_target_pairs={{0,8},{1,9},{2,10},{3,11},{4,12},{5,13},{6,14},{7,15},{8,0},{9,1},... | collective-permute-start | bytes 319496 | tf_op jit(solution)/shard_map/ppermute | solution.py:618
  22.3 1.8 %copy-start.1 = (bf16[512,512]{1,0:T(8,128)(2,1)S(1)}, bf16[512,512]{1,0:T(8,128)(2,1)}, u32[]{:S(2)}) copy-start(bf16[512,512]{1,0:T(8,128)(2,1)} %refs_14_.1) | copy-start | bytes 1572868
  22.3 1.8 %copy-start.2 = (bf16[32,512]{1,0:T(8,128)(2,1)S(1)}, bf16[32,512]{1,0:T(8,128)(2,1)}, u32[]{:S(2)}) copy-start(bf16[32,512]{1,0:T(8,128)(2,1)} %refs_15_.1) | copy-start | bytes 98308
  22.3 1.8 %copy-start.3 = (s32[3,1,8]{2,1,0:T(1,128)S(1)}, s32[3,1,8]{2,1,0:T(1,128)}, u32[]{:S(2)}) copy-start(s32[3,1,8]{2,1,0:T(1,128)} %shift_ref.1) | copy-start | bytes 292
  22.3 1.8 %copy-start.4 = (s32[1,8]{1,0:T(1,128)S(1)}, s32[1,8]{1,0:T(1,128)}, u32[]{:S(2)}) copy-start(s32[1,8]{1,0:T(1,128)} %list_ref.1) | copy-start | bytes 100
  22.3 1.8 %copy-start.5 = (s32[1,8]{1,0:T(1,128)S(1)}, s32[1,8]{1,0:T(1,128)}, u32[]{:S(2)}) copy-start(s32[1,8]{1,0:T(1,128)} %valid_ref.1) | copy-start | bytes 100
  22.3 1.8 %copy-start.6 = (f32[3]{0:T(128)S(1)}, f32[3]{0:T(128)}, u32[]{:S(2)}) copy-start(f32[3]{0:T(128)} %param.15) | copy-start | bytes 40
  22.3 1.7 %collective-permute-start.12 = (bf16[104,512]{1,0:T(8,128)(2,1)S(1)}, bf16[104,512]{1,0:T(8,128)(2,1)S(1)}, u32[]{:S(2)}, u32[]{:S(2)}) collective-permute-start(bf16[104,512]{1,0:T(8,128)(2,1)S(1)} %collective-permute-done.9.refs_0_.refs_3_), channel_id=1, source_target_pairs={{0,8},{1,9},{2,10},{3,11},{4,12},{5,13},{6,14},{7,15},{8,0},{9,1},... | collective-permute-start | bytes 319496 | tf_op jit(solution)/shard_map/ppermute | solution.py:618

commit v9 on v8

--- a/solution.py
+++ b/solution.py
@@ -12,7 +12,6 @@
 rbf_step = 2.0
 rbf_width = 2.0
 two_pi = 2.0 * math.pi
-log2_e = 1.0 / math.log(2.0)
 highest = lax.Precision.HIGHEST
 
 
@@ -307,9 +306,9 @@
         tail = jnp.where(row == k, part.astype(jnp.float32), tail)
     stack = jnp.concatenate([h, h, m, h, l, m, tail.astype(jnp.bfloat16)], axis=0)
     w1_ref[...] = mm(unit(hidden, hidden, jnp.bfloat16), stack, ((1,), (1,))).astype(jnp.bfloat16)
-    h, l = parts_of(log2_e * pw_ref[...], 2)
+    h, l = parts_of(pw_ref[...], 2)
     w2_ref[...] = jnp.concatenate([h, h, l], axis=1)
-    str_ref[...] = jnp.broadcast_to(to_column(log2_e * cs_ref[...]), str_ref.shape)
+    str_ref[...] = jnp.broadcast_to(to_column(cs_ref[...]), str_ref.shape)
     q = mm(pack_ref[:atoms, :], wqkv_ref[:, :dim], ((1,), (0,)))
     q = q.astype(jnp.bfloat16).astype(jnp.float32)
     lane = lax.broadcasted_iota(jnp.int32, (per, width), 1) // head_dim
@@ -353,16 +352,20 @@
     return out
 
 
-def attend(qexp, keys, vals, scale, bias3):
-    rows = qexp.shape[0]
-    count = keys.shape[0]
-    atoms, per, _ = bias3.shape
-    s = mm(qexp, keys, ((1,), (1,))).reshape(atoms, per, count) * scale + bias3
-    top = jnp.max(s, axis=-1, keepdims=True)
-    p = jnp.exp2(s - top)
-    total = jnp.sum(p, axis=-1, keepdims=True)
-    o = mm(p.astype(jnp.bfloat16).reshape(rows, count), vals, ((1,), (0,)))
-    return top, total, o.reshape(atoms, per, vals.shape[1])
+def attend(qexps, keys, vals, scale, biases):
+    rows = qexps[0].shape[0]
+    count = keys[0].shape[0]
+    atoms, per, _ = biases[0].shape
+    scores = [mm(q, k, ((1,), (1,))) for q, k in zip(qexps, keys)]
+    tops, sums, probs = [], [], []
+    for s, bias3 in zip(scores, biases):
+        s = s.reshape(atoms, per, count) * scale + bias3
+        tops.append(jnp.max(s, axis=-1, keepdims=True))
+        p = jnp.exp(s - tops[-1])
+        sums.append(jnp.sum(p, axis=-1, keepdims=True))
+        probs.append(p.astype(jnp.bfloat16).reshape(rows, count))
+    outs = [mm(p, v, ((1,), (0,))) for p, v in zip(probs, vals)]
+    return [(t, n, o.reshape(atoms, per, o.shape[-1])) for t, n, o in zip(tops, sums, outs)]
 
 
 def absorb(head_dim, plan, pieces, wqkv_ref, qexp_ref, str_ref, own_ref, kv_ref):
@@ -386,20 +389,17 @@
     for c in range(3):
         term = own_ref[1, :, c : c + 1] * cos_k[c : c + 1] + own_ref[2, :, c : c + 1] * sin_k[c : c + 1]
         waves = term if waves is None else waves + term
-    out = []
-    for g in range(groups):
-        low, high = g * width, (g + 1) * width
-        bias3 = str_ref[g * per : (g + 1) * per, :1][None] * waves[:, None, :]
-        out.append(
-            attend(
-                qexp_ref[g],
-                kv[:, low:high],
-                kv[:, dim + low : dim + high],
-                log2_e * head_dim ** (-0.5),
-                bias3,
-            )
-        )
-    return out
+    spans = [(g * width, (g + 1) * width) for g in range(groups)]
+    return attend(
+        [qexp_ref[g] for g in range(groups)],
+        [kv[:, low:high] for low, high in spans],
+        [kv[:, dim + low : dim + high] for low, high in spans],
+        head_dim ** (-0.5),
+        [
+            str_ref[g * per : (g + 1) * per, :1][None] * waves[:, None, :]
+            for g in range(groups)
+        ],
+    )
 
 
 def widen(column, lanes):
@@ -437,7 +437,7 @@
     top, total, o = got[g]
     width = o.shape[-1]
     best = jnp.maximum(widen(top, 128), top_ref[g])
-    a, b = jnp.exp2(top_ref[g] - best), jnp.exp2(widen(top, 128) - best)
+    a, b = jnp.exp(top_ref[g] - best), jnp.exp(widen(top, 128) - best)
     summed = a * sum_ref[g] + b * widen(total, 128)
     acc = repeat_lanes(a, width) * acc_ref[g] + repeat_lanes(b, width) * o
     return best, summed, acc
@@ -536,25 +536,26 @@
     live = (chosen(valid_ref[...], lane) > 0)[None]
     block = lax.broadcasted_iota(jnp.int32, (1, per, width), 2) // head_dim
     keep = block == lax.broadcasted_iota(jnp.int32, (1, per, width), 1)
+    spans = [(g * width, (g + 1) * width) for g in range(groups)]
+    scores = [mm(qexp_ref[g], near_ref[:, low:high], ((1,), (1,))) for g, (low, high) in enumerate(spans)]
+    fars = []
+    for g in range(groups):
+        _, summed, far = merge(got, g, acc_in, top_in, sum_in)
+        far = far * repeat_lanes(1.0 / summed, width)
+        fars.append(jnp.sum(jnp.where(keep, far, 0.0), axis=1).astype(jnp.bfloat16))
+    probs, sums = [], []
+    for g in range(groups):
+        s = scores[g].reshape(atoms, per, listed) * head_dim ** (-0.5) + bias_ref[g]
+        s = jnp.where(live, s, -1e30)
+        p = jnp.exp(s - jnp.max(s, axis=-1, keepdims=True))
+        sums.append(1.0 / jnp.sum(p, axis=-1, keepdims=True))
+        probs.append(p.astype(jnp.bfloat16).reshape(rows, listed))
+    outs = [mm(probs[g], near_ref[:, dim + low : dim + high], ((1,), (0,))) for g, (low, high) in enumerate(spans)]
     pieces = []
     for g in range(groups):
-        low, high = g * width, (g + 1) * width
-        _, summed, far = merge(got, g, acc_in, top_in, sum_in)
-        far = far * repeat_lanes(1.0 / summed, width)
-        far = jnp.sum(jnp.where(keep, far, 0.0), axis=1).astype(jnp.bfloat16)
-        s = mm(qexp_ref[g], near_ref[:, low:high], ((1,), (1,)))
-        s = s.reshape(atoms, per, listed) * (log2_e * head_dim ** (-0.5)) + bias_ref[g]
-        s = jnp.where(live, s, -1e30)
-        p = jnp.exp2(s - jnp.max(s, axis=-1, keepdims=True))
-        summed = jnp.sum(p, axis=-1, keepdims=True)
-        o = mm(
-            p.astype(jnp.bfloat16).reshape(rows, listed),
-            near_ref[:, dim + low : dim + high],
-            ((1,), (0,)),
-        )
-        o = o.reshape(atoms, per, width) * (1.0 / summed)
+        o = outs[g].reshape(atoms, per, width) * sums[g]
         close = jnp.sum(jnp.where(keep, o, 0.0), axis=1).astype(jnp.bfloat16)
-        pieces.append((close.astype(jnp.float32) + far.astype(jnp.float32)).astype(jnp.bfloat16))
+        pieces.append((close.astype(jnp.float32) + fars[g].astype(jnp.float32)).astype(jnp.bfloat16))
     combined = jnp.concatenate(pieces, axis=1)
     moved = mm(combined, wout_ref[...], ((1,), (0,)))
     out_ref[...] = (in_ref[...].astype(jnp.float32) + moved).astype(jnp.bfloat16)

time: 27.3 us -> 27.2 us (level)
  transfers between devices with their start and end apart: 13 -> 13, of which waited for: 4 -> 4; matrix products, arithmetic and copies ran while one was open for 0% -> 0% of each run, Pallas kernels for 16% -> 15%
where the time goes in v9:
time: 27.2 us; the launch traced here: 27 us
  starting transfers between devices  13.1 us (48%)
  Pallas kernels  8.3 us (31%)
  waiting for transfers between devices  5.41 us (20%)
    ppermute x13, starting transfers between devices, swap(): return lax.ppermute(array, axes, [(i, i ^ mask) for i in range(total)])  13.1 us
    pallas_call x8, Pallas kernels, call(): pl.pallas_call(kernel, out_shape=outs, in_specs=specs, out_specs=[vmem] *...  8.3 us
    ppermute x13, waiting for transfers between devices, swap(): return lax.ppermute(array, axes, [(i, i ^ mask) for i in range(total)])  5.41 us
  transfers between devices with their start and end apart: 13, of which 4 were waited for; matrix products, arithmetic and copies ran while one was open for 0% of the time, Pallas kernels for 15%

profile of v9, /device:TPU:0, one launch (start us, length us, event | category | flops | bytes accessed | tf_op | source)
XLA Modules:
  0.0 27.0 jit_solution(4505651358542779398)
XLA Ops:
  0.0 0.0 copy-start
  0.0 1.0 %shard_map.127 = (bf16[40,512]{1,0:T(8,128)(2,1)S(1)}, f32[16,64]{1,0:T(8,128)S(1)}, f32[1,64]{1,0:T(1,128)S(1)}, f32[16,64]{1,0:T(8,128)S(1)}, f32[1,16]{1,0:T(1,128)S(1)}) custom-call(bf16[32,512]{1,0:T(8,128)(2,1)} %refs_15_.1, f32[1,512]{1,0:T(1,128)} %bitcast.7, f32[3,32]{1,0:T(4,128)} %refs_2_.3, f32[16,64]{1,0:T(8,128)} %refs_3_.2, f32[1,64]{1,0:T(1,128)} %bitcast.8, ...), custom_call_target="tpu_custom_call" | custom-call | tf_op jit(solution)/shard_map/pallas_call | solution.py:572
  1.1 2.6 %collective-permute-start.3 = (bf16[40,512]{1,0:T(8,128)(2,1)S(1)}, bf16[40,512]{1,0:T(8,128)(2,1)S(1)}, u32[]{:S(2)}, u32[]{:S(2)}) collective-permute-start(bf16[40,512]{1,0:T(8,128)(2,1)S(1)} %get-tuple-element.53.refs_0_), channel_id=1, source_target_pairs={{0,10},{1,11},{2,8},{3,9},{4,14},{5,15},{6,12},{7,13},{8,2},{9,3},... | collective-permute-start | bytes 122888 | tf_op jit(solution)/shard_map/ppermute | solution.py:619
  3.6 2.9 %collective-permute-start.4 = (bf16[40,512]{1,0:T(8,128)(2,1)S(1)}, bf16[40,512]{1,0:T(8,128)(2,1)S(1)}, u32[]{:S(2)}, u32[]{:S(2)}) collective-permute-start(bf16[40,512]{1,0:T(8,128)(2,1)S(1)} %get-tuple-element.53.refs_0_), channel_id=1, source_target_pairs={{0,12},{1,13},{2,14},{3,15},{4,8},{5,9},{6,10},{7,11},{8,4},{9,5},... | collective-permute-start | bytes 122888 | tf_op jit(solution)/shard_map/ppermute | solution.py:619
  6.5 0.0 collective-permute-start.5
  6.5 1.5 %collective-permute-start = (bf16[40,512]{1,0:T(8,128)(2,1)S(1)}, bf16[40,512]{1,0:T(8,128)(2,1)S(1)}, u32[]{:S(2)}, u32[]{:S(2)}) collective-permute-start(bf16[40,512]{1,0:T(8,128)(2,1)S(1)} %get-tuple-element.53.refs_0_), channel_id=1, source_target_pairs={{0,9},{1,8},{2,11},{3,10},{4,13},{5,12},{6,15},{7,14},{8,1},{9,0},... | collective-permute-start | bytes 122888 | tf_op jit(solution)/shard_map/ppermute | solution.py:619
  7.9 1.3 %collective-permute-start.1 = (bf16[40,512]{1,0:T(8,128)(2,1)S(1)}, bf16[40,512]{1,0:T(8,128)(2,1)S(1)}, u32[]{:S(2)}, u32[]{:S(2)}) collective-permute-start(bf16[40,512]{1,0:T(8,128)(2,1)S(1)} %get-tuple-element.53.refs_0_), channel_id=1, source_target_pairs={{0,24},{1,25},{2,26},{3,27},{4,28},{5,29},{6,30},{7,31},{8,16},{9,... | collective-permute-start | bytes 122888 | tf_op jit(solution)/shard_map/ppermute | solution.py:619
  9.2 0.0 collective-permute-done.3.refs_0_
  9.2 0.1 collective-permute-start.2
  9.3 0.0 collective-permute-done.4.refs_1_
  9.3 2.8 %collective-permute-done.5.refs_2_ = bf16[40,512]{1,0:T(8,128)(2,1)S(1)} collective-permute-done((bf16[40,512]{1,0:T(8,128)(2,1)S(1)}, bf16[40,512]{1,0:T(8,128)(2,1)S(1)}, u32[]{:S(2)}, u32[]{:S(2)}) %collective-permute-start.5) | collective-permute-done | bytes 40992 | tf_op jit(solution)/shard_map/ppermute | solution.py:619
  12.1 0.1 shard_map.128.refs_4_
  12.2 0.0 collective-permute-done.refs_1_
  12.2 0.0 collective-permute-done.1.refs_2_
  12.2 1.3 %collective-permute-done.2.refs_3_ = bf16[40,512]{1,0:T(8,128)(2,1)S(1)} collective-permute-done((bf16[40,512]{1,0:T(8,128)(2,1)S(1)}, bf16[40,512]{1,0:T(8,128)(2,1)S(1)}, u32[]{:S(2)}, u32[]{:S(2)}) %collective-permute-start.2) | collective-permute-done | bytes 40992 | tf_op jit(solution)/shard_map/ppermute | solution.py:619
  13.5 0.1 shard_map.129.refs_1_.refs_0_
  13.6 0.4 %collective-permute-start.8 = (bf16[240,512]{1,0:T(8,128)(2,1)S(1)}, bf16[240,512]{1,0:T(8,128)(2,1)S(1)}, u32[]{:S(2)}, u32[]{:S(2)}) collective-permute-start(bf16[240,512]{1,0:T(8,128)(2,1)S(1)} %shard_map.129.refs_1_.refs_0_), channel_id=1, source_target_pairs={{0,8},{1,9},{2,10},{3,11},{4,12},{5,13},{6,14},{7,15},{8,0},{9,1},... | collective-permute-start | bytes 737288 | tf_op jit(solution)/shard_map/ppermute | solution.py:619
  14.0 0.3 %collective-permute-start.6 = (bf16[104,512]{1,0:T(8,128)(2,1)S(1)}, bf16[104,512]{1,0:T(8,128)(2,1)S(1)}, u32[]{:S(2)}, u32[]{:S(2)}) collective-permute-start(bf16[104,512]{1,0:T(8,128)(2,1)S(1)} %shard_map.128.refs_4_), channel_id=1, source_target_pairs={{0,9},{1,8},{2,11},{3,10},{4,13},{5,12},{6,15},{7,14},{8,1},{9,0},... | collective-permute-start | bytes 319496 | tf_op jit(solution)/shard_map/ppermute | solution.py:619
  14.3 1.0 %collective-permute-start.7 = (bf16[104,512]{1,0:T(8,128)(2,1)S(1)}, bf16[104,512]{1,0:T(8,128)(2,1)S(1)}, u32[]{:S(2)}, u32[]{:S(2)}) collective-permute-start(bf16[104,512]{1,0:T(8,128)(2,1)S(1)} %shard_map.128.refs_4_), channel_id=1, source_target_pairs={{0,24},{1,25},{2,26},{3,27},{4,28},{5,29},{6,30},{7,31},{8,16},{9,... | collective-permute-start | bytes 319496 | tf_op jit(solution)/shard_map/ppermute | solution.py:619
  15.3 1.7 %collective-permute-start.9 = (bf16[104,512]{1,0:T(8,128)(2,1)S(1)}, bf16[104,512]{1,0:T(8,128)(2,1)S(1)}, u32[]{:S(2)}, u32[]{:S(2)}) collective-permute-start(bf16[104,512]{1,0:T(8,128)(2,1)S(1)} %shard_map.128.refs_4_), channel_id=1, source_target_pairs={{0,25},{1,24},{2,27},{3,26},{4,29},{5,28},{6,31},{7,30},{8,17},{9,... | collective-permute-start | bytes 319496 | tf_op jit(solution)/shard_map/ppermute | solution.py:619
  17.0 0.0 copy-done
  17.0 0.9 %shard_map.130 = (bf16[1024,1024]{1,0:T(8,128)(2,1)S(1)}, f32[2,32,8,256]{3,2,1,0:T(8,128)S(1)}, f32[2,32,8,128]{3,2,1,0:T(8,128)S(1)}, f32[2,32,8,128]{3,2,1,0:...) custom-call(bf16[40,512]{1,0:T(8,128)(2,1)S(1)} %get-tuple-element.5, ...), custom_call_target="tpu_custom_call" | custom-call | tf_op jit(solution)/shard_map/pallas_call | solution.py:572
  17.9 0.0 collective-permute-done.8.refs_0_.refs_4_
  17.9 1.0 %shard_map.131 = (bf16[1024,1024]{1,0:T(8,128)(2,1)S(1)}, f32[2,32,8,256]{3,2,1,0:T(8,128)S(1)}, f32[2,32,8,128]{3,2,1,0:T(8,128)S(1)}, f32[2,32,8,128]{3,2,1,0:T(8,128)S(1)}) custom-call(bf16[240,512]{1,0:T(8,128)(2,1)S(1)} %collective-permute-done.8.refs_0_.refs_4_, ...), custom_call_target="tpu_custom_call", output_to_operand_aliasing={{0}: (5, {}), {1}: (6, {}), {2}: (7, {}), {3}: (8, {})} | custom-call | tf_op jit(solution)/shard_map/pallas_call | solution.py:572
  18.9 0.0 collective-permute-done.6.refs_0_.refs_1_
  18.9 0.1 collective-permute-done.7.refs_1_.refs_2_
  19.0 1.1 %collective-permute-start.10 = (bf16[104,512]{1,0:T(8,128)(2,1)S(1)}, bf16[104,512]{1,0:T(8,128)(2,1)S(1)}, u32[]{:S(2)}, u32[]{:S(2)}) collective-permute-start(bf16[104,512]{1,0:T(8,128)(2,1)S(1)} %collective-permute-done.6.refs_0_.refs_1_), channel_id=1, source_target_pairs={{0,8},{1,9},{2,10},{3,11},{4,12},{5,13},{6,14},{7,15},{8,0},{9,1},... | collective-permute-start | bytes 319496 | tf_op jit(solution)/shard_map/ppermute | solution.py:619
  20.2 0.0 collective-permute-start.11
  20.2 1.0 %shard_map.132 = (bf16[1024,1024]{1,0:T(8,128)(2,1)S(1)}, f32[2,32,8,256]{3,2,1,0:T(8,128)S(1)}, f32[2,32,8,128]{3,2,1,0:T(8,128)S(1)}, f32[2,32,8,128]{3,2,1,0:T(8,128)S(1)}) custom-call(bf16[104,512]{1,0:T(8,128)(2,1)S(1)} %collective-permute-done.6.refs_0_.refs_1_, ...), custom_call_target="tpu_custom_call", output_to_operand_aliasing={{0}: (6, {}), {1}: (7, {}), {2}: (8, {}), {3}: (9, {})} | custom-call | tf_op jit(solution)/shard_map/pallas_call | solution.py:572
  21.2 1.1 %collective-permute-done.9.refs_0_.refs_3_ = bf16[104,512]{1,0:T(8,128)(2,1)S(1)} collective-permute-done((bf16[104,512]{1,0:T(8,128)(2,1)S(1)}, bf16[104,512]{1,0:T(8,128)(2,1)S(1)}, u32[]{:S(2)}, u32[]{:S(2)}) %collective-permute-start.9) | collective-permute-done | bytes 106528 | tf_op jit(solution)/shard_map/ppermute | solution.py:619
  22.3 0.0 copy-start.1
  22.3 0.0 copy-start.2
  22.3 0.0 copy-start.3
  22.3 0.0 copy-start.4
  22.3 0.0 copy-start.5
  22.3 0.0 copy-start.6
  22.3 0.4 %collective-permute-start.12 = (bf16[104,512]{1,0:T(8,128)(2,1)S(1)}, bf16[104,512]{1,0:T(8,128)(2,1)S(1)}, u32[]{:S(2)}, u32[]{:S(2)}) collective-permute-start(bf16[104,512]{1,0:T(8,128)(2,1)S(1)} %collective-permute-done.9.refs_0_.refs_3_), channel_id=1, source_target_pairs={{0,8},{1,9},{2,10},{3,11},{4,12},{5,13},{6,14},{7,15},{8,0},{9,1},... | collective-permute-start | bytes 319496 | tf_op jit(solution)/shard_map/ppermute | solution.py:619
  22.7 0.0 collective-permute-done.10.refs_1_.refs_5_
  22.7 0.0 collective-permute-done.11.refs_2_.refs_6_
  22.7 1.2 %shard_map.133 = (bf16[1024,1024]{1,0:T(8,128)(2,1)S(1)}, f32[2,32,8,256]{3,2,1,0:T(8,128)S(1)}, f32[2,32,8,128]{3,2,1,0:T(8,128)S(1)}, f32[2,32,8,128]{3,2,1,0:T(8,128)S(1)}) custom-call(bf16[104,512]{1,0:T(8,128)(2,1)S(1)} %collective-permute-done.9.refs_0_.refs_3_, ...), custom_call_target="tpu_custom_call", output_to_operand_aliasing={{0}: (7, {}), {1}: (8, {}), {2}: (9, {}), {3}: (10, {})} | custom-call | tf_op jit(solution)/shard_map/pallas_call | solution.py:572
  24.0 0.0 collective-permute-done.12.refs_7_
  24.0 0.0 copy-done.1
  24.0 0.0 copy-done.2
  24.0 0.0 copy-done.3
  24.0 0.0 copy-done.4
  24.0 0.0 copy-done.5
  24.0 0.0 copy-done.6
  24.0 3.0 %shard_map.134 = (bf16[32,512]{1,0:T(8,128)(2,1)}, bf16[1024,1024]{1,0:T(8,128)(2,1)S(1)}) custom-call(s32[1,8]{1,0:T(1,128)S(1)} %copy-done.4, s32[1,8]{1,0:T(1,128)S(1)} %copy-done.5, s32[3,1,8]{2,1,0:T(1,128)S(1)} %copy-done.3, f32[1,3]{1,0:T(1,128)S(1)} %bitcast.5, ...), custom_call_target="tpu_custom_call", output_to_operand_aliasing={{1}: (20, {})} | custom-call | tf_op jit(solution)/shard_map/pallas_call | solution.py:572
Async XLA Ops:
  0.0 17.0 %copy-start = (bf16[512,1536]{1,0:T(8,128)(2,1)S(1)}, bf16[512,1536]{1,0:T(8,128)(2,1)}, u32[]{:S(2)}) copy-start(bf16[512,1536]{1,0:T(8,128)(2,1)} %refs_8_.1) | copy-start | bytes 4718596
  1.1 8.2 %collective-permute-start.3 = (bf16[40,512]{1,0:T(8,128)(2,1)S(1)}, bf16[40,512]{1,0:T(8,128)(2,1)S(1)}, u32[]{:S(2)}, u32[]{:S(2)}) collective-permute-start(bf16[40,512]{1,0:T(8,128)(2,1)S(1)} %get-tuple-element.53.refs_0_), channel_id=1, source_target_pairs={{0,10},{1,11},{2,8},{3,9},{4,14},{5,15},{6,12},{7,13},{8,2},{9,3},... | collective-permute-start | bytes 122888 | tf_op jit(solution)/shard_map/ppermute | solution.py:619
  3.6 5.7 %collective-permute-start.4 = (bf16[40,512]{1,0:T(8,128)(2,1)S(1)}, bf16[40,512]{1,0:T(8,128)(2,1)S(1)}, u32[]{:S(2)}, u32[]{:S(2)}) collective-permute-start(bf16[40,512]{1,0:T(8,128)(2,1)S(1)} %get-tuple-element.53.refs_0_), channel_id=1, source_target_pairs={{0,12},{1,13},{2,14},{3,15},{4,8},{5,9},{6,10},{7,11},{8,4},{9,5},... | collective-permute-start | bytes 122888 | tf_op jit(solution)/shard_map/ppermute | solution.py:619
  6.5 5.6 %collective-permute-start.5 = (bf16[40,512]{1,0:T(8,128)(2,1)S(1)}, bf16[40,512]{1,0:T(8,128)(2,1)S(1)}, u32[]{:S(2)}, u32[]{:S(2)}) collective-permute-start(bf16[40,512]{1,0:T(8,128)(2,1)S(1)} %get-tuple-element.53.refs_0_), channel_id=1, source_target_pairs={{0,14},{1,15},{2,12},{3,13},{4,10},{5,11},{6,8},{7,9},{8,6},{9,7},... | collective-permute-start | bytes 122888 | tf_op jit(solution)/shard_map/ppermute | solution.py:619
  6.5 5.7 %collective-permute-start = (bf16[40,512]{1,0:T(8,128)(2,1)S(1)}, bf16[40,512]{1,0:T(8,128)(2,1)S(1)}, u32[]{:S(2)}, u32[]{:S(2)}) collective-permute-start(bf16[40,512]{1,0:T(8,128)(2,1)S(1)} %get-tuple-element.53.refs_0_), channel_id=1, source_target_pairs={{0,9},{1,8},{2,11},{3,10},{4,13},{5,12},{6,15},{7,14},{8,1},{9,0},... | collective-permute-start | bytes 122888 | tf_op jit(solution)/shard_map/ppermute | solution.py:619
  7.9 4.3 %collective-permute-start.1 = (bf16[40,512]{1,0:T(8,128)(2,1)S(1)}, bf16[40,512]{1,0:T(8,128)(2,1)S(1)}, u32[]{:S(2)}, u32[]{:S(2)}) collective-permute-start(bf16[40,512]{1,0:T(8,128)(2,1)S(1)} %get-tuple-element.53.refs_0_), channel_id=1, source_target_pairs={{0,24},{1,25},{2,26},{3,27},{4,28},{5,29},{6,30},{7,31},{8,16},{9,... | collective-permute-start | bytes 122888 | tf_op jit(solution)/shard_map/ppermute | solution.py:619
  9.2 4.3 %collective-permute-start.2 = (bf16[40,512]{1,0:T(8,128)(2,1)S(1)}, bf16[40,512]{1,0:T(8,128)(2,1)S(1)}, u32[]{:S(2)}, u32[]{:S(2)}) collective-permute-start(bf16[40,512]{1,0:T(8,128)(2,1)S(1)} %get-tuple-element.53.refs_0_), channel_id=1, source_target_pairs={{0,25},{1,24},{2,27},{3,26},{4,29},{5,28},{6,31},{7,30},{8,17},{9,... | collective-permute-start | bytes 122888 | tf_op jit(solution)/shard_map/ppermute | solution.py:619
  13.6 4.3 %collective-permute-start.8 = (bf16[240,512]{1,0:T(8,128)(2,1)S(1)}, bf16[240,512]{1,0:T(8,128)(2,1)S(1)}, u32[]{:S(2)}, u32[]{:S(2)}) collective-permute-start(bf16[240,512]{1,0:T(8,128)(2,1)S(1)} %shard_map.129.refs_1_.refs_0_), channel_id=1, source_target_pairs={{0,8},{1,9},{2,10},{3,11},{4,12},{5,13},{6,14},{7,15},{8,0},{9,1},... | collective-permute-start | bytes 737288 | tf_op jit(solution)/shard_map/ppermute | solution.py:619
  14.0 4.9 %collective-permute-start.6 = (bf16[104,512]{1,0:T(8,128)(2,1)S(1)}, bf16[104,512]{1,0:T(8,128)(2,1)S(1)}, u32[]{:S(2)}, u32[]{:S(2)}) collective-permute-start(bf16[104,512]{1,0:T(8,128)(2,1)S(1)} %shard_map.128.refs_4_), channel_id=1, source_target_pairs={{0,9},{1,8},{2,11},{3,10},{4,13},{5,12},{6,15},{7,14},{8,1},{9,0},... | collective-permute-start | bytes 319496 | tf_op jit(solution)/shard_map/ppermute | solution.py:619
  14.3 4.8 %collective-permute-start.7 = (bf16[104,512]{1,0:T(8,128)(2,1)S(1)}, bf16[104,512]{1,0:T(8,128)(2,1)S(1)}, u32[]{:S(2)}, u32[]{:S(2)}) collective-permute-start(bf16[104,512]{1,0:T(8,128)(2,1)S(1)} %shard_map.128.refs_4_), channel_id=1, source_target_pairs={{0,24},{1,25},{2,26},{3,27},{4,28},{5,29},{6,30},{7,31},{8,16},{9,... | collective-permute-start | bytes 319496 | tf_op jit(solution)/shard_map/ppermute | solution.py:619
  15.3 7.0 %collective-permute-start.9 = (bf16[104,512]{1,0:T(8,128)(2,1)S(1)}, bf16[104,512]{1,0:T(8,128)(2,1)S(1)}, u32[]{:S(2)}, u32[]{:S(2)}) collective-permute-start(bf16[104,512]{1,0:T(8,128)(2,1)S(1)} %shard_map.128.refs_4_), channel_id=1, source_target_pairs={{0,25},{1,24},{2,27},{3,26},{4,29},{5,28},{6,31},{7,30},{8,17},{9,... | collective-permute-start | bytes 319496 | tf_op jit(solution)/shard_map/ppermute | solution.py:619
  19.0 3.7 %collective-permute-start.10 = (bf16[104,512]{1,0:T(8,128)(2,1)S(1)}, bf16[104,512]{1,0:T(8,128)(2,1)S(1)}, u32[]{:S(2)}, u32[]{:S(2)}) collective-permute-start(bf16[104,512]{1,0:T(8,128)(2,1)S(1)} %collective-permute-done.6.refs_0_.refs_1_), channel_id=1, source_target_pairs={{0,8},{1,9},{2,10},{3,11},{4,12},{5,13},{6,14},{7,15},{8,0},{9,1},... | collective-permute-start | bytes 319496 | tf_op jit(solution)/shard_map/ppermute | solution.py:619
  20.2 2.5 %collective-permute-start.11 = (bf16[104,512]{1,0:T(8,128)(2,1)S(1)}, bf16[104,512]{1,0:T(8,128)(2,1)S(1)}, u32[]{:S(2)}, u32[]{:S(2)}) collective-permute-start(bf16[104,512]{1,0:T(8,128)(2,1)S(1)} %collective-permute-done.7.refs_1_.refs_2_), channel_id=1, source_target_pairs={{0,8},{1,9},{2,10},{3,11},{4,12},{5,13},{6,14},{7,15},{8,0},{9,1},... | collective-permute-start | bytes 319496 | tf_op jit(solution)/shard_map/ppermute | solution.py:619
  22.3 1.7 %copy-start.1 = (bf16[512,512]{1,0:T(8,128)(2,1)S(1)}, bf16[512,512]{1,0:T(8,128)(2,1)}, u32[]{:S(2)}) copy-start(bf16[512,512]{1,0:T(8,128)(2,1)} %refs_14_.1) | copy-start | bytes 1572868
  22.3 1.7 %copy-start.2 = (bf16[32,512]{1,0:T(8,128)(2,1)S(1)}, bf16[32,512]{1,0:T(8,128)(2,1)}, u32[]{:S(2)}) copy-start(bf16[32,512]{1,0:T(8,128)(2,1)} %refs_15_.1) | copy-start | bytes 98308
  22.3 1.7 %copy-start.3 = (s32[3,1,8]{2,1,0:T(1,128)S(1)}, s32[3,1,8]{2,1,0:T(1,128)}, u32[]{:S(2)}) copy-start(s32[3,1,8]{2,1,0:T(1,128)} %shift_ref.1) | copy-start | bytes 292
  22.3 1.7 %copy-start.4 = (s32[1,8]{1,0:T(1,128)S(1)}, s32[1,8]{1,0:T(1,128)}, u32[]{:S(2)}) copy-start(s32[1,8]{1,0:T(1,128)} %list_ref.1) | copy-start | bytes 100
  22.3 1.7 %copy-start.5 = (s32[1,8]{1,0:T(1,128)S(1)}, s32[1,8]{1,0:T(1,128)}, u32[]{:S(2)}) copy-start(s32[1,8]{1,0:T(1,128)} %valid_ref.1) | copy-start | bytes 100
  22.3 1.7 %copy-start.6 = (f32[3]{0:T(128)S(1)}, f32[3]{0:T(128)}, u32[]{:S(2)}) copy-start(f32[3]{0:T(128)} %param.15) | copy-start | bytes 40
  22.3 1.6 %collective-permute-start.12 = (bf16[104,512]{1,0:T(8,128)(2,1)S(1)}, bf16[104,512]{1,0:T(8,128)(2,1)S(1)}, u32[]{:S(2)}, u32[]{:S(2)}) collective-permute-start(bf16[104,512]{1,0:T(8,128)(2,1)S(1)} %collective-permute-done.9.refs_0_.refs_3_), channel_id=1, source_target_pairs={{0,8},{1,9},{2,10},{3,11},{4,12},{5,13},{6,14},{7,15},{8,0},{9,1},... | collective-permute-start | bytes 319496 | tf_op jit(solution)/shard_map/ppermute | solution.py:619
